TPU v7x, 32 devices: a whole 2x2x4 slice. The times are simulated.
32 devices in a mesh: field: 2 (over x), focus: 2 (over core), strip: 8 (over z, y).
Axes of the slice: x: 2, y: 2, z: 4, core: 2. Of those that a mesh axis runs over, the one named last changes fastest.
Arguments:
- slices: bfloat16 [32, 4096, 4096], P(('field', 'focus'), 'strip'), parts along dimension 0, may hold values from 0 to 1
- otf_rows: float32 [4096], replicated, may hold values from 0.1 to 1
- otf_cols: float32 [4096], replicated, may hold values from 0.1 to 1
Outputs:
- restored: float32 [8192, 4096], P(('field', 'focus', 'strip')), parts along dimension 0
There are 2 independent parts, one for each index of `field`. A program takes and returns all parts, laid end to end along the dimension named above; an argument that names none is the same for every part. Nothing has to cross between parts.
All inputs are finite; a program needn't handle non-finite values.
Results may differ from a plain program's by a relative error of at most 0.011.
Values may be sent and summed in bfloat16 or wider, within the bound.
No kernel may reach another device: no remote copies, remote signals or barrier semaphores. Data moves between devices by JAX's collectives and lax.ppermute only.
A program may use at most 256 MiB of HBM per device.

v0:
```python
import math

import jax
import jax.numpy as jnp
from jax import lax
from jax.sharding import PartitionSpec as P

floor_weight = 0.01
noise_ratio = 0.01


def extended(cells, sides, width):
    for axis, dim in sides:
        count = lax.axis_size(axis)
        ends = count - 1
        head = lax.slice_in_dim(cells, 0, width, axis=dim)
        tail = lax.slice_in_dim(cells, cells.shape[dim] - width, cells.shape[dim], axis=dim)
        cells = jnp.concatenate(
            [
                lax.ppermute(tail, axis, [(i, (i + 1) % count) for i in range(ends)]),
                cells,
                lax.ppermute(head, axis, [((i + 1) % count, i) for i in range(ends)]),
            ],
            axis=dim,
        )
    return cells


def cosine_block(first_row, height, length):
    low_count = min(64, length)
    high_count = length // low_count
    frequency = first_row + lax.broadcasted_iota(jnp.int32, (height, 1), 0)
    high_sample = lax.broadcasted_iota(jnp.int32, (1, high_count), 1)
    low_sample = lax.broadcasted_iota(jnp.int32, (1, low_count), 1)
    high_phase = 2 * low_count * high_sample * frequency % (4 * length)
    low_phase = (2 * low_sample + 1) * frequency % (4 * length)
    unit = jnp.float32(math.pi / (2 * length))
    high_angle = high_phase.astype(jnp.float32) * unit
    low_angle = low_phase.astype(jnp.float32) * unit
    norming = jnp.where(
        frequency == 0, jnp.float32(math.sqrt(1.0 / length)), jnp.float32(math.sqrt(2.0 / length))
    )
    high_cos = (norming * jnp.cos(high_angle))[:, :, None]
    high_sin = (norming * jnp.sin(high_angle))[:, :, None]
    low_cos = jnp.cos(low_angle)[:, None, :]
    low_sin = jnp.sin(low_angle)[:, None, :]
    table = high_cos * low_cos - high_sin * low_sin
    return table.reshape(height, length).astype(jnp.bfloat16)


def cosine_table(length):
    height = min(512, length)
    starts = jnp.arange(length // height, dtype=jnp.int32) * height
    return lax.map(lambda first_row: cosine_block(first_row, height, length), starts).reshape(
        length, length
    )


def laplace(padded, center, spacing, margin):
    count = center.shape[1]
    total = (
        padded[:, margin + spacing : margin + spacing + count, :]
        + padded[:, margin - spacing : margin - spacing + count, :]
    )
    widened = jnp.pad(center, ((0, 0), (0, 0), (spacing, spacing)))
    total = total + widened[:, :, 2 * spacing :] + widened[:, :, : -2 * spacing]
    return total - 4.0 * center


def contract(left, right, left_dim, right_dim):
    return lax.dot_general(
        left, right, (((left_dim,), (right_dim,)), ((), ())), preferred_element_type=jnp.float32
    )


def body(slices, otf_rows, otf_cols):
    focus_count = lax.axis_size("focus")
    strip_count = lax.axis_size("strip")
    length = slices.shape[2]
    piece = length // (focus_count * strip_count)
    margin = 4
    padded = extended(slices, (("strip", 1),), margin).astype(jnp.float32)
    center = padded[:, margin:-margin, :]
    fine_term = laplace(padded, center, 1, margin)
    middle_term = laplace(padded, center, 2, margin)
    coarse_term = laplace(padded, center, 4, margin)
    weight = (
        floor_weight
        + fine_term * fine_term
        + 0.5 * middle_term * middle_term
        + 0.25 * coarse_term * coarse_term
    )
    numerator = jnp.sum(weight * center, axis=0)
    denominator = jnp.sum(weight, axis=0)
    numerator, denominator = (
        lax.psum_scatter(numerator, "focus", scatter_dimension=0, tiled=True),
        lax.psum_scatter(denominator, "focus", scatter_dimension=0, tiled=True),
    )
    row_block = (numerator / denominator).astype(jnp.bfloat16)
    cosines = cosine_table(length)
    along_cols = contract(cosines, row_block, 1, 1).astype(jnp.bfloat16)
    arrived = lax.all_to_all(
        along_cols, ("focus", "strip"), split_axis=0, concat_axis=1, tiled=True
    )
    column_block = (
        arrived.reshape(piece, focus_count, strip_count, piece)
        .transpose(0, 2, 1, 3)
        .reshape(piece, length)
    )
    spectrum = contract(column_block, cosines, 1, 1)
    owner = lax.axis_index("focus") * strip_count + lax.axis_index("strip")
    local_cols = lax.dynamic_slice_in_dim(otf_cols, owner * piece, piece, 0)
    response = local_cols[:, None] * otf_rows[None, :]
    filtered = (spectrum * (response / (response * response + noise_ratio))).astype(jnp.bfloat16)
    back_cols = contract(cosines, filtered, 0, 1).astype(jnp.bfloat16)
    rows_back = lax.all_to_all(
        back_cols, ("focus", "strip"), split_axis=0, concat_axis=1, tiled=True
    )
    return jnp.dot(rows_back, cosines, preferred_element_type=jnp.float32)


def solution(mesh):
    in_specs = (P(("field", "focus"), "strip", None), P(), P())
    out_specs = P(("field", "focus", "strip"), None)
    return jax.shard_map(body, mesh=mesh, in_specs=in_specs, out_specs=out_specs, check_vma=False)
```

profile of v0, /device:TPU:0, one launch (start us, length us, event | category | flops | bytes accessed | tf_op | source)
XLA Modules:
  0.0 783.3 jit_solution(7468507866088875308)
XLA Ops:
  8.0 4.9 collective-permute-start
  14.2 9.8 %collective-permute-done = bf16[8,4,4096]{2,1,0:T(4,128)(2,1)S(1)} collective-permute-done((bf16[8,4,4096]{2,1,0:T(4,128)(2,1)S(1)}, bf16[8,4,4096]{2,1,0:T(4,128)(2,1)S(1)}, u32[]{:S(2)}, u32[]{:S(2)}) %collective-permute-start) | collective-permute-done | bytes 262176 | tf_op jit(solution)/shard_map/ppermute | solution.py:20
  24.1 32.4 %maximum_convert_fusion = f32[8,520,4096]{2,1,0:T(8,128)} fusion(bf16[8,4,4096]{2,1,0:T(4,128)(2,1)S(1)} %collective-permute-done.1, bf16[8,512,4096]{2,1,0:T(8,128)(2,1)} %param.5, bf16[8,4,4096]{2,1,0:T(4,128)(2,1)S(1)} %collective-permute-done), kind=kLoop, calls=%fused_computation.45 | loop fusion | flops 102236160 | bytes 102236160 | tf_op jit(solution)/shard_map/convert_element_type | solution.py:82
  56.5 44.1 %slice.62 = f32[8,512,4096]{2,1,0:T(8,128)} slice(f32[8,520,4096]{2,1,0:T(8,128)} %maximum_convert_fusion), slice={[0:8], [4:516], [0:4096]} | slice | bytes 134217728 | tf_op jit(solution)/shard_map/slice | solution.py:83
  100.5 343.3 %fusion.23 = (f32[512,4096]{1,0:T(8,128)}, f32[512,4096]{1,0:T(8,128)}) fusion(f32[8,520,4096]{2,1,0:T(8,128)} %maximum_convert_fusion, f32[8,512,4096]{2,1,0:T(8,128)} %slice.62), kind=kLoop, calls=%fused_computation.55 | loop fusion | flops 398458880 | bytes 553648128 | tf_op jit(solution)/shard_map/reduce_sum | solution.py:94
  444.7 145.2 %while.12 = (s32[]{:T(128)}, bf16[8,512,4096]{2,1,0:T(8,128)(2,1)}, s32[8]{0:T(128)S(1)}, s32[]{:T(128)}) while((s32[]{:T(128)}, bf16[8,512,4096]{2,1,0:T(8,128)(2,1)}, s32[8]{0:T(128)S(1)}, s32[]{:T(128)}) %tuple.37), condition=%wide.region_1.2_spmd, body=%wide.region_0.1_spmd.sunk | while | flops 9373890 | bytes 22029896 | solution.py:54
  447.7 3.8 subtract_convert_fusion.2
  451.4 6.9 copy.17
  458.4 5.5 constant_dynamic-update-slice_fusion.2
  466.9 3.8 subtract_convert_fusion.2
  470.7 6.6 copy.17
  477.3 5.8 constant_dynamic-update-slice_fusion.2
  486.1 3.8 subtract_convert_fusion.2
  489.9 6.4 copy.17
  496.3 4.6 constant_dynamic-update-slice_fusion.2
  503.9 3.8 subtract_convert_fusion.2
  507.7 6.4 copy.17
  514.1 4.6 constant_dynamic-update-slice_fusion.2
  525.5 6.4 copy.17
  531.8 4.6 constant_dynamic-update-slice_fusion.2
  543.2 6.4 copy.17
  549.6 4.6 constant_dynamic-update-slice_fusion.2
  561.0 6.4 copy.17
  567.4 4.6 constant_dynamic-update-slice_fusion.2
  578.8 6.4 copy.17
  585.2 4.6 constant_dynamic-update-slice_fusion.2
  589.8 18.7 %convolution_convert_fusion = bf16[4096,256]{1,0:T(8,128)(2,1)} fusion(bf16[4096,4096]{1,0:T(8,128)(2,1)} %bitcast.33, f32[256,4096]{1,0:T(8,128)} %reduce-scatter.3.cloned.1.call-done, f32[256,4096]{1,0:T(8,128)} %reduce-scatter.5.cloned.1.call-done), kind=kOutput, calls=%fused_computation.49 | convolution fusion | flops 8593080320 | bytes 44040192 | tf_op jit(solution)/shard_map/dot_general | solution.py:71
  608.5 6.0 all-to-all-start
  615.3 46.8 %all-to-all-done = bf16[16,256,256]{2,1,0:T(8,128)(2,1)S(1)} async-done(((bf16[16,256,256]{2,1,0:T(8,128)(2,1)}), bf16[16,256,256]{2,1,0:T(8,128)(2,1)S(1)}, u32[]{:S(2)}, u32[]{:S(2)}) %all-to-all-start) | async-done | bytes 2097184 | tf_op jit(solution)/shard_map/all_to_all | solution.py:102
  664.5 37.6 %convolution_convert_fusion.1 = bf16[4096,256]{1,0:T(8,128)(2,1)} fusion(bf16[4096,4096]{1,0:T(8,128)(2,1)} %bitcast.34, bf16[256,4096]{0,1:T(8,128)(2,1)} %bitcast.39, f32[4096]{0:T(1024)S(1)} %copy-done, f32[256]{0:T(256)S(1)} %dynamic_slice.10), kind=kOutput, calls=%fused_computation.51 | convolution fusion | flops 17187209216 | bytes 37766144 | tf_op jit(solution)/shard_map/dot_general | solution.py:71
  705.0 54.3 %all_to_all.35 = bf16[16,256,256]{1,2,0:T(8,128)(2,1)S(1)} all-to-all(bf16[16,256,256]{1,2,0:T(8,128)(2,1)S(1)} %copy.12), channel_id=1, replica_groups=mesh['field'=2,'focus'=2,'strip'=8] {'focus','strip'}, dimensions={0} | all-to-all | bytes 4194304 | tf_op jit(solution)/shard_map/all_to_all | solution.py:116
  759.3 17.2 %fusion.25 = f32[256,4096]{1,0:T(8,128)} fusion(bf16[256,4096]{0,1:T(8,128)(2,1)S(1)} %bitcast.36, bf16[4096,4096]{1,0:T(8,128)(2,1)} %bitcast.35), kind=kOutput, calls=%fused_computation.57 | convolution fusion | flops 8589934592 | bytes 39845888 | tf_op jit(solution)/shard_map/dot_general | solution.py:119
  (60 shorter events, 48.5 us)
Async XLA Ops:
  6.5 583.3 %reduce-scatter.3.cloned.1.call-start = ((), (), s32[]{:S(2)}) async-start(), calls=%async_computation.4 | async-start | bytes 12582912 | tf_op jit(solution)/shard_map/reduce_scatter | solution.py:96
  8.0 16.1 %collective-permute-start = (bf16[8,4,4096]{2,1,0:T(4,128)(2,1)S(1)}, bf16[8,4,4096]{2,1,0:T(4,128)(2,1)S(1)}, u32[]{:S(2)}, u32[]{:S(2)}) collective-permute-start(bf16[8,4,4096]{2,1,0:T(4,128)(2,1)S(1)} %get-tuple-element.64), channel_id=1, source_target_pairs={{0,1},{1,2},{2,3},{3,4},{4,5},{5,6},{6,7},{8,9},{9,10},{10,11},{11... | collective-permute-start | bytes 786440 | tf_op jit(solution)/shard_map/ppermute | solution.py:20
  12.9 11.2 %collective-permute-start.1 = (bf16[8,4,4096]{2,1,0:T(4,128)(2,1)S(1)}, bf16[8,4,4096]{2,1,0:T(4,128)(2,1)S(1)}, u32[]{:S(2)}, u32[]{:S(2)}) collective-permute-start(bf16[8,4,4096]{2,1,0:T(4,128)(2,1)S(1)} %get-tuple-element.65), channel_id=1, source_target_pairs={{1,0},{2,1},{3,2},{4,3},{5,4},{6,5},{7,6},{9,8},{10,9},{11,10},{12... | collective-permute-start | bytes 786440 | tf_op jit(solution)/shard_map/ppermute | solution.py:22
  443.9 146.0 %reduce-scatter.5.cloned.1.call-start = ((), (), s32[]{:S(2)}) async-start(), calls=%async_computation.5 | async-start | bytes 12582912 | tf_op jit(solution)/shard_map/reduce_scatter | solution.py:97
  589.8 74.7 %copy-start = (f32[4096]{0:T(1024)S(1)}, f32[4096]{0:T(1024)}, u32[]{:S(2)}) copy-start(f32[4096]{0:T(1024)} %param.6) | copy-start | bytes 49156
  608.5 53.6 %all-to-all-start = ((bf16[16,256,256]{2,1,0:T(8,128)(2,1)}), bf16[16,256,256]{2,1,0:T(8,128)(2,1)S(1)}, u32[]{:S(2)}, u32[]{:S(2)}) async-start(bf16[16,256,256]{2,1,0:T(8,128)(2,1)} %bitcast.38), calls=%async_computation.2 | async-start | bytes 4194304 | tf_op jit(solution)/shard_map/all_to_all | solution.py:102
Sparse Core Ops, SparseCore 0:
  444.0 18.5 reduce-scatter.2
  464.9 17.6 reduce-scatter.4
where the time goes:
time: 785 us; the launch traced here: 783 us
  other arithmetic  425 us (54%)
  local copies, waits for them, and re-layouts  147 us (19%)
  matrix products  73.5 us (9%)
  waiting for transfers between devices  57.2 us (7%)
  blocking collectives  54.3 us (7%)
  between operations  13.5 us (2%)
  starting transfers between devices  12.4 us (2%)
    reduce_sum x1, other arithmetic, body(): denominator = jnp.sum(weight, axis=0)  343 us
    dynamic_update_slice x16, local copies, waits for them, and re-layouts, cosine_table(): lax.map(lambda first_row: cosine_block(first_row, height, length), starts)  90.9 us
    dot_general x2, matrix products, contract(): lax.dot_general(left, right, (((left_dim,), (right_dim,)), ((), ())), pre...  56.3 us
    all_to_all x1, blocking collectives, body(): lax.all_to_all(back_cols, ('focus', 'strip'), split_axis=0, concat_axis=1...  54.3 us
    all_to_all x1, waiting for transfers between devices, body(): lax.all_to_all(along_cols, ('focus', 'strip'), split_axis=0, concat_axis=...  46.8 us
    slice x1, local copies, waits for them, and re-layouts, body(): center = padded[:, margin:-margin, :]  44.1 us
    convert_element_type x1, other arithmetic, body(): padded = extended(slices, (('strip', 1),), margin).astype(jnp.float32)  32.4 us
    convert_element_type x8, other arithmetic, cosine_block(): return table.reshape(height, length).astype(jnp.bfloat16)  30.1 us
  transfers between devices with their start and end apart: 5, of which 2 were waited for; matrix products, arithmetic and copies ran while one was open for 19% of the time, Pallas kernels for 0%

commit v1 on v0

v1 whole, which is shorter than its diff:
```python
import functools
import math

import jax
import jax.numpy as jnp
from jax import lax
from jax.experimental import pallas as pl
from jax.experimental.pallas import tpu as pltpu
from jax.sharding import PartitionSpec as P

floor_weight = 0.01
noise_ratio = 0.01
lane_block = 256
row_chunks = 2


def dot(left, right):
    return jnp.dot(left, right, preferred_element_type=jnp.float32)


def dot_last(left, right):
    return lax.dot_general(left, right, (((1,), (1,)), ((), ())), preferred_element_type=jnp.float32)


def edge_rows(slices, width):
    count = lax.axis_size("strip")
    ends = count - 1
    head = slices[:, :width, :]
    tail = slices[:, slices.shape[1] - width :, :]
    above = lax.ppermute(tail, "strip", [(i, i + 1) for i in range(ends)])
    below = lax.ppermute(head, "strip", [(i + 1, i) for i in range(ends)])
    return above, below


def band():
    source = lax.broadcasted_iota(jnp.int32, (256, 512), 0)
    column = lax.broadcasted_iota(jnp.int32, (256, 512), 1)
    which = column // 128
    offset = source - column % 128 - 64
    spacing = jnp.where(which == 0, 1, jnp.where(which == 1, 2, 4))
    lap = jnp.where(offset == 0, -4.0, jnp.where(jnp.abs(offset) == spacing, 1.0, 0.0))
    return jnp.where(which == 3, jnp.where(offset == 0, 1.0, 0.0), lap).astype(jnp.bfloat16)


def exchange_matrix():
    row = lax.broadcasted_iota(jnp.int32, (lane_block, lane_block), 0)
    column = lax.broadcasted_iota(jnp.int32, (lane_block, lane_block), 1)
    return (row + column == lane_block - 1).astype(jnp.bfloat16)


def stencil_kernel(
    place, main, above, below, head, tail, weights, out,
    edges, copies_a, copies_b, laps_a, laps_b, held,
    *, tile_rows, count, cols, tiles, step, parts,
):
    tile = place[0] + pl.program_id(0)
    first = tile == 0
    last = tile == tiles - 1
    edge_row = lax.broadcasted_iota(jnp.int32, (16, cols), 0)
    lane = lax.broadcasted_iota(jnp.int32, (step, 128), 1)
    for s in range(count):
        upper = jnp.where(first, head[s], above[s])
        lower = jnp.where(last, tail[s], below[s])
        edges[s] = jnp.where(edge_row < 8, lower, upper)
    frames = cols // 128 + 1
    copies = (copies_a, copies_b)
    laps = (laps_a, laps_b)

    def start_of(frame):
        return frame * 128 - 128 if isinstance(frame, int) else pl.multiple_of(frame * 128 - 128, 128)

    def window(source, frame, rows, low, high):
        size = (high - low) * rows
        if isinstance(frame, int) and frame == 0:
            piece = source[low:high, :, pl.ds(0, 128)].reshape(size, 128)
            return jnp.concatenate([jnp.zeros_like(piece), piece], axis=1)
        if isinstance(frame, int) and frame == frames - 1:
            piece = source[low:high, :, pl.ds(cols - 128, 128)].reshape(size, 128)
            return jnp.concatenate([piece, jnp.zeros_like(piece)], axis=1)
        return source[low:high, :, pl.ds(start_of(frame), 256)].reshape(size, 256)

    def spread_edges(slot, frame):
        rows = dot(window(edges, frame, 16, 0, count), weights[:, pl.ds(384, 128)])
        for s in range(count):
            copies[slot][s, pl.ds(0, 8), :] = rows[16 * s + 8 : 16 * s + 16]
            copies[slot][s, pl.ds(8 + tile_rows, 8), :] = rows[16 * s : 16 * s + 8]

    def spread(slot, frame, low, high):
        rows = dot(window(main, frame, tile_rows, low, high), weights[...])
        for s in range(low, high):
            at = (s - low) * tile_rows
            copies[slot][s, pl.ds(8, tile_rows), :] = rows[at : at + tile_rows, 384:]
            for k in range(3):
                laps[slot][s, k] = rows[at : at + tile_rows, 128 * k : 128 * k + 128]

    def gather(slot, frame, low, high):
        for r in range(low, high, step):
            numerator = jnp.zeros((step, 128), jnp.float32)
            denominator = numerator
            for s in range(count):
                centers = copies[slot]

                def lap(k, d):
                    pair = centers[s, pl.ds(8 + r + d, step), :] + centers[s, pl.ds(8 + r - d, step), :]
                    return laps[slot][s, k, pl.ds(r, step), :] + pair

                fine, middle, coarse = lap(0, 1), lap(1, 2), lap(2, 4)
                weight = floor_weight + (
                    fine * fine + 0.5 * (middle * middle + 0.5 * (coarse * coarse))
                )
                numerator += weight * centers[s, pl.ds(8 + r, step), :]
                denominator += weight
            for k, value in enumerate((numerator, denominator)):
                turned = pltpu.roll(value, 64, 1)
                if not (isinstance(frame, int) and frame == 0):
                    joined = jnp.where(lane < 64, held[k, pl.ds(r, step), :], turned)
                    out[k, pl.ds(r, step), pl.ds(start_of(frame), 128)] = joined
                held[k, pl.ds(r, step), :] = turned

    def both(slot, frame):
        spread_edges(slot, frame)
        for q in range(parts):
            spread(slot, frame, q * count // parts, (q + 1) * count // parts)
            gather(1 - slot, frame - 1, q * tile_rows // parts, (q + 1) * tile_rows // parts)

    spread_edges(0, 0)
    spread(0, 0, 0, count)
    both(1, 1)
    both(0, 2)

    def two(i, carry):
        both(1, 2 * i + 1)
        both(0, 2 * i + 2)
        return carry

    lax.fori_loop(1, frames // 2 - 1, two, 0)
    both(1, frames - 2)
    both(0, frames - 1)
    gather(0, frames - 1, 0, tile_rows)


def stencil(place, slices, head, tail, weights, out_rows):
    count, rows, cols = slices.shape
    tile_rows = math.gcd(128, out_rows)
    per = tile_rows // 16
    blocks = rows // 16
    step = min(16, tile_rows)
    parts = math.gcd(math.gcd(4, count), tile_rows // step)
    kernel = functools.partial(
        stencil_kernel, tile_rows=tile_rows, count=count, cols=cols, tiles=rows // tile_rows, step=step, parts=parts
    )
    edge = (count, 16, cols)
    grid_spec = pltpu.PrefetchScalarGridSpec(
        num_scalar_prefetch=1,
        grid=(out_rows // tile_rows,),
        in_specs=[
            pl.BlockSpec((count, tile_rows, cols), lambda t, at: (0, at[0] + t, 0)),
            pl.BlockSpec(edge, lambda t, at: (0, jnp.maximum((at[0] + t) * per - 1, 0), 0)),
            pl.BlockSpec(edge, lambda t, at: (0, jnp.minimum((at[0] + t) * per + per, blocks - 1), 0)),
            pl.BlockSpec(edge, lambda t, at: (0, 0, 0)),
            pl.BlockSpec(edge, lambda t, at: (0, 0, 0)),
            pl.BlockSpec((256, 512), lambda t, at: (0, 0)),
        ],
        out_specs=pl.BlockSpec((2, tile_rows, cols), lambda t, at: (0, t, 0)),
        scratch_shapes=[
            pltpu.VMEM(edge, jnp.bfloat16),
            pltpu.VMEM((count, tile_rows + 16, 128), jnp.float32),
            pltpu.VMEM((count, tile_rows + 16, 128), jnp.float32),
            pltpu.VMEM((count, 3, tile_rows, 128), jnp.float32),
            pltpu.VMEM((count, 3, tile_rows, 128), jnp.float32),
            pltpu.VMEM((2, tile_rows, 128), jnp.float32),
        ],
    )
    pixels = count * out_rows * cols
    return pl.pallas_call(
        kernel,
        grid_spec=grid_spec,
        out_shape=jax.ShapeDtypeStruct((2, out_rows, cols), jnp.float32),
        cost_estimate=pl.CostEstimate(flops=pixels * 2048, bytes_accessed=pixels * 3, transcendentals=0),
        compiler_params=pltpu.CompilerParams(vmem_limit_bytes=60 << 20),
        name="stencil",
    )(place, slices, slices, slices, head, tail, weights)


def table_kernel(near, turn, far, out, *, half):
    near_cos, near_sin = near[0, 0], near[0, 1]
    turn_cos, turn_sin = turn[0, 0], turn[0, 1]
    low_cos = near_cos * turn_cos - near_sin * turn_sin
    low_sin = near_sin * turn_cos + near_cos * turn_sin
    shape = low_cos.shape
    for j in range(half // 128):
        high_cos = jnp.broadcast_to(far[0, 0, :, j : j + 1], shape)
        high_sin = jnp.broadcast_to(far[0, 1, :, j : j + 1], shape)
        out[0, :, pl.ds(j * 128, 128)] = (high_cos * low_cos - high_sin * low_sin).astype(jnp.bfloat16)


def cosine_halves(length):
    half = length // 2
    rows = min(256, half)
    unit = jnp.float32(math.pi / (2 * length))

    def pair(phase, scale):
        angle = (phase % (4 * length)).astype(jnp.float32) * unit
        return jnp.stack([jnp.cos(angle) * scale, jnp.sin(angle) * scale], axis=1)

    def iota(shape, dim):
        return lax.broadcasted_iota(jnp.int32, shape, dim)

    odd = (2, rows, 128)
    near = pair((2 * iota(odd, 2) + 1) * (2 * iota(odd, 1) + iota(odd, 0)), 1.0)
    blocks = (half // rows, 1, 128)
    turn = pair((2 * iota(blocks, 2) + 1) * (2 * rows * iota(blocks, 0)), 1.0)
    steps = (2, half, half // 128)
    frequency = 2 * iota(steps, 1) + iota(steps, 0)
    norming = jnp.where(
        frequency == 0, jnp.float32(math.sqrt(1.0 / length)), jnp.float32(math.sqrt(2.0 / length))
    )
    far = pair(256 * iota(steps, 2) * frequency, norming)
    return pl.pallas_call(
        functools.partial(table_kernel, half=half),
        grid=(2, half // rows),
        in_specs=[
            pl.BlockSpec((1, 2, rows, 128), lambda p, b: (p, 0, 0, 0)),
            pl.BlockSpec((1, 2, 1, 128), lambda p, b: (b, 0, 0, 0)),
            pl.BlockSpec((1, 2, rows, half // 128), lambda p, b: (p, 0, b, 0)),
        ],
        out_specs=pl.BlockSpec((1, rows, half), lambda p, b: (p, b, 0)),
        out_shape=jax.ShapeDtypeStruct((2, half, half), jnp.bfloat16),
        name="cosines",
    )(near, turn, far)


def merge_kernel(own, other, mirror, out, *, cols):
    def merged(at):
        numerator = own[0, :, pl.ds(at, lane_block)] + other[0, :, pl.ds(at, lane_block)]
        denominator = own[1, :, pl.ds(at, lane_block)] + other[1, :, pl.ds(at, lane_block)]
        return (numerator / denominator).astype(jnp.bfloat16)

    for at in range(0, cols // 2, lane_block):
        near = merged(at).astype(jnp.float32)
        far = dot(merged(cols - lane_block - at), mirror[...])
        out[0, :, pl.ds(at, lane_block)] = (near + far).astype(jnp.bfloat16)
        out[1, :, pl.ds(at, lane_block)] = (near - far).astype(jnp.bfloat16)


def merge(own, other, mirror):
    _, rows, cols = own.shape
    tile = min(64, rows)
    return pl.pallas_call(
        functools.partial(merge_kernel, cols=cols),
        grid=(rows // tile,),
        in_specs=[
            pl.BlockSpec((2, tile, cols), lambda t: (0, t, 0)),
            pl.BlockSpec((2, tile, cols), lambda t: (0, t, 0)),
            pl.BlockSpec((lane_block, lane_block), lambda t: (0, 0)),
        ],
        out_specs=pl.BlockSpec((2, tile, cols // 2), lambda t: (0, t, 0)),
        out_shape=jax.ShapeDtypeStruct((2, rows, cols // 2), jnp.bfloat16),
        name="merge",
    )(own, other, mirror)


def rows_kernel(table, folded, out):
    values = dot_last(table[0], folded[0]).astype(jnp.bfloat16)
    out[...] = values.reshape(out.shape)


def transform_rows(table, folded, parity, devices):
    _, rows, half = folded.shape
    own = half // devices
    tile = max(256, own)
    return pl.pallas_call(
        rows_kernel,
        grid=(half // tile,),
        in_specs=[
            pl.BlockSpec((1, tile, half), lambda t: (parity, t, 0)),
            pl.BlockSpec((1, rows, half), lambda t: (parity, 0, 0)),
        ],
        out_specs=pl.BlockSpec((tile // own, own, rows), lambda t: (t, 0, 0)),
        out_shape=jax.ShapeDtypeStruct((devices, own, rows), jnp.bfloat16),
        name="transform_rows",
    )(table, folded)


def columns_kernel(*refs, chunks, half, order):
    table, rows_response, cols_response, mirror = refs[:4]
    arrived = refs[4 : 4 + chunks]
    out, folded, total = refs[4 + chunks :]
    parity = pl.program_id(0)
    step = pl.program_id(1)
    blocks = half // lane_block

    @pl.when((parity == 0) & (step == 0))
    def _():
        for j in range(blocks):
            near = jnp.concatenate([part[order[j]] for part in arrived], axis=1).astype(jnp.float32)
            far = dot(
                jnp.concatenate([part[order[2 * blocks - 1 - j]] for part in arrived], axis=1), mirror[...]
            )
            folded[0, :, pl.ds(j * lane_block, lane_block)] = (near + far).astype(jnp.bfloat16)
            folded[1, :, pl.ds(j * lane_block, lane_block)] = (near - far).astype(jnp.bfloat16)

    spectrum = dot_last(folded[parity], table[0])
    response = cols_response[...] * rows_response[0]
    filtered = (spectrum * (response / (response * response + noise_ratio))).astype(jnp.bfloat16)
    part = dot(filtered, table[0])

    @pl.when(step == 0)
    def _():
        total[parity] = part

    @pl.when(step > 0)
    def _():
        total[parity] += part

    @pl.when((parity == 1) & (step == pl.num_programs(1) - 1))
    def _():
        for j in range(blocks):
            even = total[0, :, pl.ds(j * lane_block, lane_block)]
            odd = total[1, :, pl.ds(j * lane_block, lane_block)]
            out[j] = (even + odd).astype(jnp.bfloat16)
            out[2 * blocks - 1 - j] = dot((even - odd).astype(jnp.bfloat16), mirror[...]).astype(jnp.bfloat16)


def filter_columns(table, rows_response, cols_response, mirror, arrived, order):
    half = table.shape[1]
    blocks, own, _ = arrived[0].shape
    tile = min(256, half)
    chunks = len(arrived)
    whole = pl.BlockSpec((blocks, own, lane_block // chunks), lambda p, t: (0, 0, 0))
    return pl.pallas_call(
        functools.partial(columns_kernel, chunks=chunks, half=half, order=order),
        grid=(2, half // tile),
        in_specs=[
            pl.BlockSpec((1, tile, half), lambda p, t: (p, t, 0)),
            pl.BlockSpec((1, 1, tile), lambda p, t: (p, 0, t)),
            pl.BlockSpec((own, 1), lambda p, t: (0, 0)),
            pl.BlockSpec((lane_block, lane_block), lambda p, t: (0, 0)),
        ]
        + [whole] * chunks,
        out_specs=pl.BlockSpec((blocks, own, lane_block), lambda p, t: (0, 0, 0)),
        out_shape=jax.ShapeDtypeStruct((blocks, own, lane_block), jnp.bfloat16),
        scratch_shapes=[
            pltpu.VMEM((2, own, half), jnp.bfloat16),
            pltpu.VMEM((2, own, half), jnp.float32),
        ],
        compiler_params=pltpu.CompilerParams(vmem_limit_bytes=60 << 20),
        name="filter_columns",
    )(table, rows_response, cols_response, mirror, *arrived)


def turn(values):
    return jnp.transpose(values.astype(jnp.float32)).astype(jnp.bfloat16)


def even_kernel(table, arrived, out, turned, *, half):
    @pl.when(pl.program_id(0) == 0)
    def _():
        rows = arrived.shape[2]
        turned[...] = turn(arrived[...].reshape(half, rows))

    out[...] = dot(turned[...], table[0])


def restore_even(table, arrived):
    half = table.shape[1]
    devices, own, rows = arrived.shape
    tile = min(256, half)
    return pl.pallas_call(
        functools.partial(even_kernel, half=half),
        grid=(half // tile,),
        in_specs=[
            pl.BlockSpec((1, half, tile), lambda t: (0, 0, t)),
            pl.BlockSpec((devices, own, rows), lambda t: (0, 0, 0)),
        ],
        out_specs=pl.BlockSpec((rows, tile), lambda t: (0, t)),
        out_shape=jax.ShapeDtypeStruct((rows, half), jnp.float32),
        scratch_shapes=[pltpu.VMEM((rows, half), jnp.bfloat16)],
        compiler_params=pltpu.CompilerParams(vmem_limit_bytes=60 << 20),
        name="restore_even",
    )(table, arrived)


def odd_kernel(table, arrived, even, mirror, out, turned, *, half, tile):
    step = pl.program_id(0)

    @pl.when(step == 0)
    def _():
        rows = arrived.shape[2]
        turned[...] = turn(arrived[...].reshape(half, rows))

    odd = dot(turned[...], table[0])
    out[:, pl.ds(pl.multiple_of(step * tile, tile), tile)] = even[...] + odd
    left = even[...] - odd
    back = jnp.zeros_like(left)
    for _ in range(3):
        piece = left.astype(jnp.bfloat16)
        back += dot(piece, mirror[...])
        left = left - piece.astype(jnp.float32)
    out[:, pl.ds(pl.multiple_of(2 * half - tile - step * tile, tile), tile)] = back


def restore(table, arrived, even, mirror):
    half = table.shape[1]
    devices, own, rows = arrived.shape
    tile = lane_block
    return pl.pallas_call(
        functools.partial(odd_kernel, half=half, tile=tile),
        grid=(half // tile,),
        in_specs=[
            pl.BlockSpec((1, half, tile), lambda t: (1, 0, t)),
            pl.BlockSpec((devices, own, rows), lambda t: (0, 0, 0)),
            pl.BlockSpec((rows, tile), lambda t: (0, t)),
            pl.BlockSpec((lane_block, lane_block), lambda t: (0, 0)),
        ],
        out_specs=pl.BlockSpec((rows, 2 * half), lambda t: (0, 0)),
        out_shape=jax.ShapeDtypeStruct((rows, 2 * half), jnp.float32),
        scratch_shapes=[pltpu.VMEM((rows, half), jnp.bfloat16)],
        compiler_params=pltpu.CompilerParams(vmem_limit_bytes=60 << 20),
        name="restore",
    )(table, arrived, even, mirror)


def body(slices, otf_rows, otf_cols):
    axes = ("focus", "strip")
    focus_count = lax.axis_size("focus")
    devices = focus_count * lax.axis_size("strip")
    rows, length = slices.shape[1:]
    half = length // 2
    piece = length // devices
    above, below = edge_rows(slices, 4)
    table = cosine_halves(length)
    head = jnp.pad(above, ((0, 0), (12, 0), (0, 0)))
    tail = jnp.pad(below, ((0, 0), (0, 12), (0, 0)))
    weights = band()
    mirror = exchange_matrix()
    focus = lax.axis_index("focus")
    chunks = row_chunks if piece % (16 * row_chunks) == 0 else 1
    if piece // chunks * chunks != piece or piece < lane_block:
        chunks = 1
    chunk_rows = piece // chunks
    tile_rows = math.gcd(128, chunk_rows)
    swap = [(i, focus_count - 1 - i) for i in range(focus_count)]
    arrived = ([], [])
    for chunk in range(chunks):
        def sums(half_index):
            place = (half_index * piece + chunk * chunk_rows) // tile_rows
            return stencil(place.astype(jnp.int32).reshape(1), slices, head, tail, weights, chunk_rows)

        sent = sums(focus_count - 1 - focus)
        received = lax.ppermute(sent, "focus", swap)
        own = sums(focus)
        folded = merge(own, received, mirror)
        for parity in range(2):
            along = transform_rows(table, folded, parity, devices)
            moved = lax.all_to_all(along, axes, split_axis=0, concat_axis=0, tiled=True)
            arrived[parity].append(moved)
    blocks = length // lane_block
    per = lane_block // piece
    owner = focus * lax.axis_size("strip") + lax.axis_index("strip")
    own = half // devices
    rows_response = otf_rows.reshape(half, 2).T.reshape(2, 1, half)
    local_cols = lax.dynamic_slice_in_dim(otf_cols.reshape(half, 2), owner * own, own, 0)
    strips = devices // focus_count
    order = [b % focus_count * strips + b // focus_count if per == 1 else b for b in range(blocks)]
    restored = []
    for parity in range(2):
        parts = arrived[parity]
        if per > 1:
            parts = [
                part.reshape(focus_count, devices // focus_count, own, piece)
                .transpose(1, 0, 2, 3)
                .reshape(blocks, per, own, piece)
                .transpose(0, 2, 1, 3)
                .reshape(blocks, own, lane_block)
                for part in parts
            ]
        back = filter_columns(table, rows_response, local_cols[:, parity : parity + 1], mirror, parts, order)
        if per > 1:
            back = back.reshape(blocks, own, per, piece).transpose(0, 2, 1, 3).reshape(devices, own, piece)
        restored.append(lax.all_to_all(back, axes, split_axis=0, concat_axis=0, tiled=True))
    even = restore_even(table, restored[0])
    return restore(table, restored[1], even, mirror)


def solution(mesh):
    in_specs = (P(("field", "focus"), "strip", None), P(), P())
    out_specs = P(("field", "focus", "strip"), None)
    return jax.shard_map(body, mesh=mesh, in_specs=in_specs, out_specs=out_specs, check_vma=False)
```

time: 785 us -> 341 us (0.43)
  other arithmetic: 425 us -> 5.54 us
  Pallas kernels: 0 us -> 239 us
  local copies, waits for them, and re-layouts: 147 us -> 11.1 us
  matrix products: 73.5 us -> 0 us
  blocking collectives: 54.3 us -> 0 us
  starting transfers between devices: 12.4 us -> 35.8 us
  between operations: 13.5 us -> 0.23 us
  waiting for transfers between devices: 57.2 us -> 46.3 us
    reduce_sum x1 -> x0, other arithmetic: 343 us -> none  [body(): denominator = jnp.sum(weight, axis=0)]
    pallas_call x0 -> x15, Pallas kernels: none -> 239 us  [the longest x4 111 us: stencil(): pl.pallas_call(kernel, grid_spec=grid_spec, out_shape=jax.ShapeDtypeStruc...]
    dynamic_update_slice x16 -> x0, local copies, waits for them, and re-layouts: 90.9 us -> none  [cosine_table(): lax.map(lambda first_row: cosine_block(first_row, height, length), starts)]
    dot_general x3 -> x0, matrix products: 73.5 us -> none  [the longest x2 56.3 us: contract(): lax.dot_general(left, right, (((left_dim,), (right_dim,)), ((), ())), pre...]
    convert_element_type x9 -> x3, other arithmetic: 62.5 us -> 1.67 us  [the longest x1 0.91 us: band(): jnp.where(which == 3, jnp.where(offset == 0, 1.0, 0.0), lap)]
    all_to_all x1 -> x0, blocking collectives: 54.3 us -> none  [body(): lax.all_to_all(back_cols, ('focus', 'strip'), split_axis=0, concat_axis=1...]
    slice x2, local copies, waits for them, and re-layouts: 45.5 us -> 2.16 us  [the longest x1 1.45 us: edge_rows(): head = slices[:, :width, :]]
    all_to_all x1 -> x6, starting transfers between devices: 6.01 us -> 28.5 us  [the longest x4 19.2 us: body(): moved = lax.all_to_all(along, axes, split_axis=0, concat_axis=0, tiled=True)]
  transfers between devices with their start and end apart: 5 -> 10, of which waited for: 2 -> 5; matrix products, arithmetic and copies ran while one was open for 19% -> 4% of each run, Pallas kernels for 0% -> 59%
where the time goes in v1:
time: 341 us; the launch traced here: 338 us
  Pallas kernels  239 us (70%)
  waiting for transfers between devices  46.3 us (14%)
  starting transfers between devices  35.8 us (10%)
  local copies, waits for them, and re-layouts  11.1 us (3%)
  other arithmetic  5.54 us (2%)
    pallas_call x4, Pallas kernels, stencil(): pl.pallas_call(kernel, grid_spec=grid_spec, out_shape=jax.ShapeDtypeStruc...  111 us
    pallas_call x2, Pallas kernels, filter_columns(): pl.pallas_call(functools.partial(columns_kernel, chunks=chunks, half=half...  42.7 us
    pallas_call x4, Pallas kernels, transform_rows(): pl.pallas_call(rows_kernel, grid=(half // tile,), in_specs=[pl.BlockSpec(...  33.3 us
    all_to_all x2, waiting for transfers between devices, body(): lax.all_to_all(back, axes, split_axis=0, concat_axis=0, tiled=True)  22.3 us
    pallas_call x1, Pallas kernels, cosine_halves(): pl.pallas_call(functools.partial(table_kernel, half=half), grid=(2, half...  21.7 us
    all_to_all x4, starting transfers between devices, body(): moved = lax.all_to_all(along, axes, split_axis=0, concat_axis=0, tiled=True)  19.2 us
    all_to_all x4, waiting for transfers between devices, body(): moved = lax.all_to_all(along, axes, split_axis=0, concat_axis=0, tiled=True)  14.9 us
    pallas_call x1, Pallas kernels, restore(): pl.pallas_call(functools.partial(odd_kernel, half=half, tile=tile), grid=...  12.1 us
  transfers between devices with their start and end apart: 10, of which 5 were waited for; matrix products, arithmetic and copies ran while one was open for 4% of the time, Pallas kernels for 59%

profile of v1, /device:TPU:0, one launch (start us, length us, event | category | flops | bytes accessed | tf_op | source)
XLA Modules:
  0.0 338.4 jit_solution(5395890503077731049)
XLA Ops:
  0.0 1.5 fusion.19
  1.5 1.3 collective-permute-start.1
  2.8 5.5 %collective-permute-start = (bf16[8,4,4096]{2,1,0:T(4,128)(2,1)S(1)}, bf16[8,4,4096]{2,1,0:T(4,128)(2,1)S(1)}, u32[]{:S(2)}, u32[]{:S(2)}) collective-permute-start(bf16[8,4,4096]{2,1,0:T(4,128)(2,1)S(1)} %get-tuple-element.6), channel_id=1, source_target_pairs={{0,1},{1,2},{2,3},{3,4},{4,5},{5,6},{6,7},{8,9},{9,10},{10,11},{11... | collective-permute-start | bytes 786440 | tf_op jit(solution)/shard_map/ppermute | solution.py:30
  9.3 9.2 %collective-permute-done = bf16[8,4,4096]{2,1,0:T(4,128)(2,1)S(1)} collective-permute-done((bf16[8,4,4096]{2,1,0:T(4,128)(2,1)S(1)}, bf16[8,4,4096]{2,1,0:T(4,128)(2,1)S(1)}, u32[]{:S(2)}, u32[]{:S(2)}) %collective-permute-start) | collective-permute-done | bytes 262176 | tf_op jit(solution)/shard_map/ppermute | solution.py:30
  18.4 1.2 pad.8.head
  20.7 27.8 %stencil.7 = f32[2,128,4096]{2,1,0:T(8,128)} custom-call(s32[1]{0:T(128)} %bitcast.5.place, bf16[8,512,4096]{2,1,0:T(8,128)(2,1)} %below.7, bf16[8,512,4096]{2,1,0:T(8,128)(2,1)} %below.7, bf16[8,512,4096]{2,1,0:T(8,128)(2,1)} %below.7, bf16[8,16,4096]{2,1,0:T(8,128)(2,1)} %pad.8.head, bf16[8,16,4096]{2,1,0:T(8,128)(2,1)} %pad.9.tail, ...), custom_call_target="tpu_custom_call" | custom-call | flops 8589934592 | bytes 12582912 | tf_op jit(solution)/shard_map/stencil/pallas_call | solution.py:175
  48.5 1.1 select_multiply_fusion.1
  49.6 27.7 %stencil.5 = f32[2,128,4096]{2,1,0:T(8,128)} custom-call(s32[1]{0:T(128)} %bitcast.3.place, bf16[8,512,4096]{2,1,0:T(8,128)(2,1)} %below.7, bf16[8,512,4096]{2,1,0:T(8,128)(2,1)} %below.7, bf16[8,512,4096]{2,1,0:T(8,128)(2,1)} %below.7, bf16[8,16,4096]{2,1,0:T(8,128)(2,1)} %pad.8.head, bf16[8,16,4096]{2,1,0:T(8,128)(2,1)} %pad.9.tail, ...), custom_call_target="tpu_custom_call" | custom-call | flops 8589934592 | bytes 12582912 | tf_op jit(solution)/shard_map/stencil/pallas_call | solution.py:175
  77.8 2.7 copy.8.far
  83.3 21.7 %cosines.1.table.refs_0_ = bf16[2,2048,2048]{2,1,0:T(8,128)(2,1)} custom-call(f32[2,2,256,128]{3,2,1,0:T(8,128)} %pad_maximum_fusion.near, f32[8,2,1,128]{3,2,1,0:T(1,128)} %pad_maximum_fusion.2.turn, f32[2,2,2048,16]{3,2,1,0:T(8,128)} %copy.8.far), custom_call_target="tpu_custom_call" | custom-call | tf_op jit(solution)/shard_map/cosines/pallas_call | solution.py:219
  105.7 27.7 %stencil.6.own = f32[2,128,4096]{2,1,0:T(8,128)} custom-call(s32[1]{0:T(128)} %bitcast.4.place, bf16[8,512,4096]{2,1,0:T(8,128)(2,1)} %below.7, bf16[8,512,4096]{2,1,0:T(8,128)(2,1)} %below.7, bf16[8,512,4096]{2,1,0:T(8,128)(2,1)} %below.7, bf16[8,16,4096]{2,1,0:T(8,128)(2,1)} %pad.8.head, bf16[8,16,4096]{2,1,0:T(8,128)(2,1)} %pad.9.tail, ...), custom_call_target="tpu_custom_call" | custom-call | flops 8589934592 | bytes 12582912 | tf_op jit(solution)/shard_map/stencil/pallas_call | solution.py:175
  133.4 4.7 %merge.3.folded = bf16[2,128,2048]{2,1,0:T(8,128)(2,1)} custom-call(f32[2,128,4096]{2,1,0:T(8,128)} %stencil.6.own, f32[2,128,4096]{2,1,0:T(8,128)} %collective-permute-done.3.other, bf16[256,256]{1,0:T(8,128)(2,1)} %fusion.8.mirror.refs_3_), custom_call_target="tpu_custom_call" | custom-call | tf_op jit(solution)/shard_map/merge/pallas_call | solution.py:249
  138.0 8.3 %transform_rows.5 = bf16[16,128,128]{2,1,0:T(8,128)(2,1)} custom-call(bf16[2,2048,2048]{2,1,0:T(8,128)(2,1)} %cosines.1.table.refs_0_, bf16[2,128,2048]{2,1,0:T(8,128)(2,1)} %merge.3.folded), custom_call_target="tpu_custom_call" | custom-call | tf_op jit(solution)/shard_map/transform_rows/pallas_call | solution.py:272
  146.4 5.9 %all-to-all-start.1 = ((bf16[16,128,128]{2,1,0:T(8,128)(2,1)}), bf16[16,128,128]{2,1,0:T(8,128)(2,1)S(1)}, u32[]{:S(2)}, u32[]{:S(2)}) async-start(bf16[16,128,128]{2,1,0:T(8,128)(2,1)} %transform_rows.5), calls=%async_computation.1 | async-start | bytes 1048576 | tf_op jit(solution)/shard_map/all_to_all | solution.py:456
  152.3 8.3 %transform_rows.7 = bf16[16,128,128]{2,1,0:T(8,128)(2,1)} custom-call(bf16[2,2048,2048]{2,1,0:T(8,128)(2,1)} %cosines.1.table.refs_0_, bf16[2,128,2048]{2,1,0:T(8,128)(2,1)} %merge.3.folded), custom_call_target="tpu_custom_call" | custom-call | tf_op jit(solution)/shard_map/transform_rows/pallas_call | solution.py:272
  160.6 7.5 %all-to-all-done.1.refs_5_ = bf16[16,128,128]{2,1,0:T(8,128)(2,1)S(1)} async-done(((bf16[16,128,128]{2,1,0:T(8,128)(2,1)}), bf16[16,128,128]{2,1,0:T(8,128)(2,1)S(1)}, u32[]{:S(2)}, u32[]{:S(2)}) %all-to-all-start.1) | async-done | bytes 524320 | tf_op jit(solution)/shard_map/all_to_all | solution.py:456
  168.1 3.6 %all-to-all-start.4 = ((bf16[16,128,128]{2,1,0:T(8,128)(2,1)}), bf16[16,128,128]{2,1,0:T(8,128)(2,1)S(1)}, u32[]{:S(2)}, u32[]{:S(2)}) async-start(bf16[16,128,128]{2,1,0:T(8,128)(2,1)} %transform_rows.7), calls=%async_computation.4 | async-start | bytes 1048576 | tf_op jit(solution)/shard_map/all_to_all | solution.py:456
  171.6 27.7 %stencil.4.own = f32[2,128,4096]{2,1,0:T(8,128)} custom-call(s32[1]{0:T(128)} %bitcast.2.place, bf16[8,512,4096]{2,1,0:T(8,128)(2,1)} %below.7, bf16[8,512,4096]{2,1,0:T(8,128)(2,1)} %below.7, bf16[8,512,4096]{2,1,0:T(8,128)(2,1)} %below.7, bf16[8,16,4096]{2,1,0:T(8,128)(2,1)} %pad.8.head, bf16[8,16,4096]{2,1,0:T(8,128)(2,1)} %pad.9.tail, ...), custom_call_target="tpu_custom_call" | custom-call | flops 8589934592 | bytes 12582912 | tf_op jit(solution)/shard_map/stencil/pallas_call | solution.py:175
  199.3 4.7 %merge.2.folded = bf16[2,128,2048]{2,1,0:T(8,128)(2,1)} custom-call(f32[2,128,4096]{2,1,0:T(8,128)} %stencil.4.own, f32[2,128,4096]{2,1,0:T(8,128)} %collective-permute-done.2.other, bf16[256,256]{1,0:T(8,128)(2,1)} %fusion.8.mirror.refs_3_), custom_call_target="tpu_custom_call" | custom-call | tf_op jit(solution)/shard_map/merge/pallas_call | solution.py:249
  204.0 8.3 %transform_rows.6 = bf16[16,128,128]{2,1,0:T(8,128)(2,1)} custom-call(bf16[2,2048,2048]{2,1,0:T(8,128)(2,1)} %cosines.1.table.refs_0_, bf16[2,128,2048]{2,1,0:T(8,128)(2,1)} %merge.2.folded), custom_call_target="tpu_custom_call" | custom-call | tf_op jit(solution)/shard_map/transform_rows/pallas_call | solution.py:272
  212.4 5.9 %all-to-all-start.3 = ((bf16[16,128,128]{2,1,0:T(8,128)(2,1)}), bf16[16,128,128]{2,1,0:T(8,128)(2,1)S(1)}, u32[]{:S(2)}, u32[]{:S(2)}) async-start(bf16[16,128,128]{2,1,0:T(8,128)(2,1)} %transform_rows.6), calls=%async_computation.3 | async-start | bytes 1048576 | tf_op jit(solution)/shard_map/all_to_all | solution.py:456
  218.3 8.3 %transform_rows.4 = bf16[16,128,128]{2,1,0:T(8,128)(2,1)} custom-call(bf16[2,2048,2048]{2,1,0:T(8,128)(2,1)} %cosines.1.table.refs_0_, bf16[2,128,2048]{2,1,0:T(8,128)(2,1)} %merge.2.folded), custom_call_target="tpu_custom_call" | custom-call | tf_op jit(solution)/shard_map/transform_rows/pallas_call | solution.py:272
  226.7 7.4 %all-to-all-done.3.refs_4_ = bf16[16,128,128]{2,1,0:T(8,128)(2,1)S(1)} async-done(((bf16[16,128,128]{2,1,0:T(8,128)(2,1)}), bf16[16,128,128]{2,1,0:T(8,128)(2,1)S(1)}, u32[]{:S(2)}, u32[]{:S(2)}) %all-to-all-start.3) | async-done | bytes 524320 | tf_op jit(solution)/shard_map/all_to_all | solution.py:456
  234.1 3.8 %all-to-all-start = ((bf16[16,128,128]{2,1,0:T(8,128)(2,1)}), bf16[16,128,128]{2,1,0:T(8,128)(2,1)S(1)}, u32[]{:S(2)}, u32[]{:S(2)}) async-start(bf16[16,128,128]{2,1,0:T(8,128)(2,1)} %transform_rows.4), calls=%async_computation | async-start | bytes 1048576 | tf_op jit(solution)/shard_map/all_to_all | solution.py:456
  241.6 21.3 %filter_columns.3 = bf16[16,128,256]{2,1,0:T(8,128)(2,1)} custom-call(bf16[2,2048,2048]{2,1,0:T(8,128)(2,1)} %cosines.1.table.refs_0_, f32[2,1,2048]{2,1,0:T(1,128)} %reshape.262.refs_1_, f32[128,1]{1,0:T(8,128)} %get-tuple-element.7.refs_2_, bf16[256,256]{1,0:T(8,128)(2,1)} %fusion.8.mirror.refs_3_, bf16[16,128,128]{2,1,0:T(8,128)(2,1)} %copy-done.5, ...), custom_call_target="tpu_custom_call" | custom-call | tf_op jit(solution)/shard_map/filter_columns/pallas_call | solution.py:331
  263.0 5.7 %all-to-all-start.5 = ((bf16[16,128,256]{2,1,0:T(8,128)(2,1)}), bf16[16,128,256]{2,1,0:T(8,128)(2,1)S(1)}, u32[]{:S(2)}, u32[]{:S(2)}) async-start(bf16[16,128,256]{2,1,0:T(8,128)(2,1)} %filter_columns.3), calls=%async_computation.5 | async-start | bytes 2097152 | tf_op jit(solution)/shard_map/all_to_all | solution.py:481
  268.6 21.4 %filter_columns.2 = bf16[16,128,256]{2,1,0:T(8,128)(2,1)} custom-call(bf16[2,2048,2048]{2,1,0:T(8,128)(2,1)} %cosines.1.table.refs_0_, f32[2,1,2048]{2,1,0:T(1,128)} %reshape.262.refs_1_, f32[128,1]{1,0:T(8,128)} %get-tuple-element.8.refs_2_, bf16[256,256]{1,0:T(8,128)(2,1)} %fusion.8.mirror.refs_3_, bf16[16,128,128]{2,1,0:T(8,128)(2,1)} %copy-done.4, ...), custom_call_target="tpu_custom_call" | custom-call | tf_op jit(solution)/shard_map/filter_columns/pallas_call | solution.py:331
  290.0 5.2 %all-to-all-done.5.arrived = bf16[16,128,256]{2,1,0:T(8,128)(2,1)S(1)} async-done(((bf16[16,128,256]{2,1,0:T(8,128)(2,1)}), bf16[16,128,256]{2,1,0:T(8,128)(2,1)S(1)}, u32[]{:S(2)}, u32[]{:S(2)}) %all-to-all-start.5) | async-done | bytes 1048608 | tf_op jit(solution)/shard_map/all_to_all | solution.py:481
  295.2 3.7 %all-to-all-start.2 = ((bf16[16,128,256]{2,1,0:T(8,128)(2,1)}), bf16[16,128,256]{2,1,0:T(8,128)(2,1)S(1)}, u32[]{:S(2)}, u32[]{:S(2)}) async-start(bf16[16,128,256]{2,1,0:T(8,128)(2,1)} %filter_columns.2), calls=%async_computation.2 | async-start | bytes 2097152 | tf_op jit(solution)/shard_map/all_to_all | solution.py:481
  298.8 9.3 %restore_even.1.even = f32[256,2048]{1,0:T(8,128)} custom-call(bf16[2,2048,2048]{2,1,0:T(8,128)(2,1)} %cosines.1.table.refs_0_, bf16[16,128,256]{2,1,0:T(8,128)(2,1)} %copy-done), custom_call_target="tpu_custom_call" | custom-call | tf_op jit(solution)/shard_map/restore_even/pallas_call | solution.py:369
  308.1 17.1 %all-to-all-done.2.arrived = bf16[16,128,256]{2,1,0:T(8,128)(2,1)S(1)} async-done(((bf16[16,128,256]{2,1,0:T(8,128)(2,1)}), bf16[16,128,256]{2,1,0:T(8,128)(2,1)S(1)}, u32[]{:S(2)}, u32[]{:S(2)}) %all-to-all-start.2) | async-done | bytes 1048608 | tf_op jit(solution)/shard_map/all_to_all | solution.py:481
  326.3 12.1 %restore.1 = f32[256,4096]{1,0:T(8,128)} custom-call(bf16[2,2048,2048]{2,1,0:T(8,128)(2,1)} %cosines.1.table.refs_0_, bf16[16,128,256]{2,1,0:T(8,128)(2,1)} %copy-done.1, f32[256,2048]{1,0:T(8,128)} %restore_even.1.even, bf16[256,256]{1,0:T(8,128)(2,1)} %fusion.8.mirror.refs_3_), custom_call_target="tpu_custom_call" | custom-call | tf_op jit(solution)/shard_map/restore/pallas_call | solution.py:407
  (45 shorter events, 10.7 us)
Async XLA Ops:
  1.5 18.1 %collective-permute-start.1 = (bf16[8,4,4096]{2,1,0:T(4,128)(2,1)S(1)}, bf16[8,4,4096]{2,1,0:T(4,128)(2,1)S(1)}, u32[]{:S(2)}, u32[]{:S(2)}) collective-permute-start(bf16[8,4,4096]{2,1,0:T(4,128)(2,1)S(1)} %get-tuple-element.5), channel_id=1, source_target_pairs={{1,0},{2,1},{3,2},{4,3},{5,4},{6,5},{7,6},{9,8},{10,9},{11,10},{12... | collective-permute-start | bytes 786440 | tf_op jit(solution)/shard_map/ppermute | solution.py:31
  2.8 15.7 %collective-permute-start = (bf16[8,4,4096]{2,1,0:T(4,128)(2,1)S(1)}, bf16[8,4,4096]{2,1,0:T(4,128)(2,1)S(1)}, u32[]{:S(2)}, u32[]{:S(2)}) collective-permute-start(bf16[8,4,4096]{2,1,0:T(4,128)(2,1)S(1)} %get-tuple-element.6), channel_id=1, source_target_pairs={{0,1},{1,2},{2,3},{3,4},{4,5},{5,6},{6,7},{8,9},{9,10},{10,11},{11... | collective-permute-start | bytes 786440 | tf_op jit(solution)/shard_map/ppermute | solution.py:30
  48.5 84.9 %collective-permute-start.3 = (f32[2,128,4096]{2,1,0:T(8,128)}, f32[2,128,4096]{2,1,0:T(8,128)}, u32[]{:S(2)}, u32[]{:S(2)}) collective-permute-start(f32[2,128,4096]{2,1,0:T(8,128)} %stencil.7), channel_id=1, source_target_pairs={{0,8},{8,0},{1,9},{9,1},{2,10},{10,2},{3,11},{11,3},{4,12},{12,4},... | collective-permute-start | bytes 12582920 | tf_op jit(solution)/shard_map/ppermute | solution.py:451
  77.3 122.0 %collective-permute-start.2 = (f32[2,128,4096]{2,1,0:T(8,128)}, f32[2,128,4096]{2,1,0:T(8,128)}, u32[]{:S(2)}, u32[]{:S(2)}) collective-permute-start(f32[2,128,4096]{2,1,0:T(8,128)} %stencil.5), channel_id=1, source_target_pairs={{0,8},{8,0},{1,9},{9,1},{2,10},{10,2},{3,11},{11,3},{4,12},{12,4},... | collective-permute-start | bytes 12582920 | tf_op jit(solution)/shard_map/ppermute | solution.py:451
  146.4 21.7 %all-to-all-start.1 = ((bf16[16,128,128]{2,1,0:T(8,128)(2,1)}), bf16[16,128,128]{2,1,0:T(8,128)(2,1)S(1)}, u32[]{:S(2)}, u32[]{:S(2)}) async-start(bf16[16,128,128]{2,1,0:T(8,128)(2,1)} %transform_rows.5), calls=%async_computation.1 | async-start | bytes 1048576 | tf_op jit(solution)/shard_map/all_to_all | solution.py:456
  168.0 31.3 %copy-start.2 = (bf16[16,128,128]{2,1,0:T(8,128)(2,1)}, bf16[16,128,128]{2,1,0:T(8,128)(2,1)S(1)}, u32[]{:S(2)}) copy-start(bf16[16,128,128]{2,1,0:T(8,128)(2,1)S(1)} %all-to-all-done.1.refs_5_) | copy-start | bytes 1572868
  168.1 44.3 %all-to-all-start.4 = ((bf16[16,128,128]{2,1,0:T(8,128)(2,1)}), bf16[16,128,128]{2,1,0:T(8,128)(2,1)S(1)}, u32[]{:S(2)}, u32[]{:S(2)}) async-start(bf16[16,128,128]{2,1,0:T(8,128)(2,1)} %transform_rows.7), calls=%async_computation.4 | async-start | bytes 1048576 | tf_op jit(solution)/shard_map/all_to_all | solution.py:456
  212.4 14.3 %copy-start.3 = (bf16[16,128,128]{2,1,0:T(8,128)(2,1)}, bf16[16,128,128]{2,1,0:T(8,128)(2,1)S(1)}, u32[]{:S(2)}) copy-start(bf16[16,128,128]{2,1,0:T(8,128)(2,1)S(1)} %all-to-all-done.4.refs_5_) | copy-start | bytes 1572868
  212.4 21.7 %all-to-all-start.3 = ((bf16[16,128,128]{2,1,0:T(8,128)(2,1)}), bf16[16,128,128]{2,1,0:T(8,128)(2,1)S(1)}, u32[]{:S(2)}, u32[]{:S(2)}) async-start(bf16[16,128,128]{2,1,0:T(8,128)(2,1)} %transform_rows.6), calls=%async_computation.3 | async-start | bytes 1048576 | tf_op jit(solution)/shard_map/all_to_all | solution.py:456
  218.3 19.6 %copy-start.6 = (f32[4096]{0:T(1024)S(1)}, f32[4096]{0:T(1024)}, u32[]{:S(2)}) copy-start(f32[4096]{0:T(1024)} %param.4) | copy-start | bytes 49156
  218.3 21.6 %copy-start.7 = (f32[4096]{0:T(1024)S(1)}, f32[4096]{0:T(1024)}, u32[]{:S(2)}) copy-start(f32[4096]{0:T(1024)} %param.5) | copy-start | bytes 49156
  234.1 7.6 %copy-start.5 = (bf16[16,128,128]{2,1,0:T(8,128)(2,1)}, bf16[16,128,128]{2,1,0:T(8,128)(2,1)S(1)}, u32[]{:S(2)}) copy-start(bf16[16,128,128]{2,1,0:T(8,128)(2,1)S(1)} %all-to-all-done.3.refs_4_) | copy-start | bytes 1572868
  234.1 28.9 %all-to-all-start = ((bf16[16,128,128]{2,1,0:T(8,128)(2,1)}), bf16[16,128,128]{2,1,0:T(8,128)(2,1)S(1)}, u32[]{:S(2)}, u32[]{:S(2)}) async-start(bf16[16,128,128]{2,1,0:T(8,128)(2,1)} %transform_rows.4), calls=%async_computation | async-start | bytes 1048576 | tf_op jit(solution)/shard_map/all_to_all | solution.py:456
  263.0 5.7 %copy-start.4 = (bf16[16,128,128]{2,1,0:T(8,128)(2,1)}, bf16[16,128,128]{2,1,0:T(8,128)(2,1)S(1)}, u32[]{:S(2)}) copy-start(bf16[16,128,128]{2,1,0:T(8,128)(2,1)S(1)} %all-to-all-done.refs_4_) | copy-start | bytes 1572868
  263.0 32.2 %all-to-all-start.5 = ((bf16[16,128,256]{2,1,0:T(8,128)(2,1)}), bf16[16,128,256]{2,1,0:T(8,128)(2,1)S(1)}, u32[]{:S(2)}, u32[]{:S(2)}) async-start(bf16[16,128,256]{2,1,0:T(8,128)(2,1)} %filter_columns.3), calls=%async_computation.5 | async-start | bytes 2097152 | tf_op jit(solution)/shard_map/all_to_all | solution.py:481
  295.2 3.7 %copy-start = (bf16[16,128,256]{2,1,0:T(8,128)(2,1)}, bf16[16,128,256]{2,1,0:T(8,128)(2,1)S(1)}, u32[]{:S(2)}) copy-start(bf16[16,128,256]{2,1,0:T(8,128)(2,1)S(1)} %all-to-all-done.5.arrived) | copy-start | bytes 3145732
  295.2 30.1 %all-to-all-start.2 = ((bf16[16,128,256]{2,1,0:T(8,128)(2,1)}), bf16[16,128,256]{2,1,0:T(8,128)(2,1)S(1)}, u32[]{:S(2)}, u32[]{:S(2)}) async-start(bf16[16,128,256]{2,1,0:T(8,128)(2,1)} %filter_columns.2), calls=%async_computation.2 | async-start | bytes 2097152 | tf_op jit(solution)/shard_map/all_to_all | solution.py:481
  325.3 1.0 copy-start.1

commit v2 on v1

--- a/solution.py
+++ b/solution.py
@@ -182,16 +182,27 @@
     )(place, slices, slices, slices, head, tail, weights)
 
 
-def table_kernel(near, turn, far, out, *, half):
-    near_cos, near_sin = near[0, 0], near[0, 1]
-    turn_cos, turn_sin = turn[0, 0], turn[0, 1]
-    low_cos = near_cos * turn_cos - near_sin * turn_sin
-    low_sin = near_sin * turn_cos + near_cos * turn_sin
-    shape = low_cos.shape
-    for j in range(half // 128):
-        high_cos = jnp.broadcast_to(far[0, 0, :, j : j + 1], shape)
-        high_sin = jnp.broadcast_to(far[0, 1, :, j : j + 1], shape)
-        out[0, :, pl.ds(j * 128, 128)] = (high_cos * low_cos - high_sin * low_sin).astype(jnp.bfloat16)
+def table_kernel(near, turn, step, out, *, half):
+    parity, block = pl.program_id(0), pl.program_id(1)
+    group = min(64, out.shape[1])
+    norm = math.sqrt(1.0 / half)
+    for at in range(0, out.shape[1], group):
+        rows = pl.ds(at, group)
+        near_cos, near_sin = near[0, 0, rows, :], near[0, 1, rows, :]
+        low_cos = near_cos * turn[0, 0] - near_sin * turn[0, 1]
+        low_sin = near_sin * turn[0, 0] + near_cos * turn[0, 1]
+        step_cos = jnp.broadcast_to(step[0, rows, 0:1], low_cos.shape)
+        step_sin = jnp.broadcast_to(step[0, rows, 1:2], low_cos.shape)
+        row = at + lax.broadcasted_iota(jnp.int32, low_cos.shape, 0)
+        first = (row == 0) & (parity == 0) & (block == 0)
+        scale = jnp.where(first, norm * math.sqrt(0.5), norm)
+        before = scale * low_cos
+        here = scale * (step_cos * low_cos - step_sin * low_sin)
+        twice = step_cos + step_cos
+        out[0, rows, pl.ds(0, 128)] = before.astype(jnp.bfloat16)
+        for j in range(1, half // 128):
+            out[0, rows, pl.ds(j * 128, 128)] = here.astype(jnp.bfloat16)
+            before, here = here, twice * here - before
 
 
 def cosine_halves(length):
@@ -199,35 +210,31 @@
     rows = min(256, half)
     unit = jnp.float32(math.pi / (2 * length))
 
-    def pair(phase, scale):
+    def pair(phase, axis):
         angle = (phase % (4 * length)).astype(jnp.float32) * unit
-        return jnp.stack([jnp.cos(angle) * scale, jnp.sin(angle) * scale], axis=1)
+        return jnp.stack([jnp.cos(angle), jnp.sin(angle)], axis=axis)
 
     def iota(shape, dim):
         return lax.broadcasted_iota(jnp.int32, shape, dim)
 
     odd = (2, rows, 128)
-    near = pair((2 * iota(odd, 2) + 1) * (2 * iota(odd, 1) + iota(odd, 0)), 1.0)
+    near = pair((2 * iota(odd, 2) + 1) * (2 * iota(odd, 1) + iota(odd, 0)), 1)
     blocks = (half // rows, 1, 128)
-    turn = pair((2 * iota(blocks, 2) + 1) * (2 * rows * iota(blocks, 0)), 1.0)
-    steps = (2, half, half // 128)
-    frequency = 2 * iota(steps, 1) + iota(steps, 0)
-    norming = jnp.where(
-        frequency == 0, jnp.float32(math.sqrt(1.0 / length)), jnp.float32(math.sqrt(2.0 / length))
-    )
-    far = pair(256 * iota(steps, 2) * frequency, norming)
+    turn = pair((2 * iota(blocks, 2) + 1) * (2 * rows * iota(blocks, 0)), 1)
+    steps = (2, half)
+    step = pair(256 * (2 * iota(steps, 1) + iota(steps, 0)), 2)
     return pl.pallas_call(
         functools.partial(table_kernel, half=half),
         grid=(2, half // rows),
         in_specs=[
             pl.BlockSpec((1, 2, rows, 128), lambda p, b: (p, 0, 0, 0)),
             pl.BlockSpec((1, 2, 1, 128), lambda p, b: (b, 0, 0, 0)),
-            pl.BlockSpec((1, 2, rows, half // 128), lambda p, b: (p, 0, b, 0)),
+            pl.BlockSpec((1, rows, 2), lambda p, b: (p, b, 0)),
         ],
         out_specs=pl.BlockSpec((1, rows, half), lambda p, b: (p, b, 0)),
         out_shape=jax.ShapeDtypeStruct((2, half, half), jnp.bfloat16),
         name="cosines",
-    )(near, turn, far)
+    )(near, turn, step)
 
 
 def merge_kernel(own, other, mirror, out, *, cols):
@@ -268,7 +275,7 @@
 def transform_rows(table, folded, parity, devices):
     _, rows, half = folded.shape
     own = half // devices
-    tile = max(256, own)
+    tile = max(512, own)
     return pl.pallas_call(
         rows_kernel,
         grid=(half // tile,),
@@ -325,7 +332,7 @@
 def filter_columns(table, rows_response, cols_response, mirror, arrived, order):
     half = table.shape[1]
     blocks, own, _ = arrived[0].shape
-    tile = min(256, half)
+    tile = min(512, half)
     chunks = len(arrived)
     whole = pl.BlockSpec((blocks, own, lane_block // chunks), lambda p, t: (0, 0, 0))
     return pl.pallas_call(
@@ -365,7 +372,7 @@
 def restore_even(table, arrived):
     half = table.shape[1]
     devices, own, rows = arrived.shape
-    tile = min(256, half)
+    tile = min(512, half)
     return pl.pallas_call(
         functools.partial(even_kernel, half=half),
         grid=(half // tile,),
@@ -392,18 +399,21 @@
     odd = dot(turned[...], table[0])
     out[:, pl.ds(pl.multiple_of(step * tile, tile), tile)] = even[...] + odd
     left = even[...] - odd
-    back = jnp.zeros_like(left)
-    for _ in range(3):
-        piece = left.astype(jnp.bfloat16)
-        back += dot(piece, mirror[...])
-        left = left - piece.astype(jnp.float32)
-    out[:, pl.ds(pl.multiple_of(2 * half - tile - step * tile, tile), tile)] = back
+    base = pl.multiple_of(2 * half - tile - step * tile, tile)
+    for at in range(0, tile, lane_block):
+        rest = left[:, at : at + lane_block]
+        back = jnp.zeros_like(rest)
+        for _ in range(3):
+            piece = rest.astype(jnp.bfloat16)
+            back += dot(piece, mirror[...])
+            rest = rest - piece.astype(jnp.float32)
+        out[:, pl.ds(base + tile - lane_block - at, lane_block)] = back
 
 
 def restore(table, arrived, even, mirror):
     half = table.shape[1]
     devices, own, rows = arrived.shape
-    tile = lane_block
+    tile = min(512, half)
     return pl.pallas_call(
         functools.partial(odd_kernel, half=half, tile=tile),
         grid=(half // tile,),
@@ -430,10 +440,11 @@
     piece = length // devices
     above, below = edge_rows(slices, 4)
     table = cosine_halves(length)
+    weights = band()
+    mirror = exchange_matrix()
+    above, below, table = lax.optimization_barrier((above, below, table))
     head = jnp.pad(above, ((0, 0), (12, 0), (0, 0)))
     tail = jnp.pad(below, ((0, 0), (0, 12), (0, 0)))
-    weights = band()
-    mirror = exchange_matrix()
     focus = lax.axis_index("focus")
     chunks = row_chunks if piece % (16 * row_chunks) == 0 else 1
     if piece // chunks * chunks != piece or piece < lane_block:

time: 341 us -> 309 us (0.906)
  Pallas kernels: 239 us -> 206 us
    pallas_call x2, Pallas kernels: 42.7 us -> 30.2 us  [filter_columns(): pl.pallas_call(functools.partial(columns_kernel, chunks=chunks, half=half...]
    ppermute x1, waiting for transfers between devices: 9.16 us -> 0.01 us  [edge_rows(): above = lax.ppermute(tail, 'strip', [(i, i + 1) for i in range(ends)])]
    all_to_all x2, waiting for transfers between devices: 22.3 us -> 30.7 us  [body(): lax.all_to_all(back, axes, split_axis=0, concat_axis=0, tiled=True)]
    pallas_call x4, Pallas kernels: 33.3 us -> 25.2 us  [transform_rows(): pl.pallas_call(rows_kernel, grid=(half // tile,), in_specs=[pl.BlockSpec(...]
    pallas_call x1, Pallas kernels: 21.7 us -> 13.9 us  [cosine_halves(): pl.pallas_call(functools.partial(table_kernel, half=half), grid=(2, half...]
    all_to_all x4, waiting for transfers between devices: 14.9 us -> 18.9 us  [body(): moved = lax.all_to_all(along, axes, split_axis=0, concat_axis=0, tiled=True)]
  transfers between devices with their start and end apart: 10 -> 10, of which waited for: 5 -> 4; matrix products, arithmetic and copies ran while one was open for 4% -> 3% of each run, Pallas kernels for 59% -> 55%
where the time goes in v2:
time: 309 us; the launch traced here: 308 us
  Pallas kernels  206 us (67%)
  waiting for transfers between devices  49.6 us (16%)
  starting transfers between devices  36.5 us (12%)
  local copies, waits for them, and re-layouts  10.4 us (3%)
  other arithmetic  4.94 us (2%)
    pallas_call x4, Pallas kernels, stencil(): pl.pallas_call(kernel, grid_spec=grid_spec, out_shape=jax.ShapeDtypeStruc...  111 us
    all_to_all x2, waiting for transfers between devices, body(): lax.all_to_all(back, axes, split_axis=0, concat_axis=0, tiled=True)  30.7 us
    pallas_call x2, Pallas kernels, filter_columns(): pl.pallas_call(functools.partial(columns_kernel, chunks=chunks, half=half...  30.2 us
    pallas_call x4, Pallas kernels, transform_rows(): pl.pallas_call(rows_kernel, grid=(half // tile,), in_specs=[pl.BlockSpec(...  25.2 us
    all_to_all x4, starting transfers between devices, body(): moved = lax.all_to_all(along, axes, split_axis=0, concat_axis=0, tiled=True)  20.4 us
    all_to_all x4, waiting for transfers between devices, body(): moved = lax.all_to_all(along, axes, split_axis=0, concat_axis=0, tiled=True)  18.9 us
    pallas_call x1, Pallas kernels, cosine_halves(): pl.pallas_call(functools.partial(table_kernel, half=half), grid=(2, half...  13.9 us
    pallas_call x1, Pallas kernels, restore(): pl.pallas_call(functools.partial(odd_kernel, half=half, tile=tile), grid=...  9.43 us
  transfers between devices with their start and end apart: 10, of which 4 were waited for; matrix products, arithmetic and copies ran while one was open for 3% of the time, Pallas kernels for 55%

profile of v2, /device:TPU:0, one launch (start us, length us, event | category | flops | bytes accessed | tf_op | source)
XLA Modules:
  0.0 307.7 jit_solution(3849304221569554467)
XLA Ops:
  0.0 1.5 fusion.20
  1.5 4.9 %collective-permute-start = (bf16[8,4,4096]{2,1,0:T(4,128)(2,1)S(1)}, bf16[8,4,4096]{2,1,0:T(4,128)(2,1)S(1)}, u32[]{:S(2)}, u32[]{:S(2)}) collective-permute-start(bf16[8,4,4096]{2,1,0:T(4,128)(2,1)S(1)} %get-tuple-element.12), channel_id=1, source_target_pairs={{0,1},{1,2},{2,3},{3,4},{4,5},{5,6},{6,7},{8,9},{9,10},{10,11},{11... | collective-permute-start | bytes 786440 | tf_op jit(solution)/shard_map/ppermute | solution.py:30
  6.4 1.3 collective-permute-start.1
  7.7 1.1 fusion.6
  11.1 2.0 copy.8.step
  13.1 13.9 %cosines.1.table.refs_0_ = bf16[2,2048,2048]{2,1,0:T(8,128)(2,1)} custom-call(f32[2,2,256,128]{3,2,1,0:T(8,128)} %pad_maximum_fusion.near, f32[8,2,1,128]{3,2,1,0:T(1,128)} %pad_maximum_fusion.2.turn, f32[2,2048,2]{2,1,0:T(8,128)} %copy.8.step), custom_call_target="tpu_custom_call" | custom-call | tf_op jit(solution)/shard_map/cosines/pallas_call | solution.py:226
  27.9 1.2 pad.8.head
  29.1 1.1 pad.9.tail
  30.1 27.7 %stencil.7 = f32[2,128,4096]{2,1,0:T(8,128)} custom-call(s32[1]{0:T(128)} %bitcast.5.place, bf16[8,512,4096]{2,1,0:T(8,128)(2,1)} %below.7, bf16[8,512,4096]{2,1,0:T(8,128)(2,1)} %below.7, bf16[8,512,4096]{2,1,0:T(8,128)(2,1)} %below.7, bf16[8,16,4096]{2,1,0:T(8,128)(2,1)} %pad.8.head, bf16[8,16,4096]{2,1,0:T(8,128)(2,1)} %pad.9.tail, ...), custom_call_target="tpu_custom_call" | custom-call | flops 8589934592 | bytes 12582912 | tf_op jit(solution)/shard_map/stencil/pallas_call | solution.py:175
  57.8 27.7 %stencil.5 = f32[2,128,4096]{2,1,0:T(8,128)} custom-call(s32[1]{0:T(128)} %bitcast.3.place, bf16[8,512,4096]{2,1,0:T(8,128)(2,1)} %below.7, bf16[8,512,4096]{2,1,0:T(8,128)(2,1)} %below.7, bf16[8,512,4096]{2,1,0:T(8,128)(2,1)} %below.7, bf16[8,16,4096]{2,1,0:T(8,128)(2,1)} %pad.8.head, bf16[8,16,4096]{2,1,0:T(8,128)(2,1)} %pad.9.tail, ...), custom_call_target="tpu_custom_call" | custom-call | flops 8589934592 | bytes 12582912 | tf_op jit(solution)/shard_map/stencil/pallas_call | solution.py:175
  86.6 27.9 %stencil.6.own = f32[2,128,4096]{2,1,0:T(8,128)} custom-call(s32[1]{0:T(128)} %bitcast.4.place, bf16[8,512,4096]{2,1,0:T(8,128)(2,1)} %below.7, bf16[8,512,4096]{2,1,0:T(8,128)(2,1)} %below.7, bf16[8,512,4096]{2,1,0:T(8,128)(2,1)} %below.7, bf16[8,16,4096]{2,1,0:T(8,128)(2,1)} %pad.8.head, bf16[8,16,4096]{2,1,0:T(8,128)(2,1)} %pad.9.tail, ...), custom_call_target="tpu_custom_call" | custom-call | flops 8589934592 | bytes 12582912 | tf_op jit(solution)/shard_map/stencil/pallas_call | solution.py:175
  114.5 4.7 %merge.3.folded = bf16[2,128,2048]{2,1,0:T(8,128)(2,1)} custom-call(f32[2,128,4096]{2,1,0:T(8,128)} %stencil.6.own, f32[2,128,4096]{2,1,0:T(8,128)} %collective-permute-done.3.other, bf16[256,256]{1,0:T(8,128)(2,1)} %fusion.4.mirror.refs_3_), custom_call_target="tpu_custom_call" | custom-call | tf_op jit(solution)/shard_map/merge/pallas_call | solution.py:256
  119.2 6.3 %transform_rows.7 = bf16[16,128,128]{2,1,0:T(8,128)(2,1)} custom-call(bf16[2,2048,2048]{2,1,0:T(8,128)(2,1)} %cosines.1.table.refs_0_, bf16[2,128,2048]{2,1,0:T(8,128)(2,1)} %merge.3.folded), custom_call_target="tpu_custom_call" | custom-call | tf_op jit(solution)/shard_map/transform_rows/pallas_call | solution.py:279
  125.5 7.1 %all-to-all-start.4 = ((bf16[16,128,128]{2,1,0:T(8,128)(2,1)}), bf16[16,128,128]{2,1,0:T(8,128)(2,1)S(1)}, u32[]{:S(2)}, u32[]{:S(2)}) async-start(bf16[16,128,128]{2,1,0:T(8,128)(2,1)} %transform_rows.7), calls=%async_computation.4 | async-start | bytes 1048576 | tf_op jit(solution)/shard_map/all_to_all | solution.py:467
  132.6 27.7 %stencil.4.own = f32[2,128,4096]{2,1,0:T(8,128)} custom-call(s32[1]{0:T(128)} %bitcast.2.place, bf16[8,512,4096]{2,1,0:T(8,128)(2,1)} %below.7, bf16[8,512,4096]{2,1,0:T(8,128)(2,1)} %below.7, bf16[8,512,4096]{2,1,0:T(8,128)(2,1)} %below.7, bf16[8,16,4096]{2,1,0:T(8,128)(2,1)} %pad.8.head, bf16[8,16,4096]{2,1,0:T(8,128)(2,1)} %pad.9.tail, ...), custom_call_target="tpu_custom_call" | custom-call | flops 8589934592 | bytes 12582912 | tf_op jit(solution)/shard_map/stencil/pallas_call | solution.py:175
  160.3 4.7 %merge.2.folded = bf16[2,128,2048]{2,1,0:T(8,128)(2,1)} custom-call(f32[2,128,4096]{2,1,0:T(8,128)} %stencil.4.own, f32[2,128,4096]{2,1,0:T(8,128)} %collective-permute-done.2.other, bf16[256,256]{1,0:T(8,128)(2,1)} %fusion.4.mirror.refs_3_), custom_call_target="tpu_custom_call" | custom-call | tf_op jit(solution)/shard_map/merge/pallas_call | solution.py:256
  165.0 6.3 %transform_rows.6 = bf16[16,128,128]{2,1,0:T(8,128)(2,1)} custom-call(bf16[2,2048,2048]{2,1,0:T(8,128)(2,1)} %cosines.1.table.refs_0_, bf16[2,128,2048]{2,1,0:T(8,128)(2,1)} %merge.2.folded), custom_call_target="tpu_custom_call" | custom-call | tf_op jit(solution)/shard_map/transform_rows/pallas_call | solution.py:279
  171.3 6.0 %all-to-all-start.3 = ((bf16[16,128,128]{2,1,0:T(8,128)(2,1)}), bf16[16,128,128]{2,1,0:T(8,128)(2,1)S(1)}, u32[]{:S(2)}, u32[]{:S(2)}) async-start(bf16[16,128,128]{2,1,0:T(8,128)(2,1)} %transform_rows.6), calls=%async_computation.3 | async-start | bytes 1048576 | tf_op jit(solution)/shard_map/all_to_all | solution.py:467
  177.3 6.3 %transform_rows.5 = bf16[16,128,128]{2,1,0:T(8,128)(2,1)} custom-call(bf16[2,2048,2048]{2,1,0:T(8,128)(2,1)} %cosines.1.table.refs_0_, bf16[2,128,2048]{2,1,0:T(8,128)(2,1)} %merge.3.folded), custom_call_target="tpu_custom_call" | custom-call | tf_op jit(solution)/shard_map/transform_rows/pallas_call | solution.py:279
  183.6 9.5 %all-to-all-done.3.refs_4_ = bf16[16,128,128]{2,1,0:T(8,128)(2,1)S(1)} async-done(((bf16[16,128,128]{2,1,0:T(8,128)(2,1)}), bf16[16,128,128]{2,1,0:T(8,128)(2,1)S(1)}, u32[]{:S(2)}, u32[]{:S(2)}) %all-to-all-start.3) | async-done | bytes 524320 | tf_op jit(solution)/shard_map/all_to_all | solution.py:467
  193.0 3.6 %all-to-all-start.1 = ((bf16[16,128,128]{2,1,0:T(8,128)(2,1)}), bf16[16,128,128]{2,1,0:T(8,128)(2,1)S(1)}, u32[]{:S(2)}, u32[]{:S(2)}) async-start(bf16[16,128,128]{2,1,0:T(8,128)(2,1)} %transform_rows.5), calls=%async_computation.1 | async-start | bytes 1048576 | tf_op jit(solution)/shard_map/all_to_all | solution.py:467
  196.6 6.3 %transform_rows.4 = bf16[16,128,128]{2,1,0:T(8,128)(2,1)} custom-call(bf16[2,2048,2048]{2,1,0:T(8,128)(2,1)} %cosines.1.table.refs_0_, bf16[2,128,2048]{2,1,0:T(8,128)(2,1)} %merge.2.folded), custom_call_target="tpu_custom_call" | custom-call | tf_op jit(solution)/shard_map/transform_rows/pallas_call | solution.py:279
  203.0 9.4 %all-to-all-done.1.refs_5_ = bf16[16,128,128]{2,1,0:T(8,128)(2,1)S(1)} async-done(((bf16[16,128,128]{2,1,0:T(8,128)(2,1)}), bf16[16,128,128]{2,1,0:T(8,128)(2,1)S(1)}, u32[]{:S(2)}, u32[]{:S(2)}) %all-to-all-start.1) | async-done | bytes 524320 | tf_op jit(solution)/shard_map/all_to_all | solution.py:467
  212.4 3.8 %all-to-all-start = ((bf16[16,128,128]{2,1,0:T(8,128)(2,1)}), bf16[16,128,128]{2,1,0:T(8,128)(2,1)S(1)}, u32[]{:S(2)}, u32[]{:S(2)}) async-start(bf16[16,128,128]{2,1,0:T(8,128)(2,1)} %transform_rows.4), calls=%async_computation | async-start | bytes 1048576 | tf_op jit(solution)/shard_map/all_to_all | solution.py:467
  219.9 15.1 %filter_columns.3 = bf16[16,128,256]{2,1,0:T(8,128)(2,1)} custom-call(bf16[2,2048,2048]{2,1,0:T(8,128)(2,1)} %cosines.1.table.refs_0_, f32[2,1,2048]{2,1,0:T(1,128)} %reshape.282.refs_1_, f32[128,1]{1,0:T(8,128)} %get-tuple-element.13.refs_2_, bf16[256,256]{1,0:T(8,128)(2,1)} %fusion.4.mirror.refs_3_, bf16[16,128,128]{2,1,0:T(8,128)(2,1)} %copy-done.4, ...), custom_call_target="tpu_custom_call" | custom-call | tf_op jit(solution)/shard_map/filter_columns/pallas_call | solution.py:338
  235.0 5.7 %all-to-all-start.5 = ((bf16[16,128,256]{2,1,0:T(8,128)(2,1)}), bf16[16,128,256]{2,1,0:T(8,128)(2,1)S(1)}, u32[]{:S(2)}, u32[]{:S(2)}) async-start(bf16[16,128,256]{2,1,0:T(8,128)(2,1)} %filter_columns.3), calls=%async_computation.5 | async-start | bytes 2097152 | tf_op jit(solution)/shard_map/all_to_all | solution.py:492
  240.7 15.1 %filter_columns.2 = bf16[16,128,256]{2,1,0:T(8,128)(2,1)} custom-call(bf16[2,2048,2048]{2,1,0:T(8,128)(2,1)} %cosines.1.table.refs_0_, f32[2,1,2048]{2,1,0:T(1,128)} %reshape.282.refs_1_, f32[128,1]{1,0:T(8,128)} %get-tuple-element.14.refs_2_, bf16[256,256]{1,0:T(8,128)(2,1)} %fusion.4.mirror.refs_3_, bf16[16,128,128]{2,1,0:T(8,128)(2,1)} %copy-done.5, ...), custom_call_target="tpu_custom_call" | custom-call | tf_op jit(solution)/shard_map/filter_columns/pallas_call | solution.py:338
  255.8 11.4 %all-to-all-done.5.arrived = bf16[16,128,256]{2,1,0:T(8,128)(2,1)S(1)} async-done(((bf16[16,128,256]{2,1,0:T(8,128)(2,1)}), bf16[16,128,256]{2,1,0:T(8,128)(2,1)S(1)}, u32[]{:S(2)}, u32[]{:S(2)}) %all-to-all-start.5) | async-done | bytes 1048608 | tf_op jit(solution)/shard_map/all_to_all | solution.py:492
  267.2 3.7 %all-to-all-start.2 = ((bf16[16,128,256]{2,1,0:T(8,128)(2,1)}), bf16[16,128,256]{2,1,0:T(8,128)(2,1)S(1)}, u32[]{:S(2)}, u32[]{:S(2)}) async-start(bf16[16,128,256]{2,1,0:T(8,128)(2,1)} %filter_columns.2), calls=%async_computation.2 | async-start | bytes 2097152 | tf_op jit(solution)/shard_map/all_to_all | solution.py:492
  270.9 7.2 %restore_even.1.even = f32[256,2048]{1,0:T(8,128)} custom-call(bf16[2,2048,2048]{2,1,0:T(8,128)(2,1)} %cosines.1.table.refs_0_, bf16[16,128,256]{2,1,0:T(8,128)(2,1)} %copy-done), custom_call_target="tpu_custom_call" | custom-call | tf_op jit(solution)/shard_map/restore_even/pallas_call | solution.py:376
  278.1 19.2 %all-to-all-done.2.arrived = bf16[16,128,256]{2,1,0:T(8,128)(2,1)S(1)} async-done(((bf16[16,128,256]{2,1,0:T(8,128)(2,1)}), bf16[16,128,256]{2,1,0:T(8,128)(2,1)S(1)}, u32[]{:S(2)}, u32[]{:S(2)}) %all-to-all-start.2) | async-done | bytes 1048608 | tf_op jit(solution)/shard_map/all_to_all | solution.py:492
  298.3 9.4 %restore.1 = f32[256,4096]{1,0:T(8,128)} custom-call(bf16[2,2048,2048]{2,1,0:T(8,128)(2,1)} %cosines.1.table.refs_0_, bf16[16,128,256]{2,1,0:T(8,128)(2,1)} %copy-done.1, f32[256,2048]{1,0:T(8,128)} %restore_even.1.even, bf16[256,256]{1,0:T(8,128)(2,1)} %fusion.4.mirror.refs_3_), custom_call_target="tpu_custom_call" | custom-call | tf_op jit(solution)/shard_map/restore/pallas_call | solution.py:417
  (44 shorter events, 9.1 us)
Async XLA Ops:
  1.5 26.4 %collective-permute-start = (bf16[8,4,4096]{2,1,0:T(4,128)(2,1)S(1)}, bf16[8,4,4096]{2,1,0:T(4,128)(2,1)S(1)}, u32[]{:S(2)}, u32[]{:S(2)}) collective-permute-start(bf16[8,4,4096]{2,1,0:T(4,128)(2,1)S(1)} %get-tuple-element.12), channel_id=1, source_target_pairs={{0,1},{1,2},{2,3},{3,4},{4,5},{5,6},{6,7},{8,9},{9,10},{10,11},{11... | collective-permute-start | bytes 786440 | tf_op jit(solution)/shard_map/ppermute | solution.py:30
  6.4 21.5 %collective-permute-start.1 = (bf16[8,4,4096]{2,1,0:T(4,128)(2,1)S(1)}, bf16[8,4,4096]{2,1,0:T(4,128)(2,1)S(1)}, u32[]{:S(2)}, u32[]{:S(2)}) collective-permute-start(bf16[8,4,4096]{2,1,0:T(4,128)(2,1)S(1)} %get-tuple-element.11), channel_id=1, source_target_pairs={{1,0},{2,1},{3,2},{4,3},{5,4},{6,5},{7,6},{9,8},{10,9},{11,10},{12... | collective-permute-start | bytes 786440 | tf_op jit(solution)/shard_map/ppermute | solution.py:31
  57.8 56.7 %collective-permute-start.3 = (f32[2,128,4096]{2,1,0:T(8,128)}, f32[2,128,4096]{2,1,0:T(8,128)}, u32[]{:S(2)}, u32[]{:S(2)}) collective-permute-start(f32[2,128,4096]{2,1,0:T(8,128)} %stencil.7), channel_id=1, source_target_pairs={{0,8},{8,0},{1,9},{9,1},{2,10},{10,2},{3,11},{11,3},{4,12},{12,4},... | collective-permute-start | bytes 12582920 | tf_op jit(solution)/shard_map/ppermute | solution.py:462
  85.5 74.8 %collective-permute-start.2 = (f32[2,128,4096]{2,1,0:T(8,128)}, f32[2,128,4096]{2,1,0:T(8,128)}, u32[]{:S(2)}, u32[]{:S(2)}) collective-permute-start(f32[2,128,4096]{2,1,0:T(8,128)} %stencil.5), channel_id=1, source_target_pairs={{0,8},{8,0},{1,9},{9,1},{2,10},{10,2},{3,11},{11,3},{4,12},{12,4},... | collective-permute-start | bytes 12582920 | tf_op jit(solution)/shard_map/ppermute | solution.py:462
  125.5 45.8 %all-to-all-start.4 = ((bf16[16,128,128]{2,1,0:T(8,128)(2,1)}), bf16[16,128,128]{2,1,0:T(8,128)(2,1)S(1)}, u32[]{:S(2)}, u32[]{:S(2)}) async-start(bf16[16,128,128]{2,1,0:T(8,128)(2,1)} %transform_rows.7), calls=%async_computation.4 | async-start | bytes 1048576 | tf_op jit(solution)/shard_map/all_to_all | solution.py:467
  171.3 12.3 %copy-start.2 = (bf16[16,128,128]{2,1,0:T(8,128)(2,1)}, bf16[16,128,128]{2,1,0:T(8,128)(2,1)S(1)}, u32[]{:S(2)}) copy-start(bf16[16,128,128]{2,1,0:T(8,128)(2,1)S(1)} %all-to-all-done.4.refs_5_) | copy-start | bytes 1572868
  171.3 21.8 %all-to-all-start.3 = ((bf16[16,128,128]{2,1,0:T(8,128)(2,1)}), bf16[16,128,128]{2,1,0:T(8,128)(2,1)S(1)}, u32[]{:S(2)}, u32[]{:S(2)}) async-start(bf16[16,128,128]{2,1,0:T(8,128)(2,1)} %transform_rows.6), calls=%async_computation.3 | async-start | bytes 1048576 | tf_op jit(solution)/shard_map/all_to_all | solution.py:467
  193.0 9.9 %copy-start.4 = (bf16[16,128,128]{2,1,0:T(8,128)(2,1)}, bf16[16,128,128]{2,1,0:T(8,128)(2,1)S(1)}, u32[]{:S(2)}) copy-start(bf16[16,128,128]{2,1,0:T(8,128)(2,1)S(1)} %all-to-all-done.3.refs_4_) | copy-start | bytes 1572868
  193.0 19.3 %all-to-all-start.1 = ((bf16[16,128,128]{2,1,0:T(8,128)(2,1)}), bf16[16,128,128]{2,1,0:T(8,128)(2,1)S(1)}, u32[]{:S(2)}, u32[]{:S(2)}) async-start(bf16[16,128,128]{2,1,0:T(8,128)(2,1)} %transform_rows.5), calls=%async_computation.1 | async-start | bytes 1048576 | tf_op jit(solution)/shard_map/all_to_all | solution.py:467
  196.6 19.6 %copy-start.6 = (f32[4096]{0:T(1024)S(1)}, f32[4096]{0:T(1024)}, u32[]{:S(2)}) copy-start(f32[4096]{0:T(1024)} %param.5) | copy-start | bytes 49156
  196.6 20.6 %copy-start.7 = (f32[4096]{0:T(1024)S(1)}, f32[4096]{0:T(1024)}, u32[]{:S(2)}) copy-start(f32[4096]{0:T(1024)} %param.4) | copy-start | bytes 49156
  212.4 22.6 %copy-start.3 = (bf16[16,128,128]{2,1,0:T(8,128)(2,1)}, bf16[16,128,128]{2,1,0:T(8,128)(2,1)S(1)}, u32[]{:S(2)}) copy-start(bf16[16,128,128]{2,1,0:T(8,128)(2,1)S(1)} %all-to-all-done.1.refs_5_) | copy-start | bytes 1572868
  212.4 22.6 %all-to-all-start = ((bf16[16,128,128]{2,1,0:T(8,128)(2,1)}), bf16[16,128,128]{2,1,0:T(8,128)(2,1)S(1)}, u32[]{:S(2)}, u32[]{:S(2)}) async-start(bf16[16,128,128]{2,1,0:T(8,128)(2,1)} %transform_rows.4), calls=%async_computation | async-start | bytes 1048576 | tf_op jit(solution)/shard_map/all_to_all | solution.py:467
  235.0 5.7 %copy-start.5 = (bf16[16,128,128]{2,1,0:T(8,128)(2,1)}, bf16[16,128,128]{2,1,0:T(8,128)(2,1)S(1)}, u32[]{:S(2)}) copy-start(bf16[16,128,128]{2,1,0:T(8,128)(2,1)S(1)} %all-to-all-done.refs_4_) | copy-start | bytes 1572868
  235.0 32.2 %all-to-all-start.5 = ((bf16[16,128,256]{2,1,0:T(8,128)(2,1)}), bf16[16,128,256]{2,1,0:T(8,128)(2,1)S(1)}, u32[]{:S(2)}, u32[]{:S(2)}) async-start(bf16[16,128,256]{2,1,0:T(8,128)(2,1)} %filter_columns.3), calls=%async_computation.5 | async-start | bytes 2097152 | tf_op jit(solution)/shard_map/all_to_all | solution.py:492
  267.2 3.7 %copy-start = (bf16[16,128,256]{2,1,0:T(8,128)(2,1)}, bf16[16,128,256]{2,1,0:T(8,128)(2,1)S(1)}, u32[]{:S(2)}) copy-start(bf16[16,128,256]{2,1,0:T(8,128)(2,1)S(1)} %all-to-all-done.5.arrived) | copy-start | bytes 3145732
  267.2 30.1 %all-to-all-start.2 = ((bf16[16,128,256]{2,1,0:T(8,128)(2,1)}), bf16[16,128,256]{2,1,0:T(8,128)(2,1)S(1)}, u32[]{:S(2)}, u32[]{:S(2)}) async-start(bf16[16,128,256]{2,1,0:T(8,128)(2,1)} %filter_columns.2), calls=%async_computation.2 | async-start | bytes 2097152 | tf_op jit(solution)/shard_map/all_to_all | solution.py:492
  297.3 1.0 copy-start.1

commit v3 on v2

--- a/solution.py
+++ b/solution.py
@@ -7,6 +7,7 @@
 from jax.experimental import pallas as pl
 from jax.experimental.pallas import tpu as pltpu
 from jax.sharding import PartitionSpec as P
+
 
 floor_weight = 0.01
 noise_ratio = 0.01
@@ -49,7 +50,7 @@
 
 
 def stencil_kernel(
-    place, main, above, below, head, tail, weights, out,
+    place, main, above, below, ends, weights, out,
     edges, copies_a, copies_b, laps_a, laps_b, held,
     *, tile_rows, count, cols, tiles, step, parts,
 ):
@@ -59,8 +60,8 @@
     edge_row = lax.broadcasted_iota(jnp.int32, (16, cols), 0)
     lane = lax.broadcasted_iota(jnp.int32, (step, 128), 1)
     for s in range(count):
-        upper = jnp.where(first, head[s], above[s])
-        lower = jnp.where(last, tail[s], below[s])
+        upper = jnp.where(first, ends[s], above[s])
+        lower = jnp.where(last, ends[s], below[s])
         edges[s] = jnp.where(edge_row < 8, lower, upper)
     frames = cols // 128 + 1
     copies = (copies_a, copies_b)
@@ -139,7 +140,7 @@
     gather(0, frames - 1, 0, tile_rows)
 
 
-def stencil(place, slices, head, tail, weights, out_rows):
+def stencil(place, slices, ends, weights, out_rows):
     count, rows, cols = slices.shape
     tile_rows = math.gcd(128, out_rows)
     per = tile_rows // 16
@@ -158,7 +159,6 @@
             pl.BlockSpec(edge, lambda t, at: (0, jnp.maximum((at[0] + t) * per - 1, 0), 0)),
             pl.BlockSpec(edge, lambda t, at: (0, jnp.minimum((at[0] + t) * per + per, blocks - 1), 0)),
             pl.BlockSpec(edge, lambda t, at: (0, 0, 0)),
-            pl.BlockSpec(edge, lambda t, at: (0, 0, 0)),
             pl.BlockSpec((256, 512), lambda t, at: (0, 0)),
         ],
         out_specs=pl.BlockSpec((2, tile_rows, cols), lambda t, at: (0, t, 0)),
@@ -179,20 +179,18 @@
         cost_estimate=pl.CostEstimate(flops=pixels * 2048, bytes_accessed=pixels * 3, transcendentals=0),
         compiler_params=pltpu.CompilerParams(vmem_limit_bytes=60 << 20),
         name="stencil",
-    )(place, slices, slices, slices, head, tail, weights)
-
-
-def table_kernel(near, turn, step, out, *, half):
+    )(place, slices, slices, slices, ends, weights)
+
+
+def table_kernel(near, turn, out, *, half):
     parity, block = pl.program_id(0), pl.program_id(1)
     group = min(64, out.shape[1])
     norm = math.sqrt(1.0 / half)
     for at in range(0, out.shape[1], group):
         rows = pl.ds(at, group)
-        near_cos, near_sin = near[0, 0, rows, :], near[0, 1, rows, :]
+        near_cos, near_sin, step_cos, step_sin = (near[0, k, rows, :] for k in range(4))
         low_cos = near_cos * turn[0, 0] - near_sin * turn[0, 1]
         low_sin = near_sin * turn[0, 0] + near_cos * turn[0, 1]
-        step_cos = jnp.broadcast_to(step[0, rows, 0:1], low_cos.shape)
-        step_sin = jnp.broadcast_to(step[0, rows, 1:2], low_cos.shape)
         row = at + lax.broadcasted_iota(jnp.int32, low_cos.shape, 0)
         first = (row == 0) & (parity == 0) & (block == 0)
         scale = jnp.where(first, norm * math.sqrt(0.5), norm)
@@ -208,33 +206,32 @@
 def cosine_halves(length):
     half = length // 2
     rows = min(256, half)
+    assert 512 * rows % (4 * length) == 0
     unit = jnp.float32(math.pi / (2 * length))
 
-    def pair(phase, axis):
+    def pair(phase):
         angle = (phase % (4 * length)).astype(jnp.float32) * unit
-        return jnp.stack([jnp.cos(angle), jnp.sin(angle)], axis=axis)
+        return [jnp.cos(angle), jnp.sin(angle)]
 
     def iota(shape, dim):
         return lax.broadcasted_iota(jnp.int32, shape, dim)
 
     odd = (2, rows, 128)
-    near = pair((2 * iota(odd, 2) + 1) * (2 * iota(odd, 1) + iota(odd, 0)), 1)
+    frequency = 2 * iota(odd, 1) + iota(odd, 0)
+    near = jnp.stack(pair((2 * iota(odd, 2) + 1) * frequency) + pair(256 * frequency), axis=1)
     blocks = (half // rows, 1, 128)
-    turn = pair((2 * iota(blocks, 2) + 1) * (2 * rows * iota(blocks, 0)), 1)
-    steps = (2, half)
-    step = pair(256 * (2 * iota(steps, 1) + iota(steps, 0)), 2)
+    turn = jnp.stack(pair((2 * iota(blocks, 2) + 1) * (2 * rows * iota(blocks, 0))), axis=1)
     return pl.pallas_call(
         functools.partial(table_kernel, half=half),
         grid=(2, half // rows),
         in_specs=[
-            pl.BlockSpec((1, 2, rows, 128), lambda p, b: (p, 0, 0, 0)),
+            pl.BlockSpec((1, 4, rows, 128), lambda p, b: (p, 0, 0, 0)),
             pl.BlockSpec((1, 2, 1, 128), lambda p, b: (b, 0, 0, 0)),
-            pl.BlockSpec((1, rows, 2), lambda p, b: (p, b, 0)),
         ],
         out_specs=pl.BlockSpec((1, rows, half), lambda p, b: (p, b, 0)),
         out_shape=jax.ShapeDtypeStruct((2, half, half), jnp.bfloat16),
         name="cosines",
-    )(near, turn, step)
+    )(near, turn)
 
 
 def merge_kernel(own, other, mirror, out, *, cols):
@@ -250,15 +247,16 @@
         out[1, :, pl.ds(at, lane_block)] = (near - far).astype(jnp.bfloat16)
 
 
-def merge(own, other, mirror):
+def merge(own, other, mirror, at):
     _, rows, cols = own.shape
     tile = min(64, rows)
+    first = at // tile
     return pl.pallas_call(
         functools.partial(merge_kernel, cols=cols),
         grid=(rows // tile,),
         in_specs=[
             pl.BlockSpec((2, tile, cols), lambda t: (0, t, 0)),
-            pl.BlockSpec((2, tile, cols), lambda t: (0, t, 0)),
+            pl.BlockSpec((2, tile, cols), lambda t: (0, first + t, 0)),
             pl.BlockSpec((lane_block, lane_block), lambda t: (0, 0)),
         ],
         out_specs=pl.BlockSpec((2, tile, cols // 2), lambda t: (0, t, 0)),
@@ -272,19 +270,20 @@
     out[...] = values.reshape(out.shape)
 
 
-def transform_rows(table, folded, parity, devices):
+def transform_rows(table, folded, parities, devices):
     _, rows, half = folded.shape
     own = half // devices
     tile = max(512, own)
+    first = parities[0]
     return pl.pallas_call(
         rows_kernel,
-        grid=(half // tile,),
-        in_specs=[
-            pl.BlockSpec((1, tile, half), lambda t: (parity, t, 0)),
-            pl.BlockSpec((1, rows, half), lambda t: (parity, 0, 0)),
-        ],
-        out_specs=pl.BlockSpec((tile // own, own, rows), lambda t: (t, 0, 0)),
-        out_shape=jax.ShapeDtypeStruct((devices, own, rows), jnp.bfloat16),
+        grid=(len(parities), half // tile),
+        in_specs=[
+            pl.BlockSpec((1, tile, half), lambda p, t: (first + p, t, 0)),
+            pl.BlockSpec((1, rows, half), lambda p, t: (first + p, 0, 0)),
+        ],
+        out_specs=pl.BlockSpec((tile // own, 1, own, rows), lambda p, t: (t, p, 0, 0)),
+        out_shape=jax.ShapeDtypeStruct((devices, len(parities), own, rows), jnp.bfloat16),
         name="transform_rows",
     )(table, folded)
 
@@ -300,9 +299,9 @@
     @pl.when((parity == 0) & (step == 0))
     def _():
         for j in range(blocks):
-            near = jnp.concatenate([part[order[j]] for part in arrived], axis=1).astype(jnp.float32)
+            near = jnp.concatenate([part[order[j], 0] for part in arrived], axis=1).astype(jnp.float32)
             far = dot(
-                jnp.concatenate([part[order[2 * blocks - 1 - j]] for part in arrived], axis=1), mirror[...]
+                jnp.concatenate([part[order[2 * blocks - 1 - j], 0] for part in arrived], axis=1), mirror[...]
             )
             folded[0, :, pl.ds(j * lane_block, lane_block)] = (near + far).astype(jnp.bfloat16)
             folded[1, :, pl.ds(j * lane_block, lane_block)] = (near - far).astype(jnp.bfloat16)
@@ -331,10 +330,13 @@
 
 def filter_columns(table, rows_response, cols_response, mirror, arrived, order):
     half = table.shape[1]
-    blocks, own, _ = arrived[0].shape
+    blocks, _, own, _ = arrived[0][0].shape
     tile = min(512, half)
     chunks = len(arrived)
-    whole = pl.BlockSpec((blocks, own, lane_block // chunks), lambda p, t: (0, 0, 0))
+
+    def whole(part, parity):
+        return pl.BlockSpec((blocks, 1, own, part.shape[3]), lambda p, t: (0, parity, 0, 0))
+
     return pl.pallas_call(
         functools.partial(columns_kernel, chunks=chunks, half=half, order=order),
         grid=(2, half // tile),
@@ -344,7 +346,7 @@
             pl.BlockSpec((own, 1), lambda p, t: (0, 0)),
             pl.BlockSpec((lane_block, lane_block), lambda p, t: (0, 0)),
         ]
-        + [whole] * chunks,
+        + [whole(*pair) for pair in arrived],
         out_specs=pl.BlockSpec((blocks, own, lane_block), lambda p, t: (0, 0, 0)),
         out_shape=jax.ShapeDtypeStruct((blocks, own, lane_block), jnp.bfloat16),
         scratch_shapes=[
@@ -353,7 +355,7 @@
         ],
         compiler_params=pltpu.CompilerParams(vmem_limit_bytes=60 << 20),
         name="filter_columns",
-    )(table, rows_response, cols_response, mirror, *arrived)
+    )(table, rows_response, cols_response, mirror, *(part for part, _ in arrived))
 
 
 def turn(values):
@@ -431,47 +433,56 @@
     )(table, arrived, even, mirror)
 
 
-def body(slices, otf_rows, otf_cols):
+def program(slices, otf_rows, otf_cols):
     axes = ("focus", "strip")
     focus_count = lax.axis_size("focus")
     devices = focus_count * lax.axis_size("strip")
-    rows, length = slices.shape[1:]
+    _, length = slices.shape[1:]
     half = length // 2
     piece = length // devices
+    blocks = length // lane_block
+    per = lane_block // piece
     above, below = edge_rows(slices, 4)
     table = cosine_halves(length)
     weights = band()
     mirror = exchange_matrix()
-    above, below, table = lax.optimization_barrier((above, below, table))
-    head = jnp.pad(above, ((0, 0), (12, 0), (0, 0)))
-    tail = jnp.pad(below, ((0, 0), (0, 12), (0, 0)))
     focus = lax.axis_index("focus")
-    chunks = row_chunks if piece % (16 * row_chunks) == 0 else 1
-    if piece // chunks * chunks != piece or piece < lane_block:
-        chunks = 1
-    chunk_rows = piece // chunks
-    tile_rows = math.gcd(128, chunk_rows)
-    swap = [(i, focus_count - 1 - i) for i in range(focus_count)]
-    arrived = ([], [])
-    for chunk in range(chunks):
-        def sums(half_index):
-            place = (half_index * piece + chunk * chunk_rows) // tile_rows
-            return stencil(place.astype(jnp.int32).reshape(1), slices, head, tail, weights, chunk_rows)
-
-        sent = sums(focus_count - 1 - focus)
-        received = lax.ppermute(sent, "focus", swap)
-        own = sums(focus)
-        folded = merge(own, received, mirror)
-        for parity in range(2):
-            along = transform_rows(table, folded, parity, devices)
-            moved = lax.all_to_all(along, axes, split_axis=0, concat_axis=0, tiled=True)
-            arrived[parity].append(moved)
-    blocks = length // lane_block
-    per = lane_block // piece
     owner = focus * lax.axis_size("strip") + lax.axis_index("strip")
     own = half // devices
     rows_response = otf_rows.reshape(half, 2).T.reshape(2, 1, half)
-    local_cols = lax.dynamic_slice_in_dim(otf_cols.reshape(half, 2), owner * own, own, 0)
+    local_cols = lax.dynamic_slice_in_dim(otf_cols, owner * 2 * own, 2 * own, 0).reshape(own, 2).T.reshape(2, own, 1)
+    above, below, table, rows_response, local_cols, mirror, weights = lax.optimization_barrier(
+        (above, below, table, rows_response, local_cols, mirror, weights)
+    )
+    ends = jnp.pad(above, ((0, 0), (12, 0), (0, 0))) + jnp.pad(below, ((0, 0), (0, 12), (0, 0)))
+    chunks = row_chunks if per == 1 and piece % (16 * row_chunks) == 0 else 1
+    chunk_rows = piece // chunks
+    swap = [(i, focus_count - 1 - i) for i in range(focus_count)]
+
+    def sums(ends, half_index, chunk, rows):
+        place = (half_index * piece + chunk * chunk_rows) // math.gcd(128, rows)
+        return stencil(place.astype(jnp.int32).reshape(1), slices, ends, weights, rows)
+
+    last = []
+
+    def exchange(values):
+        if last:
+            values, _ = lax.optimization_barrier((values, last[-1]))
+        last.append(lax.all_to_all(values, axes, split_axis=0, concat_axis=0, tiled=True))
+        return last[-1]
+
+    received = lax.ppermute(sums(ends, focus_count - 1 - focus, 0, piece), "focus", swap)
+    arrived = ([], [])
+    for chunk in range(chunks):
+        own_sums = sums(ends, focus, chunk, chunk_rows)
+        folded = merge(own_sums, received, mirror, chunk * chunk_rows)
+        for parities in ((0,), (1,)) if chunk == chunks - 1 else ((0, 1),):
+            along = transform_rows(table, folded, parities, devices)
+            if chunk < chunks - 1:
+                ends, along = lax.optimization_barrier((ends, along))
+            moved = exchange(along)
+            for at, parity in enumerate(parities):
+                arrived[parity].append((moved, at))
     strips = devices // focus_count
     order = [b % focus_count * strips + b // focus_count if per == 1 else b for b in range(blocks)]
     restored = []
@@ -479,17 +490,20 @@
         parts = arrived[parity]
         if per > 1:
             parts = [
-                part.reshape(focus_count, devices // focus_count, own, piece)
-                .transpose(1, 0, 2, 3)
-                .reshape(blocks, per, own, piece)
-                .transpose(0, 2, 1, 3)
-                .reshape(blocks, own, lane_block)
-                for part in parts
+                (
+                    part.reshape(focus_count, devices // focus_count, own, piece)
+                    .transpose(1, 0, 2, 3)
+                    .reshape(blocks, per, own, piece)
+                    .transpose(0, 2, 1, 3)
+                    .reshape(blocks, 1, own, lane_block),
+                    0,
+                )
+                for part, _ in parts
             ]
-        back = filter_columns(table, rows_response, local_cols[:, parity : parity + 1], mirror, parts, order)
+        back = filter_columns(table, rows_response, local_cols[parity], mirror, parts, order)
         if per > 1:
             back = back.reshape(blocks, own, per, piece).transpose(0, 2, 1, 3).reshape(devices, own, piece)
-        restored.append(lax.all_to_all(back, axes, split_axis=0, concat_axis=0, tiled=True))
+        restored.append(exchange(back))
     even = restore_even(table, restored[0])
     return restore(table, restored[1], even, mirror)
 
@@ -497,4 +511,4 @@
 def solution(mesh):
     in_specs = (P(("field", "focus"), "strip", None), P(), P())
     out_specs = P(("field", "focus", "strip"), None)
-    return jax.shard_map(body, mesh=mesh, in_specs=in_specs, out_specs=out_specs, check_vma=False)
+    return jax.shard_map(program, mesh=mesh, in_specs=in_specs, out_specs=out_specs, check_vma=False)

time: 309 us -> 283 us (0.916)
  Pallas kernels: 206 us -> 195 us
  waiting for transfers between devices: 49.6 us -> 40.1 us
  local copies, waits for them, and re-layouts: 10.4 us -> 6.04 us
  starting transfers between devices: 36.5 us -> 32.6 us
    all_to_all x6 -> x5, waiting for transfers between devices: 49.5 us -> 40.1 us  [exchange(): lax.all_to_all(values, axes, split_axis=0, concat_axis=0, tiled=True)]
    pallas_call x4 -> x3, Pallas kernels: 111 us -> 103 us  [stencil(): pl.pallas_call(kernel, grid_spec=grid_spec, out_shape=jax.ShapeDtypeStruc...]
    all_to_all x6 -> x5, starting transfers between devices: 29.8 us -> 26.3 us  [exchange(): lax.all_to_all(values, axes, split_axis=0, concat_axis=0, tiled=True)]
    pallas_call x4 -> x3, Pallas kernels: 25.2 us -> 24 us  [transform_rows(): pl.pallas_call(rows_kernel, grid=(len(parities), half // tile), in_specs=...]
  transfers between devices with their start and end apart: 10 -> 8, of which waited for: 4 -> 3; matrix products, arithmetic and copies ran while one was open for 3% -> 3% of each run, Pallas kernels for 55% -> 43%
where the time goes in v3:
time: 283 us; the launch traced here: 281 us
  Pallas kernels  195 us (69%)
  waiting for transfers between devices  40.1 us (14%)
  starting transfers between devices  32.6 us (12%)
  other arithmetic  6.82 us (2%)
  local copies, waits for them, and re-layouts  6.04 us (2%)
    pallas_call x3, Pallas kernels, stencil(): pl.pallas_call(kernel, grid_spec=grid_spec, out_shape=jax.ShapeDtypeStruc...  103 us
    all_to_all x5, waiting for transfers between devices, exchange(): lax.all_to_all(values, axes, split_axis=0, concat_axis=0, tiled=True)  40.1 us
    pallas_call x2, Pallas kernels, filter_columns(): pl.pallas_call(functools.partial(columns_kernel, chunks=chunks, half=half...  30.3 us
    all_to_all x5, starting transfers between devices, exchange(): lax.all_to_all(values, axes, split_axis=0, concat_axis=0, tiled=True)  26.3 us
    pallas_call x3, Pallas kernels, transform_rows(): pl.pallas_call(rows_kernel, grid=(len(parities), half // tile), in_specs=...  24 us
    pallas_call x1, Pallas kernels, cosine_halves(): pl.pallas_call(functools.partial(table_kernel, half=half), grid=(2, half...  12.3 us
    pallas_call x1, Pallas kernels, restore(): pl.pallas_call(functools.partial(odd_kernel, half=half, tile=tile), grid=...  9.43 us
    pallas_call x2, Pallas kernels, merge(): pl.pallas_call(functools.partial(merge_kernel, cols=cols), grid=(rows //...  9.31 us
  transfers between devices with their start and end apart: 8, of which 3 were waited for; matrix products, arithmetic and copies ran while one was open for 3% of the time, Pallas kernels for 43%

profile of v3, /device:TPU:0, one launch (start us, length us, event | category | flops | bytes accessed | tf_op | source)
XLA Modules:
  0.0 281.1 jit_solution(13061797541783467207)
XLA Ops:
  0.0 1.5 fusion.20
  1.5 4.9 %collective-permute-start = (bf16[8,4,4096]{2,1,0:T(4,128)(2,1)S(1)}, bf16[8,4,4096]{2,1,0:T(4,128)(2,1)S(1)}, u32[]{:S(2)}, u32[]{:S(2)}) collective-permute-start(bf16[8,4,4096]{2,1,0:T(4,128)(2,1)S(1)} %get-tuple-element.32), channel_id=1, source_target_pairs={{0,1},{1,2},{2,3},{3,4},{4,5},{5,6},{6,7},{8,9},{9,10},{10,11},{11... | collective-permute-start | bytes 786440 | tf_op jit(solution)/shard_map/ppermute | solution.py:31
  6.4 1.3 collective-permute-start.1
  8.4 2.1 fusion.11
  11.4 1.0 pad_maximum_fusion.near
  12.4 0.8 dynamic_slice.3
  13.3 1.0 reshape.243
  15.3 12.3 %cosines.1.table.refs_0_ = bf16[2,2048,2048]{2,1,0:T(8,128)(2,1)} custom-call(f32[2,4,256,128]{3,2,1,0:T(8,128)} %pad_maximum_fusion.near, f32[8,2,1,128]{3,2,1,0:T(1,128)} %pad_maximum_fusion.1.turn), custom_call_target="tpu_custom_call" | custom-call | tf_op jit(solution)/shard_map/cosines/pallas_call | solution.py:224
  27.6 0.9 select_convert_fusion.weights
  28.5 1.2 pad_add_fusion.ends
  29.7 48.3 %stencil.4 = f32[2,256,4096]{2,1,0:T(8,128)} custom-call(s32[1]{0:T(128)} %bitcast.6.place, bf16[8,512,4096]{2,1,0:T(8,128)(2,1)} %below.5, bf16[8,512,4096]{2,1,0:T(8,128)(2,1)} %below.5, bf16[8,512,4096]{2,1,0:T(8,128)(2,1)} %below.5, bf16[8,16,4096]{2,1,0:T(8,128)(2,1)} %pad_add_fusion.ends, bf16[256,512]{1,0:T(8,128)(2,1)} %select_convert_fusion.weights), custom_call_target="tpu_custom_call" | custom-call | flops 17179869184 | bytes 25165824 | tf_op jit(solution)/shard_map/stencil/pallas_call | solution.py:175
  78.1 27.3 %stencil.3.own = f32[2,128,4096]{2,1,0:T(8,128)} custom-call(s32[1]{0:T(128)} %bitcast.5.place, bf16[8,512,4096]{2,1,0:T(8,128)(2,1)} %below.5, bf16[8,512,4096]{2,1,0:T(8,128)(2,1)} %below.5, bf16[8,512,4096]{2,1,0:T(8,128)(2,1)} %below.5, bf16[8,16,4096]{2,1,0:T(8,128)(2,1)} %pad_add_fusion.ends, bf16[256,512]{1,0:T(8,128)(2,1)} %select_convert_fusion.weights), custom_call_target="tpu_custom_call" | custom-call | flops 8589934592 | bytes 12582912 | tf_op jit(solution)/shard_map/stencil/pallas_call | solution.py:175
  105.4 4.7 %merge.2.folded = bf16[2,128,2048]{2,1,0:T(8,128)(2,1)} custom-call(f32[2,128,4096]{2,1,0:T(8,128)} %stencil.3.own, f32[2,256,4096]{2,1,0:T(8,128)} %collective-permute-done.2.other, bf16[256,256]{1,0:T(8,128)(2,1)} %fusion.7.mirror.refs_3_), custom_call_target="tpu_custom_call" | custom-call | tf_op jit(solution)/shard_map/merge/pallas_call | solution.py:254
  110.1 11.4 %transform_rows.3 = bf16[16,2,128,128]{3,2,1,0:T(8,128)(2,1)} custom-call(bf16[2,2048,2048]{2,1,0:T(8,128)(2,1)} %cosines.1.table.refs_0_, bf16[2,128,2048]{2,1,0:T(8,128)(2,1)} %merge.2.folded), custom_call_target="tpu_custom_call" | custom-call | tf_op jit(solution)/shard_map/transform_rows/pallas_call | solution.py:278
  121.5 7.2 %all-to-all-start = ((bf16[16,2,128,128]{3,2,1,0:T(8,128)(2,1)}), bf16[16,2,128,128]{3,2,1,0:T(8,128)(2,1)S(1)}, u32[]{:S(2)}, u32[]{:S(2)}) async-start(bf16[16,2,128,128]{3,2,1,0:T(8,128)(2,1)} %transform_rows.3), calls=%async_computation | async-start | bytes 2097152 | tf_op jit(solution)/shard_map/all_to_all | solution.py:471
  128.7 27.3 %stencil.5.own = f32[2,128,4096]{2,1,0:T(8,128)} custom-call(s32[1]{0:T(128)} %bitcast.7.place, bf16[8,512,4096]{2,1,0:T(8,128)(2,1)} %below.5, bf16[8,512,4096]{2,1,0:T(8,128)(2,1)} %below.5, bf16[8,512,4096]{2,1,0:T(8,128)(2,1)} %below.5, bf16[8,16,4096]{2,1,0:T(8,128)(2,1)} %pad_add_fusion.ends, bf16[256,512]{1,0:T(8,128)(2,1)} %select_convert_fusion.weights), custom_call_target="tpu_custom_call" | custom-call | flops 8589934592 | bytes 12582912 | tf_op jit(solution)/shard_map/stencil/pallas_call | solution.py:175
  156.0 4.6 %merge.3.folded = bf16[2,128,2048]{2,1,0:T(8,128)(2,1)} custom-call(f32[2,128,4096]{2,1,0:T(8,128)} %stencil.5.own, f32[2,256,4096]{2,1,0:T(8,128)} %collective-permute-done.2.other, bf16[256,256]{1,0:T(8,128)(2,1)} %fusion.7.mirror.refs_3_), custom_call_target="tpu_custom_call" | custom-call | tf_op jit(solution)/shard_map/merge/pallas_call | solution.py:254
  160.7 6.3 %transform_rows.5 = bf16[16,1,128,128]{3,2,1,0:T(8,128)(2,1)} custom-call(bf16[2,2048,2048]{2,1,0:T(8,128)(2,1)} %cosines.1.table.refs_0_, bf16[2,128,2048]{2,1,0:T(8,128)(2,1)} %merge.3.folded), custom_call_target="tpu_custom_call" | custom-call | tf_op jit(solution)/shard_map/transform_rows/pallas_call | solution.py:278
  166.9 6.0 %all-to-all-start.1 = ((bf16[16,1,128,128]{3,2,1,0:T(8,128)(2,1)}), bf16[16,1,128,128]{3,2,1,0:T(8,128)(2,1)S(1)}, u32[]{:S(2)}, u32[]{:S(2)}) async-start(bf16[16,1,128,128]{3,2,1,0:T(8,128)(2,1)} %transform_rows.5), calls=%async_computation.1 | async-start | bytes 1048576 | tf_op jit(solution)/shard_map/all_to_all | solution.py:471
  172.9 6.3 %transform_rows.4 = bf16[16,1,128,128]{3,2,1,0:T(8,128)(2,1)} custom-call(bf16[2,2048,2048]{2,1,0:T(8,128)(2,1)} %cosines.1.table.refs_0_, bf16[2,128,2048]{2,1,0:T(8,128)(2,1)} %merge.3.folded), custom_call_target="tpu_custom_call" | custom-call | tf_op jit(solution)/shard_map/transform_rows/pallas_call | solution.py:278
  179.3 9.5 %all-to-all-done.1.refs_5_ = bf16[16,1,128,128]{3,2,1,0:T(8,128)(2,1)S(1)} async-done(((bf16[16,1,128,128]{3,2,1,0:T(8,128)(2,1)}), bf16[16,1,128,128]{3,2,1,0:T(8,128)(2,1)S(1)}, u32[]{:S(2)}, u32[]{:S(2)}) %all-to-all-start.1) | async-done | bytes 524320 | tf_op jit(solution)/shard_map/all_to_all | solution.py:471
  188.7 3.6 %all-to-all-start.2 = ((bf16[16,1,128,128]{3,2,1,0:T(8,128)(2,1)}), bf16[16,1,128,128]{3,2,1,0:T(8,128)(2,1)S(1)}, u32[]{:S(2)}, u32[]{:S(2)}) async-start(bf16[16,1,128,128]{3,2,1,0:T(8,128)(2,1)} %transform_rows.4), calls=%async_computation.2 | async-start | bytes 1048576 | tf_op jit(solution)/shard_map/all_to_all | solution.py:471
  192.3 0.7 slice_bitcast_fusion
  193.0 15.1 %filter_columns.3 = bf16[16,128,256]{2,1,0:T(8,128)(2,1)} custom-call(bf16[2,2048,2048]{2,1,0:T(8,128)(2,1)} %cosines.1.table.refs_0_, f32[2,1,2048]{2,1,0:T(1,128)} %reshape.244.refs_1_, f32[128,1]{1,0:T(8,128)} %get-tuple-element.33.refs_2_, bf16[256,256]{1,0:T(8,128)(2,1)} %fusion.7.mirror.refs_3_, bf16[16,2,128,128]{3,2,1,0:T(8,128)(2,1)} %copy-done, ...), custom_call_target="tpu_custom_call" | custom-call | tf_op jit(solution)/shard_map/filter_columns/pallas_call | solution.py:340
  208.1 5.9 %all-to-all-start.3 = ((bf16[16,128,256]{2,1,0:T(8,128)(2,1)}), bf16[16,128,256]{2,1,0:T(8,128)(2,1)S(1)}, u32[]{:S(2)}, u32[]{:S(2)}) async-start(bf16[16,128,256]{2,1,0:T(8,128)(2,1)} %filter_columns.3), calls=%async_computation.3 | async-start | bytes 2097152 | tf_op jit(solution)/shard_map/all_to_all | solution.py:471
  214.1 15.1 %filter_columns.2 = bf16[16,128,256]{2,1,0:T(8,128)(2,1)} custom-call(bf16[2,2048,2048]{2,1,0:T(8,128)(2,1)} %cosines.1.table.refs_0_, f32[2,1,2048]{2,1,0:T(1,128)} %reshape.244.refs_1_, f32[128,1]{1,0:T(8,128)} %get-tuple-element.34.refs_2_, bf16[256,256]{1,0:T(8,128)(2,1)} %fusion.7.mirror.refs_3_, bf16[16,2,128,128]{3,2,1,0:T(8,128)(2,1)} %copy-done, ...), custom_call_target="tpu_custom_call" | custom-call | tf_op jit(solution)/shard_map/filter_columns/pallas_call | solution.py:340
  229.2 11.4 %all-to-all-done.3.arrived = bf16[16,128,256]{2,1,0:T(8,128)(2,1)S(1)} async-done(((bf16[16,128,256]{2,1,0:T(8,128)(2,1)}), bf16[16,128,256]{2,1,0:T(8,128)(2,1)S(1)}, u32[]{:S(2)}, u32[]{:S(2)}) %all-to-all-start.3) | async-done | bytes 1048608 | tf_op jit(solution)/shard_map/all_to_all | solution.py:471
  240.6 3.7 %all-to-all-start.4 = ((bf16[16,128,256]{2,1,0:T(8,128)(2,1)}), bf16[16,128,256]{2,1,0:T(8,128)(2,1)S(1)}, u32[]{:S(2)}, u32[]{:S(2)}) async-start(bf16[16,128,256]{2,1,0:T(8,128)(2,1)} %filter_columns.2), calls=%async_computation.4 | async-start | bytes 2097152 | tf_op jit(solution)/shard_map/all_to_all | solution.py:471
  244.3 7.2 %restore_even.1.even = f32[256,2048]{1,0:T(8,128)} custom-call(bf16[2,2048,2048]{2,1,0:T(8,128)(2,1)} %cosines.1.table.refs_0_, bf16[16,128,256]{2,1,0:T(8,128)(2,1)} %copy-done.1), custom_call_target="tpu_custom_call" | custom-call | tf_op jit(solution)/shard_map/restore_even/pallas_call | solution.py:378
  251.5 19.2 %all-to-all-done.4.arrived = bf16[16,128,256]{2,1,0:T(8,128)(2,1)S(1)} async-done(((bf16[16,128,256]{2,1,0:T(8,128)(2,1)}), bf16[16,128,256]{2,1,0:T(8,128)(2,1)S(1)}, u32[]{:S(2)}, u32[]{:S(2)}) %all-to-all-start.4) | async-done | bytes 1048608 | tf_op jit(solution)/shard_map/all_to_all | solution.py:471
  270.7 1.0 copy-done.2
  271.7 9.4 %restore.1 = f32[256,4096]{1,0:T(8,128)} custom-call(bf16[2,2048,2048]{2,1,0:T(8,128)(2,1)} %cosines.1.table.refs_0_, bf16[16,128,256]{2,1,0:T(8,128)(2,1)} %copy-done.2, f32[256,2048]{1,0:T(8,128)} %restore_even.1.even, bf16[256,256]{1,0:T(8,128)(2,1)} %fusion.7.mirror.refs_3_), custom_call_target="tpu_custom_call" | custom-call | tf_op jit(solution)/shard_map/restore/pallas_call | solution.py:419
  (30 shorter events, 2.6 us)
Async XLA Ops:
  0.0 13.3 %copy-start.5 = (f32[4096]{0:T(1024)S(1)}, f32[4096]{0:T(1024)}, u32[]{:S(2)}) copy-start(f32[4096]{0:T(1024)} %param.4) | copy-start | bytes 49156
  1.5 27.0 %collective-permute-start = (bf16[8,4,4096]{2,1,0:T(4,128)(2,1)S(1)}, bf16[8,4,4096]{2,1,0:T(4,128)(2,1)S(1)}, u32[]{:S(2)}, u32[]{:S(2)}) collective-permute-start(bf16[8,4,4096]{2,1,0:T(4,128)(2,1)S(1)} %get-tuple-element.32), channel_id=1, source_target_pairs={{0,1},{1,2},{2,3},{3,4},{4,5},{5,6},{6,7},{8,9},{9,10},{10,11},{11... | collective-permute-start | bytes 786440 | tf_op jit(solution)/shard_map/ppermute | solution.py:31
  6.4 22.1 %collective-permute-start.1 = (bf16[8,4,4096]{2,1,0:T(4,128)(2,1)S(1)}, bf16[8,4,4096]{2,1,0:T(4,128)(2,1)S(1)}, u32[]{:S(2)}, u32[]{:S(2)}) collective-permute-start(bf16[8,4,4096]{2,1,0:T(4,128)(2,1)S(1)} %get-tuple-element.31), channel_id=1, source_target_pairs={{1,0},{2,1},{3,2},{4,3},{5,4},{6,5},{7,6},{9,8},{10,9},{11,10},{12... | collective-permute-start | bytes 786440 | tf_op jit(solution)/shard_map/ppermute | solution.py:32
  78.1 27.3 %collective-permute-start.2 = (f32[2,256,4096]{2,1,0:T(8,128)}, f32[2,256,4096]{2,1,0:T(8,128)}, u32[]{:S(2)}, u32[]{:S(2)}) collective-permute-start(f32[2,256,4096]{2,1,0:T(8,128)} %stencil.4), channel_id=1, source_target_pairs={{0,8},{8,0},{1,9},{9,1},{2,10},{10,2},{3,11},{11,3},{4,12},{12,4},... | collective-permute-start | bytes 25165832 | tf_op jit(solution)/shard_map/ppermute | solution.py:474
  121.5 45.5 %all-to-all-start = ((bf16[16,2,128,128]{3,2,1,0:T(8,128)(2,1)}), bf16[16,2,128,128]{3,2,1,0:T(8,128)(2,1)S(1)}, u32[]{:S(2)}, u32[]{:S(2)}) async-start(bf16[16,2,128,128]{3,2,1,0:T(8,128)(2,1)} %transform_rows.3), calls=%async_computation | async-start | bytes 2097152 | tf_op jit(solution)/shard_map/all_to_all | solution.py:471
  166.9 12.3 %copy-start = (bf16[16,2,128,128]{3,2,1,0:T(8,128)(2,1)}, bf16[16,2,128,128]{3,2,1,0:T(8,128)(2,1)S(1)}, u32[]{:S(2)}) copy-start(bf16[16,2,128,128]{3,2,1,0:T(8,128)(2,1)S(1)} %all-to-all-done.refs_4_) | copy-start | bytes 3145732
  166.9 21.8 %all-to-all-start.1 = ((bf16[16,1,128,128]{3,2,1,0:T(8,128)(2,1)}), bf16[16,1,128,128]{3,2,1,0:T(8,128)(2,1)S(1)}, u32[]{:S(2)}, u32[]{:S(2)}) async-start(bf16[16,1,128,128]{3,2,1,0:T(8,128)(2,1)} %transform_rows.5), calls=%async_computation.1 | async-start | bytes 1048576 | tf_op jit(solution)/shard_map/all_to_all | solution.py:471
  188.7 4.3 %copy-start.4 = (bf16[16,1,128,128]{3,2,1,0:T(8,128)(2,1)}, bf16[16,1,128,128]{3,2,1,0:T(8,128)(2,1)S(1)}, u32[]{:S(2)}) copy-start(bf16[16,1,128,128]{3,2,1,0:T(8,128)(2,1)S(1)} %all-to-all-done.1.refs_5_) | copy-start | bytes 1572868
  188.7 19.4 %all-to-all-start.2 = ((bf16[16,1,128,128]{3,2,1,0:T(8,128)(2,1)}), bf16[16,1,128,128]{3,2,1,0:T(8,128)(2,1)S(1)}, u32[]{:S(2)}, u32[]{:S(2)}) async-start(bf16[16,1,128,128]{3,2,1,0:T(8,128)(2,1)} %transform_rows.4), calls=%async_computation.2 | async-start | bytes 1048576 | tf_op jit(solution)/shard_map/all_to_all | solution.py:471
  208.1 6.0 %copy-start.3 = (bf16[16,1,128,128]{3,2,1,0:T(8,128)(2,1)}, bf16[16,1,128,128]{3,2,1,0:T(8,128)(2,1)S(1)}, u32[]{:S(2)}) copy-start(bf16[16,1,128,128]{3,2,1,0:T(8,128)(2,1)S(1)} %all-to-all-done.2.refs_5_) | copy-start | bytes 1572868
  208.1 32.5 %all-to-all-start.3 = ((bf16[16,128,256]{2,1,0:T(8,128)(2,1)}), bf16[16,128,256]{2,1,0:T(8,128)(2,1)S(1)}, u32[]{:S(2)}, u32[]{:S(2)}) async-start(bf16[16,128,256]{2,1,0:T(8,128)(2,1)} %filter_columns.3), calls=%async_computation.3 | async-start | bytes 2097152 | tf_op jit(solution)/shard_map/all_to_all | solution.py:471
  240.6 3.7 %copy-start.1 = (bf16[16,128,256]{2,1,0:T(8,128)(2,1)}, bf16[16,128,256]{2,1,0:T(8,128)(2,1)S(1)}, u32[]{:S(2)}) copy-start(bf16[16,128,256]{2,1,0:T(8,128)(2,1)S(1)} %all-to-all-done.3.arrived) | copy-start | bytes 3145732
  240.6 30.1 %all-to-all-start.4 = ((bf16[16,128,256]{2,1,0:T(8,128)(2,1)}), bf16[16,128,256]{2,1,0:T(8,128)(2,1)S(1)}, u32[]{:S(2)}, u32[]{:S(2)}) async-start(bf16[16,128,256]{2,1,0:T(8,128)(2,1)} %filter_columns.2), calls=%async_computation.4 | async-start | bytes 2097152 | tf_op jit(solution)/shard_map/all_to_all | solution.py:471
  270.7 1.0 copy-start.2

commit v4 on v3

--- a/solution.py
+++ b/solution.py
@@ -51,14 +51,13 @@
 
 def stencil_kernel(
     place, main, above, below, ends, weights, out,
-    edges, copies_a, copies_b, laps_a, laps_b, held,
+    edges, copies_a, copies_b, laps_a, laps_b, joined,
     *, tile_rows, count, cols, tiles, step, parts,
 ):
     tile = place[0] + pl.program_id(0)
     first = tile == 0
     last = tile == tiles - 1
     edge_row = lax.broadcasted_iota(jnp.int32, (16, cols), 0)
-    lane = lax.broadcasted_iota(jnp.int32, (step, 128), 1)
     for s in range(count):
         upper = jnp.where(first, ends[s], above[s])
         lower = jnp.where(last, ends[s], below[s])
@@ -111,12 +110,8 @@
                 )
                 numerator += weight * centers[s, pl.ds(8 + r, step), :]
                 denominator += weight
-            for k, value in enumerate((numerator, denominator)):
-                turned = pltpu.roll(value, 64, 1)
-                if not (isinstance(frame, int) and frame == 0):
-                    joined = jnp.where(lane < 64, held[k, pl.ds(r, step), :], turned)
-                    out[k, pl.ds(r, step), pl.ds(start_of(frame), 128)] = joined
-                held[k, pl.ds(r, step), :] = turned
+            joined[0, frame, pl.ds(r, step), :] = numerator
+            joined[1, frame, pl.ds(r, step), :] = denominator
 
     def both(slot, frame):
         spread_edges(slot, frame)
@@ -138,6 +133,15 @@
     both(1, frames - 2)
     both(0, frames - 1)
     gather(0, frames - 1, 0, tile_rows)
+    lane = lax.broadcasted_iota(jnp.int32, (tile_rows, 128), 1)
+
+    def shift_back(j, carry):
+        at = pl.ds(pl.multiple_of(j * 128, 128), 128)
+        for k in range(2):
+            out[k, :, at] = pltpu.roll(jnp.where(lane >= 64, joined[k, j], joined[k, j + 1]), 64, 1)
+        return carry
+
+    lax.fori_loop(0, frames - 1, shift_back, 0)
 
 
 def stencil(place, slices, ends, weights, out_rows):
@@ -146,7 +150,7 @@
     per = tile_rows // 16
     blocks = rows // 16
     step = min(16, tile_rows)
-    parts = math.gcd(math.gcd(4, count), tile_rows // step)
+    parts = 1
     kernel = functools.partial(
         stencil_kernel, tile_rows=tile_rows, count=count, cols=cols, tiles=rows // tile_rows, step=step, parts=parts
     )
@@ -168,7 +172,7 @@
             pltpu.VMEM((count, tile_rows + 16, 128), jnp.float32),
             pltpu.VMEM((count, 3, tile_rows, 128), jnp.float32),
             pltpu.VMEM((count, 3, tile_rows, 128), jnp.float32),
-            pltpu.VMEM((2, tile_rows, 128), jnp.float32),
+            pltpu.VMEM((2, cols // 128 + 1, tile_rows, 128), jnp.float32),
         ],
     )
     pixels = count * out_rows * cols
@@ -184,28 +188,35 @@
 
 def table_kernel(near, turn, out, *, half):
     parity, block = pl.program_id(0), pl.program_id(1)
-    group = min(64, out.shape[1])
+    period = near.shape[2]
+    group = min(64, period)
     norm = math.sqrt(1.0 / half)
-    for at in range(0, out.shape[1], group):
-        rows = pl.ds(at, group)
-        near_cos, near_sin, step_cos, step_sin = (near[0, k, rows, :] for k in range(4))
-        low_cos = near_cos * turn[0, 0] - near_sin * turn[0, 1]
-        low_sin = near_sin * turn[0, 0] + near_cos * turn[0, 1]
-        row = at + lax.broadcasted_iota(jnp.int32, low_cos.shape, 0)
-        first = (row == 0) & (parity == 0) & (block == 0)
-        scale = jnp.where(first, norm * math.sqrt(0.5), norm)
-        before = scale * low_cos
-        here = scale * (step_cos * low_cos - step_sin * low_sin)
-        twice = step_cos + step_cos
-        out[0, rows, pl.ds(0, 128)] = before.astype(jnp.bfloat16)
-        for j in range(1, half // 128):
-            out[0, rows, pl.ds(j * 128, 128)] = here.astype(jnp.bfloat16)
-            before, here = here, twice * here - before
+
+    def fill(b, carry):
+        for at in range(0, period, group):
+            near_cos, near_sin, step_cos, step_sin = (near[0, k, pl.ds(at, group), :] for k in range(4))
+            low_cos = near_cos * turn[b, 0] - near_sin * turn[b, 1]
+            low_sin = near_sin * turn[b, 0] + near_cos * turn[b, 1]
+            row = at + lax.broadcasted_iota(jnp.int32, low_cos.shape, 0)
+            first = (row == 0) & (parity == 0) & (block == 0) & (b == 0)
+            scale = jnp.where(first, norm * math.sqrt(0.5), norm)
+            before = scale * low_cos
+            here = scale * (step_cos * low_cos - step_sin * low_sin)
+            twice = step_cos + step_cos
+            rows = pl.ds(pl.multiple_of(b * period + at, group), group)
+            out[0, rows, pl.ds(0, 128)] = before.astype(jnp.bfloat16)
+            for j in range(1, half // 128):
+                out[0, rows, pl.ds(j * 128, 128)] = here.astype(jnp.bfloat16)
+                before, here = here, twice * here - before
+        return carry
+
+    lax.fori_loop(0, out.shape[1] // period, fill, 0)
 
 
 def cosine_halves(length):
     half = length // 2
     rows = min(256, half)
+    tall = min(1024, half)
     assert 512 * rows % (4 * length) == 0
     unit = jnp.float32(math.pi / (2 * length))
 
@@ -223,12 +234,12 @@
     turn = jnp.stack(pair((2 * iota(blocks, 2) + 1) * (2 * rows * iota(blocks, 0))), axis=1)
     return pl.pallas_call(
         functools.partial(table_kernel, half=half),
-        grid=(2, half // rows),
+        grid=(2, half // tall),
         in_specs=[
             pl.BlockSpec((1, 4, rows, 128), lambda p, b: (p, 0, 0, 0)),
-            pl.BlockSpec((1, 2, 1, 128), lambda p, b: (b, 0, 0, 0)),
-        ],
-        out_specs=pl.BlockSpec((1, rows, half), lambda p, b: (p, b, 0)),
+            pl.BlockSpec((tall // rows, 2, 1, 128), lambda p, b: (b, 0, 0, 0)),
+        ],
+        out_specs=pl.BlockSpec((1, tall, half), lambda p, b: (p, b, 0)),
         out_shape=jax.ShapeDtypeStruct((2, half, half), jnp.bfloat16),
         name="cosines",
     )(near, turn)
@@ -273,7 +284,7 @@
 def transform_rows(table, folded, parities, devices):
     _, rows, half = folded.shape
     own = half // devices
-    tile = max(512, own)
+    tile = max(1024, own)
     first = parities[0]
     return pl.pallas_call(
         rows_kernel,
@@ -331,7 +342,7 @@
 def filter_columns(table, rows_response, cols_response, mirror, arrived, order):
     half = table.shape[1]
     blocks, _, own, _ = arrived[0][0].shape
-    tile = min(512, half)
+    tile = min(1024, half)
     chunks = len(arrived)
 
     def whole(part, parity):
@@ -374,7 +385,7 @@
 def restore_even(table, arrived):
     half = table.shape[1]
     devices, own, rows = arrived.shape
-    tile = min(512, half)
+    tile = min(1024, half)
     return pl.pallas_call(
         functools.partial(even_kernel, half=half),
         grid=(half // tile,),
@@ -415,7 +426,7 @@
 def restore(table, arrived, even, mirror):
     half = table.shape[1]
     devices, own, rows = arrived.shape
-    tile = min(512, half)
+    tile = min(1024, half)
     return pl.pallas_call(
         functools.partial(odd_kernel, half=half, tile=tile),
         grid=(half // tile,),

time: 283 us -> 267 us (0.943)
  Pallas kernels: 195 us -> 177 us
  waiting for transfers between devices: 40.1 us -> 45.4 us
    pallas_call x3, Pallas kernels: 103 us -> 97.4 us  [stencil(): pl.pallas_call(kernel, grid_spec=grid_spec, out_shape=jax.ShapeDtypeStruc...]
    all_to_all x5, waiting for transfers between devices: 40.1 us -> 45.4 us  [exchange(): lax.all_to_all(values, axes, split_axis=0, concat_axis=0, tiled=True)]
    pallas_call x2, Pallas kernels: 30.3 us -> 26.2 us  [filter_columns(): pl.pallas_call(functools.partial(columns_kernel, chunks=chunks, half=half...]
    pallas_call x1, Pallas kernels: 12.3 us -> 8.9 us  [cosine_halves(): pl.pallas_call(functools.partial(table_kernel, half=half), grid=(2, half...]
    pallas_call x3, Pallas kernels: 24 us -> 20.7 us  [transform_rows(): pl.pallas_call(rows_kernel, grid=(len(parities), half // tile), in_specs=...]
  transfers between devices with their start and end apart: 8 -> 8, of which waited for: 3 -> 4; matrix products, arithmetic and copies ran while one was open for 3% -> 3% of each run, Pallas kernels for 43% -> 41%
where the time goes in v4:
time: 267 us
  Pallas kernels  177 us (66%)
  waiting for transfers between devices  45.4 us (17%)
  starting transfers between devices  30.9 us (12%)
  other arithmetic  6.82 us (3%)
  local copies, waits for them, and re-layouts  6.04 us (2%)
    pallas_call x3, Pallas kernels, stencil(): pl.pallas_call(kernel, grid_spec=grid_spec, out_shape=jax.ShapeDtypeStruc...  97.4 us
    all_to_all x5, waiting for transfers between devices, exchange(): lax.all_to_all(values, axes, split_axis=0, concat_axis=0, tiled=True)  45.4 us
    pallas_call x2, Pallas kernels, filter_columns(): pl.pallas_call(functools.partial(columns_kernel, chunks=chunks, half=half...  26.2 us
    all_to_all x5, starting transfers between devices, exchange(): lax.all_to_all(values, axes, split_axis=0, concat_axis=0, tiled=True)  24.7 us
    pallas_call x3, Pallas kernels, transform_rows(): pl.pallas_call(rows_kernel, grid=(len(parities), half // tile), in_specs=...  20.7 us
    pallas_call x2, Pallas kernels, merge(): pl.pallas_call(functools.partial(merge_kernel, cols=cols), grid=(rows //...  9.31 us
    pallas_call x1, Pallas kernels, cosine_halves(): pl.pallas_call(functools.partial(table_kernel, half=half), grid=(2, half...  8.9 us
    pallas_call x1, Pallas kernels, restore(): pl.pallas_call(functools.partial(odd_kernel, half=half, tile=tile), grid=...  8.68 us
  transfers between devices with their start and end apart: 8, of which 4 were waited for; matrix products, arithmetic and copies ran while one was open for 3% of the time, Pallas kernels for 41%

profile of v4, /device:TPU:0, one launch (start us, length us, event | category | flops | bytes accessed | tf_op | source)
XLA Modules:
  0.0 266.8 jit_solution(2330308888715070537)
XLA Ops:
  0.0 1.5 fusion.20
  1.5 4.9 %collective-permute-start = (bf16[8,4,4096]{2,1,0:T(4,128)(2,1)S(1)}, bf16[8,4,4096]{2,1,0:T(4,128)(2,1)S(1)}, u32[]{:S(2)}, u32[]{:S(2)}) collective-permute-start(bf16[8,4,4096]{2,1,0:T(4,128)(2,1)S(1)} %get-tuple-element.32), channel_id=1, source_target_pairs={{0,1},{1,2},{2,3},{3,4},{4,5},{5,6},{6,7},{8,9},{9,10},{10,11},{11... | collective-permute-start | bytes 786440 | tf_op jit(solution)/shard_map/ppermute | solution.py:31
  6.4 1.3 collective-permute-start.1
  8.4 2.1 fusion.11
  11.4 1.0 pad_maximum_fusion.near
  12.4 0.8 dynamic_slice.3
  13.3 1.0 reshape.243
  15.3 8.9 %cosines.1.table.refs_0_ = bf16[2,2048,2048]{2,1,0:T(8,128)(2,1)} custom-call(f32[2,4,256,128]{3,2,1,0:T(8,128)} %pad_maximum_fusion.near, f32[8,2,1,128]{3,2,1,0:T(1,128)} %pad_maximum_fusion.1.turn), custom_call_target="tpu_custom_call" | custom-call | tf_op jit(solution)/shard_map/cosines/pallas_call | solution.py:235
  24.2 0.9 select_convert_fusion.weights
  25.1 1.2 pad_add_fusion.ends
  26.4 45.6 %stencil.4 = f32[2,256,4096]{2,1,0:T(8,128)} custom-call(s32[1]{0:T(128)} %bitcast.6.place, bf16[8,512,4096]{2,1,0:T(8,128)(2,1)} %below.5, bf16[8,512,4096]{2,1,0:T(8,128)(2,1)} %below.5, bf16[8,512,4096]{2,1,0:T(8,128)(2,1)} %below.5, bf16[8,16,4096]{2,1,0:T(8,128)(2,1)} %pad_add_fusion.ends, bf16[256,512]{1,0:T(8,128)(2,1)} %select_convert_fusion.weights), custom_call_target="tpu_custom_call" | custom-call | flops 17179869184 | bytes 25165824 | tf_op jit(solution)/shard_map/stencil/pallas_call | solution.py:179
  71.9 25.9 %stencil.3.own = f32[2,128,4096]{2,1,0:T(8,128)} custom-call(s32[1]{0:T(128)} %bitcast.5.place, bf16[8,512,4096]{2,1,0:T(8,128)(2,1)} %below.5, bf16[8,512,4096]{2,1,0:T(8,128)(2,1)} %below.5, bf16[8,512,4096]{2,1,0:T(8,128)(2,1)} %below.5, bf16[8,16,4096]{2,1,0:T(8,128)(2,1)} %pad_add_fusion.ends, bf16[256,512]{1,0:T(8,128)(2,1)} %select_convert_fusion.weights), custom_call_target="tpu_custom_call" | custom-call | flops 8589934592 | bytes 12582912 | tf_op jit(solution)/shard_map/stencil/pallas_call | solution.py:179
  97.8 4.7 %merge.2.folded = bf16[2,128,2048]{2,1,0:T(8,128)(2,1)} custom-call(f32[2,128,4096]{2,1,0:T(8,128)} %stencil.3.own, f32[2,256,4096]{2,1,0:T(8,128)} %collective-permute-done.2.other, bf16[256,256]{1,0:T(8,128)(2,1)} %fusion.7.mirror.refs_3_), custom_call_target="tpu_custom_call" | custom-call | tf_op jit(solution)/shard_map/merge/pallas_call | solution.py:265
  102.5 9.5 %transform_rows.3 = bf16[16,2,128,128]{3,2,1,0:T(8,128)(2,1)} custom-call(bf16[2,2048,2048]{2,1,0:T(8,128)(2,1)} %cosines.1.table.refs_0_, bf16[2,128,2048]{2,1,0:T(8,128)(2,1)} %merge.2.folded), custom_call_target="tpu_custom_call" | custom-call | tf_op jit(solution)/shard_map/transform_rows/pallas_call | solution.py:289
  112.0 7.2 %all-to-all-start = ((bf16[16,2,128,128]{3,2,1,0:T(8,128)(2,1)}), bf16[16,2,128,128]{3,2,1,0:T(8,128)(2,1)S(1)}, u32[]{:S(2)}, u32[]{:S(2)}) async-start(bf16[16,2,128,128]{3,2,1,0:T(8,128)(2,1)} %transform_rows.3), calls=%async_computation | async-start | bytes 2097152 | tf_op jit(solution)/shard_map/all_to_all | solution.py:482
  119.2 25.9 %stencil.5.own = f32[2,128,4096]{2,1,0:T(8,128)} custom-call(s32[1]{0:T(128)} %bitcast.7.place, bf16[8,512,4096]{2,1,0:T(8,128)(2,1)} %below.5, bf16[8,512,4096]{2,1,0:T(8,128)(2,1)} %below.5, bf16[8,512,4096]{2,1,0:T(8,128)(2,1)} %below.5, bf16[8,16,4096]{2,1,0:T(8,128)(2,1)} %pad_add_fusion.ends, bf16[256,512]{1,0:T(8,128)(2,1)} %select_convert_fusion.weights), custom_call_target="tpu_custom_call" | custom-call | flops 8589934592 | bytes 12582912 | tf_op jit(solution)/shard_map/stencil/pallas_call | solution.py:179
  145.1 4.6 %merge.3.folded = bf16[2,128,2048]{2,1,0:T(8,128)(2,1)} custom-call(f32[2,128,4096]{2,1,0:T(8,128)} %stencil.5.own, f32[2,256,4096]{2,1,0:T(8,128)} %collective-permute-done.2.other, bf16[256,256]{1,0:T(8,128)(2,1)} %fusion.7.mirror.refs_3_), custom_call_target="tpu_custom_call" | custom-call | tf_op jit(solution)/shard_map/merge/pallas_call | solution.py:265
  149.7 5.6 %transform_rows.5 = bf16[16,1,128,128]{3,2,1,0:T(8,128)(2,1)} custom-call(bf16[2,2048,2048]{2,1,0:T(8,128)(2,1)} %cosines.1.table.refs_0_, bf16[2,128,2048]{2,1,0:T(8,128)(2,1)} %merge.3.folded), custom_call_target="tpu_custom_call" | custom-call | tf_op jit(solution)/shard_map/transform_rows/pallas_call | solution.py:289
  155.3 6.0 %all-to-all-start.1 = ((bf16[16,1,128,128]{3,2,1,0:T(8,128)(2,1)}), bf16[16,1,128,128]{3,2,1,0:T(8,128)(2,1)S(1)}, u32[]{:S(2)}, u32[]{:S(2)}) async-start(bf16[16,1,128,128]{3,2,1,0:T(8,128)(2,1)} %transform_rows.5), calls=%async_computation.1 | async-start | bytes 1048576 | tf_op jit(solution)/shard_map/all_to_all | solution.py:482
  161.3 5.6 %transform_rows.4 = bf16[16,1,128,128]{3,2,1,0:T(8,128)(2,1)} custom-call(bf16[2,2048,2048]{2,1,0:T(8,128)(2,1)} %cosines.1.table.refs_0_, bf16[2,128,2048]{2,1,0:T(8,128)(2,1)} %merge.3.folded), custom_call_target="tpu_custom_call" | custom-call | tf_op jit(solution)/shard_map/transform_rows/pallas_call | solution.py:289
  166.9 10.2 %all-to-all-done.1.refs_5_ = bf16[16,1,128,128]{3,2,1,0:T(8,128)(2,1)S(1)} async-done(((bf16[16,1,128,128]{3,2,1,0:T(8,128)(2,1)}), bf16[16,1,128,128]{3,2,1,0:T(8,128)(2,1)S(1)}, u32[]{:S(2)}, u32[]{:S(2)}) %all-to-all-start.1) | async-done | bytes 524320 | tf_op jit(solution)/shard_map/all_to_all | solution.py:482
  177.1 3.6 %all-to-all-start.2 = ((bf16[16,1,128,128]{3,2,1,0:T(8,128)(2,1)}), bf16[16,1,128,128]{3,2,1,0:T(8,128)(2,1)S(1)}, u32[]{:S(2)}, u32[]{:S(2)}) async-start(bf16[16,1,128,128]{3,2,1,0:T(8,128)(2,1)} %transform_rows.4), calls=%async_computation.2 | async-start | bytes 1048576 | tf_op jit(solution)/shard_map/all_to_all | solution.py:482
  181.4 13.1 %filter_columns.3 = bf16[16,128,256]{2,1,0:T(8,128)(2,1)} custom-call(bf16[2,2048,2048]{2,1,0:T(8,128)(2,1)} %cosines.1.table.refs_0_, f32[2,1,2048]{2,1,0:T(1,128)} %reshape.244.refs_1_, f32[128,1]{1,0:T(8,128)} %get-tuple-element.33.refs_2_, bf16[256,256]{1,0:T(8,128)(2,1)} %fusion.7.mirror.refs_3_, bf16[16,2,128,128]{3,2,1,0:T(8,128)(2,1)} %copy-done, ...), custom_call_target="tpu_custom_call" | custom-call | tf_op jit(solution)/shard_map/filter_columns/pallas_call | solution.py:351
  194.5 1.9 all-to-all-done.2.refs_5_
  196.4 4.0 %all-to-all-start.3 = ((bf16[16,128,256]{2,1,0:T(8,128)(2,1)}), bf16[16,128,256]{2,1,0:T(8,128)(2,1)S(1)}, u32[]{:S(2)}, u32[]{:S(2)}) async-start(bf16[16,128,256]{2,1,0:T(8,128)(2,1)} %filter_columns.3), calls=%async_computation.3 | async-start | bytes 2097152 | tf_op jit(solution)/shard_map/all_to_all | solution.py:482
  200.5 13.1 %filter_columns.2 = bf16[16,128,256]{2,1,0:T(8,128)(2,1)} custom-call(bf16[2,2048,2048]{2,1,0:T(8,128)(2,1)} %cosines.1.table.refs_0_, f32[2,1,2048]{2,1,0:T(1,128)} %reshape.244.refs_1_, f32[128,1]{1,0:T(8,128)} %get-tuple-element.34.refs_2_, bf16[256,256]{1,0:T(8,128)(2,1)} %fusion.7.mirror.refs_3_, bf16[16,2,128,128]{3,2,1,0:T(8,128)(2,1)} %copy-done, ...), custom_call_target="tpu_custom_call" | custom-call | tf_op jit(solution)/shard_map/filter_columns/pallas_call | solution.py:351
  213.6 13.4 %all-to-all-done.3.arrived = bf16[16,128,256]{2,1,0:T(8,128)(2,1)S(1)} async-done(((bf16[16,128,256]{2,1,0:T(8,128)(2,1)}), bf16[16,128,256]{2,1,0:T(8,128)(2,1)S(1)}, u32[]{:S(2)}, u32[]{:S(2)}) %all-to-all-start.3) | async-done | bytes 1048608 | tf_op jit(solution)/shard_map/all_to_all | solution.py:482
  227.0 3.9 %all-to-all-start.4 = ((bf16[16,128,256]{2,1,0:T(8,128)(2,1)}), bf16[16,128,256]{2,1,0:T(8,128)(2,1)S(1)}, u32[]{:S(2)}, u32[]{:S(2)}) async-start(bf16[16,128,256]{2,1,0:T(8,128)(2,1)} %filter_columns.2), calls=%async_computation.4 | async-start | bytes 2097152 | tf_op jit(solution)/shard_map/all_to_all | solution.py:482
  230.9 6.3 %restore_even.1.even = f32[256,2048]{1,0:T(8,128)} custom-call(bf16[2,2048,2048]{2,1,0:T(8,128)(2,1)} %cosines.1.table.refs_0_, bf16[16,128,256]{2,1,0:T(8,128)(2,1)} %copy-done.1), custom_call_target="tpu_custom_call" | custom-call | tf_op jit(solution)/shard_map/restore_even/pallas_call | solution.py:389
  237.2 19.8 %all-to-all-done.4.arrived = bf16[16,128,256]{2,1,0:T(8,128)(2,1)S(1)} async-done(((bf16[16,128,256]{2,1,0:T(8,128)(2,1)}), bf16[16,128,256]{2,1,0:T(8,128)(2,1)S(1)}, u32[]{:S(2)}, u32[]{:S(2)}) %all-to-all-start.4) | async-done | bytes 1048608 | tf_op jit(solution)/shard_map/all_to_all | solution.py:482
  257.1 1.0 copy-done.2
  258.1 8.7 %restore.1 = f32[256,4096]{1,0:T(8,128)} custom-call(bf16[2,2048,2048]{2,1,0:T(8,128)(2,1)} %cosines.1.table.refs_0_, bf16[16,128,256]{2,1,0:T(8,128)(2,1)} %copy-done.2, f32[256,2048]{1,0:T(8,128)} %restore_even.1.even, bf16[256,256]{1,0:T(8,128)(2,1)} %fusion.7.mirror.refs_3_), custom_call_target="tpu_custom_call" | custom-call | tf_op jit(solution)/shard_map/restore/pallas_call | solution.py:430
  (30 shorter events, 3.3 us)
Async XLA Ops:
  0.0 13.3 %copy-start.5 = (f32[4096]{0:T(1024)S(1)}, f32[4096]{0:T(1024)}, u32[]{:S(2)}) copy-start(f32[4096]{0:T(1024)} %param.4) | copy-start | bytes 49156
  1.5 23.6 %collective-permute-start = (bf16[8,4,4096]{2,1,0:T(4,128)(2,1)S(1)}, bf16[8,4,4096]{2,1,0:T(4,128)(2,1)S(1)}, u32[]{:S(2)}, u32[]{:S(2)}) collective-permute-start(bf16[8,4,4096]{2,1,0:T(4,128)(2,1)S(1)} %get-tuple-element.32), channel_id=1, source_target_pairs={{0,1},{1,2},{2,3},{3,4},{4,5},{5,6},{6,7},{8,9},{9,10},{10,11},{11... | collective-permute-start | bytes 786440 | tf_op jit(solution)/shard_map/ppermute | solution.py:31
  6.4 18.7 %collective-permute-start.1 = (bf16[8,4,4096]{2,1,0:T(4,128)(2,1)S(1)}, bf16[8,4,4096]{2,1,0:T(4,128)(2,1)S(1)}, u32[]{:S(2)}, u32[]{:S(2)}) collective-permute-start(bf16[8,4,4096]{2,1,0:T(4,128)(2,1)S(1)} %get-tuple-element.31), channel_id=1, source_target_pairs={{1,0},{2,1},{3,2},{4,3},{5,4},{6,5},{7,6},{9,8},{10,9},{11,10},{12... | collective-permute-start | bytes 786440 | tf_op jit(solution)/shard_map/ppermute | solution.py:32
  71.9 25.9 %collective-permute-start.2 = (f32[2,256,4096]{2,1,0:T(8,128)}, f32[2,256,4096]{2,1,0:T(8,128)}, u32[]{:S(2)}, u32[]{:S(2)}) collective-permute-start(f32[2,256,4096]{2,1,0:T(8,128)} %stencil.4), channel_id=1, source_target_pairs={{0,8},{8,0},{1,9},{9,1},{2,10},{10,2},{3,11},{11,3},{4,12},{12,4},... | collective-permute-start | bytes 25165832 | tf_op jit(solution)/shard_map/ppermute | solution.py:485
  112.0 43.3 %all-to-all-start = ((bf16[16,2,128,128]{3,2,1,0:T(8,128)(2,1)}), bf16[16,2,128,128]{3,2,1,0:T(8,128)(2,1)S(1)}, u32[]{:S(2)}, u32[]{:S(2)}) async-start(bf16[16,2,128,128]{3,2,1,0:T(8,128)(2,1)} %transform_rows.3), calls=%async_computation | async-start | bytes 2097152 | tf_op jit(solution)/shard_map/all_to_all | solution.py:482
  155.3 11.6 %copy-start = (bf16[16,2,128,128]{3,2,1,0:T(8,128)(2,1)}, bf16[16,2,128,128]{3,2,1,0:T(8,128)(2,1)S(1)}, u32[]{:S(2)}) copy-start(bf16[16,2,128,128]{3,2,1,0:T(8,128)(2,1)S(1)} %all-to-all-done.refs_4_) | copy-start | bytes 3145732
  155.3 21.8 %all-to-all-start.1 = ((bf16[16,1,128,128]{3,2,1,0:T(8,128)(2,1)}), bf16[16,1,128,128]{3,2,1,0:T(8,128)(2,1)S(1)}, u32[]{:S(2)}, u32[]{:S(2)}) async-start(bf16[16,1,128,128]{3,2,1,0:T(8,128)(2,1)} %transform_rows.5), calls=%async_computation.1 | async-start | bytes 1048576 | tf_op jit(solution)/shard_map/all_to_all | solution.py:482
  177.1 4.3 %copy-start.4 = (bf16[16,1,128,128]{3,2,1,0:T(8,128)(2,1)}, bf16[16,1,128,128]{3,2,1,0:T(8,128)(2,1)S(1)}, u32[]{:S(2)}) copy-start(bf16[16,1,128,128]{3,2,1,0:T(8,128)(2,1)S(1)} %all-to-all-done.1.refs_5_) | copy-start | bytes 1572868
  177.1 19.3 %all-to-all-start.2 = ((bf16[16,1,128,128]{3,2,1,0:T(8,128)(2,1)}), bf16[16,1,128,128]{3,2,1,0:T(8,128)(2,1)S(1)}, u32[]{:S(2)}, u32[]{:S(2)}) async-start(bf16[16,1,128,128]{3,2,1,0:T(8,128)(2,1)} %transform_rows.4), calls=%async_computation.2 | async-start | bytes 1048576 | tf_op jit(solution)/shard_map/all_to_all | solution.py:482
  196.4 4.0 %copy-start.3 = (bf16[16,1,128,128]{3,2,1,0:T(8,128)(2,1)}, bf16[16,1,128,128]{3,2,1,0:T(8,128)(2,1)S(1)}, u32[]{:S(2)}) copy-start(bf16[16,1,128,128]{3,2,1,0:T(8,128)(2,1)S(1)} %all-to-all-done.2.refs_5_) | copy-start | bytes 1572868
  196.4 30.5 %all-to-all-start.3 = ((bf16[16,128,256]{2,1,0:T(8,128)(2,1)}), bf16[16,128,256]{2,1,0:T(8,128)(2,1)S(1)}, u32[]{:S(2)}, u32[]{:S(2)}) async-start(bf16[16,128,256]{2,1,0:T(8,128)(2,1)} %filter_columns.3), calls=%async_computation.3 | async-start | bytes 2097152 | tf_op jit(solution)/shard_map/all_to_all | solution.py:482
  227.0 3.9 %copy-start.1 = (bf16[16,128,256]{2,1,0:T(8,128)(2,1)}, bf16[16,128,256]{2,1,0:T(8,128)(2,1)S(1)}, u32[]{:S(2)}) copy-start(bf16[16,128,256]{2,1,0:T(8,128)(2,1)S(1)} %all-to-all-done.3.arrived) | copy-start | bytes 3145732
  227.0 30.1 %all-to-all-start.4 = ((bf16[16,128,256]{2,1,0:T(8,128)(2,1)}), bf16[16,128,256]{2,1,0:T(8,128)(2,1)S(1)}, u32[]{:S(2)}, u32[]{:S(2)}) async-start(bf16[16,128,256]{2,1,0:T(8,128)(2,1)} %filter_columns.2), calls=%async_computation.4 | async-start | bytes 2097152 | tf_op jit(solution)/shard_map/all_to_all | solution.py:482
  257.1 1.0 copy-start.2

commit v5 on v4

--- a/solution.py
+++ b/solution.py
@@ -50,10 +50,18 @@
 
 
 def stencil_kernel(
-    place, main, above, below, ends, weights, out,
-    edges, copies_a, copies_b, laps_a, laps_b, joined,
-    *, tile_rows, count, cols, tiles, step, parts,
+    place, main, above, below, ends, *rest, merging,
+    tile_rows, count, cols, tiles, step, parts,
 ):
+    if merging:
+        received, folded, weights, edges, copies_a, copies_b, laps_a, laps_b, joined, out = rest
+    else:
+        out, weights, edges, copies_a, copies_b, laps_a, laps_b, joined = rest
+
+    @pl.when(pl.program_id(0) == 0)
+    def _():
+        weights[...] = band()
+
     tile = place[0] + pl.program_id(0)
     first = tile == 0
     last = tile == tiles - 1
@@ -95,8 +103,7 @@
 
     def gather(slot, frame, low, high):
         for r in range(low, high, step):
-            numerator = jnp.zeros((step, 128), jnp.float32)
-            denominator = numerator
+            numerator = denominator = None
             for s in range(count):
                 centers = copies[slot]
 
@@ -108,8 +115,9 @@
                 weight = floor_weight + (
                     fine * fine + 0.5 * (middle * middle + 0.5 * (coarse * coarse))
                 )
-                numerator += weight * centers[s, pl.ds(8 + r, step), :]
-                denominator += weight
+                weighted = weight * centers[s, pl.ds(8 + r, step), :]
+                numerator = weighted if s == 0 else numerator + weighted
+                denominator = weight if s == 0 else denominator + weight
             joined[0, frame, pl.ds(r, step), :] = numerator
             joined[1, frame, pl.ds(r, step), :] = denominator
 
@@ -142,19 +150,23 @@
         return carry
 
     lax.fori_loop(0, frames - 1, shift_back, 0)
-
-
-def stencil(place, slices, ends, weights, out_rows):
+    if merging:
+        fold(out, received, folded)
+
+
+def stencil(place, slices, ends, out_rows, received=None, at=0):
     count, rows, cols = slices.shape
     tile_rows = math.gcd(128, out_rows)
     per = tile_rows // 16
     blocks = rows // 16
     step = min(16, tile_rows)
     parts = 1
+    merging = received is not None
     kernel = functools.partial(
-        stencil_kernel, tile_rows=tile_rows, count=count, cols=cols, tiles=rows // tile_rows, step=step, parts=parts
+        stencil_kernel, merging=merging, tile_rows=tile_rows, count=count, cols=cols, tiles=rows // tile_rows, step=step, parts=parts
     )
     edge = (count, 16, cols)
+    width, kind = (cols // 2, jnp.bfloat16) if merging else (cols, jnp.float32)
     grid_spec = pltpu.PrefetchScalarGridSpec(
         num_scalar_prefetch=1,
         grid=(out_rows // tile_rows,),
@@ -163,46 +175,49 @@
             pl.BlockSpec(edge, lambda t, at: (0, jnp.maximum((at[0] + t) * per - 1, 0), 0)),
             pl.BlockSpec(edge, lambda t, at: (0, jnp.minimum((at[0] + t) * per + per, blocks - 1), 0)),
             pl.BlockSpec(edge, lambda t, at: (0, 0, 0)),
-            pl.BlockSpec((256, 512), lambda t, at: (0, 0)),
-        ],
-        out_specs=pl.BlockSpec((2, tile_rows, cols), lambda t, at: (0, t, 0)),
+        ]
+        + [pl.BlockSpec((2, tile_rows, cols), lambda t, place: (0, at // tile_rows + t, 0))] * merging,
+        out_specs=pl.BlockSpec((2, tile_rows, width), lambda t, at: (0, t, 0)),
         scratch_shapes=[
+            pltpu.VMEM((256, 512), jnp.bfloat16),
             pltpu.VMEM(edge, jnp.bfloat16),
             pltpu.VMEM((count, tile_rows + 16, 128), jnp.float32),
             pltpu.VMEM((count, tile_rows + 16, 128), jnp.float32),
             pltpu.VMEM((count, 3, tile_rows, 128), jnp.float32),
             pltpu.VMEM((count, 3, tile_rows, 128), jnp.float32),
             pltpu.VMEM((2, cols // 128 + 1, tile_rows, 128), jnp.float32),
-        ],
+        ]
+        + [pltpu.VMEM((2, tile_rows, cols), jnp.float32)] * merging,
     )
     pixels = count * out_rows * cols
     return pl.pallas_call(
         kernel,
         grid_spec=grid_spec,
-        out_shape=jax.ShapeDtypeStruct((2, out_rows, cols), jnp.float32),
+        out_shape=jax.ShapeDtypeStruct((2, out_rows, width), kind),
         cost_estimate=pl.CostEstimate(flops=pixels * 2048, bytes_accessed=pixels * 3, transcendentals=0),
         compiler_params=pltpu.CompilerParams(vmem_limit_bytes=60 << 20),
         name="stencil",
-    )(place, slices, slices, slices, ends, weights)
-
-
-def table_kernel(near, turn, out, *, half):
+    )(place, slices, slices, slices, ends, *((received,) * merging))
+
+
+def table_kernel(near_cos, near_sin, step_cos, step_sin, turn_cos, turn_sin, out, *, half):
     parity, block = pl.program_id(0), pl.program_id(1)
-    period = near.shape[2]
+    period = near_cos.shape[1]
     group = min(64, period)
     norm = math.sqrt(1.0 / half)
 
     def fill(b, carry):
         for at in range(0, period, group):
-            near_cos, near_sin, step_cos, step_sin = (near[0, k, pl.ds(at, group), :] for k in range(4))
-            low_cos = near_cos * turn[b, 0] - near_sin * turn[b, 1]
-            low_sin = near_sin * turn[b, 0] + near_cos * turn[b, 1]
+            near = near_cos[0, pl.ds(at, group), :], near_sin[0, pl.ds(at, group), :]
+            step = step_cos[0, pl.ds(at, group), :], step_sin[0, pl.ds(at, group), :]
+            low_cos = near[0] * turn_cos[b] - near[1] * turn_sin[b]
+            low_sin = near[1] * turn_cos[b] + near[0] * turn_sin[b]
             row = at + lax.broadcasted_iota(jnp.int32, low_cos.shape, 0)
             first = (row == 0) & (parity == 0) & (block == 0) & (b == 0)
             scale = jnp.where(first, norm * math.sqrt(0.5), norm)
             before = scale * low_cos
-            here = scale * (step_cos * low_cos - step_sin * low_sin)
-            twice = step_cos + step_cos
+            here = scale * (step[0] * low_cos - step[1] * low_sin)
+            twice = step[0] + step[0]
             rows = pl.ds(pl.multiple_of(b * period + at, group), group)
             out[0, rows, pl.ds(0, 128)] = before.astype(jnp.bfloat16)
             for j in range(1, half // 128):
@@ -229,23 +244,27 @@
 
     odd = (2, rows, 128)
     frequency = 2 * iota(odd, 1) + iota(odd, 0)
-    near = jnp.stack(pair((2 * iota(odd, 2) + 1) * frequency) + pair(256 * frequency), axis=1)
+    near = pair((2 * iota(odd, 2) + 1) * frequency) + pair(256 * frequency)
     blocks = (half // rows, 1, 128)
-    turn = jnp.stack(pair((2 * iota(blocks, 2) + 1) * (2 * rows * iota(blocks, 0))), axis=1)
+    turn = pair((2 * iota(blocks, 2) + 1) * (2 * rows * iota(blocks, 0)))
     return pl.pallas_call(
         functools.partial(table_kernel, half=half),
         grid=(2, half // tall),
         in_specs=[
-            pl.BlockSpec((1, 4, rows, 128), lambda p, b: (p, 0, 0, 0)),
-            pl.BlockSpec((tall // rows, 2, 1, 128), lambda p, b: (b, 0, 0, 0)),
-        ],
+            pl.BlockSpec((1, rows, 128), lambda p, b: (p, 0, 0)),
+        ]
+        * 4
+        + [pl.BlockSpec((tall // rows, 1, 128), lambda p, b: (b, 0, 0))] * 2,
         out_specs=pl.BlockSpec((1, tall, half), lambda p, b: (p, b, 0)),
         out_shape=jax.ShapeDtypeStruct((2, half, half), jnp.bfloat16),
         name="cosines",
-    )(near, turn)
-
-
-def merge_kernel(own, other, mirror, out, *, cols):
+    )(*near, *turn)
+
+
+def fold(own, other, out):
+    cols = own.shape[2]
+    mirror = exchange_matrix()
+
     def merged(at):
         numerator = own[0, :, pl.ds(at, lane_block)] + other[0, :, pl.ds(at, lane_block)]
         denominator = own[1, :, pl.ds(at, lane_block)] + other[1, :, pl.ds(at, lane_block)]
@@ -253,27 +272,26 @@
 
     for at in range(0, cols // 2, lane_block):
         near = merged(at).astype(jnp.float32)
-        far = dot(merged(cols - lane_block - at), mirror[...])
+        far = dot(merged(cols - lane_block - at), mirror)
         out[0, :, pl.ds(at, lane_block)] = (near + far).astype(jnp.bfloat16)
         out[1, :, pl.ds(at, lane_block)] = (near - far).astype(jnp.bfloat16)
 
 
-def merge(own, other, mirror, at):
+def merge(own, other, at):
     _, rows, cols = own.shape
     tile = min(64, rows)
     first = at // tile
     return pl.pallas_call(
-        functools.partial(merge_kernel, cols=cols),
+        fold,
         grid=(rows // tile,),
         in_specs=[
             pl.BlockSpec((2, tile, cols), lambda t: (0, t, 0)),
             pl.BlockSpec((2, tile, cols), lambda t: (0, first + t, 0)),
-            pl.BlockSpec((lane_block, lane_block), lambda t: (0, 0)),
         ],
         out_specs=pl.BlockSpec((2, tile, cols // 2), lambda t: (0, t, 0)),
         out_shape=jax.ShapeDtypeStruct((2, rows, cols // 2), jnp.bfloat16),
         name="merge",
-    )(own, other, mirror)
+    )(own, other)
 
 
 def rows_kernel(table, folded, out):
@@ -300,19 +318,20 @@
 
 
 def columns_kernel(*refs, chunks, half, order):
-    table, rows_response, cols_response, mirror = refs[:4]
-    arrived = refs[4 : 4 + chunks]
-    out, folded, total = refs[4 + chunks :]
+    table, rows_response, cols_response = refs[:3]
+    arrived = refs[3 : 3 + chunks]
+    out, folded, total = refs[3 + chunks :]
     parity = pl.program_id(0)
     step = pl.program_id(1)
     blocks = half // lane_block
 
     @pl.when((parity == 0) & (step == 0))
     def _():
+        mirror = exchange_matrix()
         for j in range(blocks):
             near = jnp.concatenate([part[order[j], 0] for part in arrived], axis=1).astype(jnp.float32)
             far = dot(
-                jnp.concatenate([part[order[2 * blocks - 1 - j], 0] for part in arrived], axis=1), mirror[...]
+                jnp.concatenate([part[order[2 * blocks - 1 - j], 0] for part in arrived], axis=1), mirror
             )
             folded[0, :, pl.ds(j * lane_block, lane_block)] = (near + far).astype(jnp.bfloat16)
             folded[1, :, pl.ds(j * lane_block, lane_block)] = (near - far).astype(jnp.bfloat16)
@@ -332,14 +351,15 @@
 
     @pl.when((parity == 1) & (step == pl.num_programs(1) - 1))
     def _():
+        mirror = exchange_matrix()
         for j in range(blocks):
             even = total[0, :, pl.ds(j * lane_block, lane_block)]
             odd = total[1, :, pl.ds(j * lane_block, lane_block)]
             out[j] = (even + odd).astype(jnp.bfloat16)
-            out[2 * blocks - 1 - j] = dot((even - odd).astype(jnp.bfloat16), mirror[...]).astype(jnp.bfloat16)
-
-
-def filter_columns(table, rows_response, cols_response, mirror, arrived, order):
+            out[2 * blocks - 1 - j] = dot((even - odd).astype(jnp.bfloat16), mirror).astype(jnp.bfloat16)
+
+
+def filter_columns(table, rows_response, cols_response, arrived, order):
     half = table.shape[1]
     blocks, _, own, _ = arrived[0][0].shape
     tile = min(1024, half)
@@ -355,7 +375,6 @@
             pl.BlockSpec((1, tile, half), lambda p, t: (p, t, 0)),
             pl.BlockSpec((1, 1, tile), lambda p, t: (p, 0, t)),
             pl.BlockSpec((own, 1), lambda p, t: (0, 0)),
-            pl.BlockSpec((lane_block, lane_block), lambda p, t: (0, 0)),
         ]
         + [whole(*pair) for pair in arrived],
         out_specs=pl.BlockSpec((blocks, own, lane_block), lambda p, t: (0, 0, 0)),
@@ -366,7 +385,7 @@
         ],
         compiler_params=pltpu.CompilerParams(vmem_limit_bytes=60 << 20),
         name="filter_columns",
-    )(table, rows_response, cols_response, mirror, *(part for part, _ in arrived))
+    )(table, rows_response, cols_response, *(part for part, _ in arrived))
 
 
 def turn(values):
@@ -401,7 +420,7 @@
     )(table, arrived)
 
 
-def odd_kernel(table, arrived, even, mirror, out, turned, *, half, tile):
+def odd_kernel(table, arrived, even, out, turned, *, half, tile):
     step = pl.program_id(0)
 
     @pl.when(step == 0)
@@ -412,18 +431,19 @@
     odd = dot(turned[...], table[0])
     out[:, pl.ds(pl.multiple_of(step * tile, tile), tile)] = even[...] + odd
     left = even[...] - odd
+    mirror = exchange_matrix()
     base = pl.multiple_of(2 * half - tile - step * tile, tile)
     for at in range(0, tile, lane_block):
         rest = left[:, at : at + lane_block]
         back = jnp.zeros_like(rest)
         for _ in range(3):
             piece = rest.astype(jnp.bfloat16)
-            back += dot(piece, mirror[...])
+            back += dot(piece, mirror)
             rest = rest - piece.astype(jnp.float32)
         out[:, pl.ds(base + tile - lane_block - at, lane_block)] = back
 
 
-def restore(table, arrived, even, mirror):
+def restore(table, arrived, even):
     half = table.shape[1]
     devices, own, rows = arrived.shape
     tile = min(1024, half)
@@ -434,14 +454,13 @@
             pl.BlockSpec((1, half, tile), lambda t: (1, 0, t)),
             pl.BlockSpec((devices, own, rows), lambda t: (0, 0, 0)),
             pl.BlockSpec((rows, tile), lambda t: (0, t)),
-            pl.BlockSpec((lane_block, lane_block), lambda t: (0, 0)),
         ],
         out_specs=pl.BlockSpec((rows, 2 * half), lambda t: (0, 0)),
         out_shape=jax.ShapeDtypeStruct((rows, 2 * half), jnp.float32),
         scratch_shapes=[pltpu.VMEM((rows, half), jnp.bfloat16)],
         compiler_params=pltpu.CompilerParams(vmem_limit_bytes=60 << 20),
         name="restore",
-    )(table, arrived, even, mirror)
+    )(table, arrived, even)
 
 
 def program(slices, otf_rows, otf_cols):
@@ -455,24 +474,18 @@
     per = lane_block // piece
     above, below = edge_rows(slices, 4)
     table = cosine_halves(length)
-    weights = band()
-    mirror = exchange_matrix()
     focus = lax.axis_index("focus")
     owner = focus * lax.axis_size("strip") + lax.axis_index("strip")
     own = half // devices
-    rows_response = otf_rows.reshape(half, 2).T.reshape(2, 1, half)
-    local_cols = lax.dynamic_slice_in_dim(otf_cols, owner * 2 * own, 2 * own, 0).reshape(own, 2).T.reshape(2, own, 1)
-    above, below, table, rows_response, local_cols, mirror, weights = lax.optimization_barrier(
-        (above, below, table, rows_response, local_cols, mirror, weights)
-    )
+    above, below, table = lax.optimization_barrier((above, below, table))
     ends = jnp.pad(above, ((0, 0), (12, 0), (0, 0))) + jnp.pad(below, ((0, 0), (0, 12), (0, 0)))
     chunks = row_chunks if per == 1 and piece % (16 * row_chunks) == 0 else 1
     chunk_rows = piece // chunks
     swap = [(i, focus_count - 1 - i) for i in range(focus_count)]
 
-    def sums(ends, half_index, chunk, rows):
+    def sums(ends, half_index, chunk, rows, *merging):
         place = (half_index * piece + chunk * chunk_rows) // math.gcd(128, rows)
-        return stencil(place.astype(jnp.int32).reshape(1), slices, ends, weights, rows)
+        return stencil(place.astype(jnp.int32).reshape(1), slices, ends, rows, *merging)
 
     last = []
 
@@ -482,15 +495,26 @@
         last.append(lax.all_to_all(values, axes, split_axis=0, concat_axis=0, tiled=True))
         return last[-1]
 
+    def responses():
+        local = lax.dynamic_slice_in_dim(otf_cols, owner * 2 * own, 2 * own, 0)
+        return otf_rows.reshape(half, 2).T.reshape(2, 1, half), local.reshape(own, 2).T.reshape(2, own, 1)
+
     received = lax.ppermute(sums(ends, focus_count - 1 - focus, 0, piece), "focus", swap)
     arrived = ([], [])
     for chunk in range(chunks):
-        own_sums = sums(ends, focus, chunk, chunk_rows)
-        folded = merge(own_sums, received, mirror, chunk * chunk_rows)
+        if chunk == 0:
+            folded = merge(sums(ends, focus, 0, chunk_rows), received, 0)
+        else:
+            folded = sums(ends, focus, chunk, chunk_rows, received, chunk * chunk_rows)
         for parities in ((0,), (1,)) if chunk == chunks - 1 else ((0, 1),):
             along = transform_rows(table, folded, parities, devices)
             if chunk < chunks - 1:
                 ends, along = lax.optimization_barrier((ends, along))
+            elif parities == (0,):
+                otf_rows, otf_cols, along = lax.optimization_barrier((otf_rows, otf_cols, along))
+                rows_response, local_cols = responses()
+            else:
+                along, rows_response, local_cols = lax.optimization_barrier((along, rows_response, local_cols))
             moved = exchange(along)
             for at, parity in enumerate(parities):
                 arrived[parity].append((moved, at))
@@ -511,12 +535,12 @@
                 )
                 for part, _ in parts
             ]
-        back = filter_columns(table, rows_response, local_cols[parity], mirror, parts, order)
+        back = filter_columns(table, rows_response, local_cols[parity], parts, order)
         if per > 1:
             back = back.reshape(blocks, own, per, piece).transpose(0, 2, 1, 3).reshape(devices, own, piece)
         restored.append(exchange(back))
     even = restore_even(table, restored[0])
-    return restore(table, restored[1], even, mirror)
+    return restore(table, restored[1], even)
 
 
 def solution(mesh):

time: 267 us -> 259 us (0.970)
  Pallas kernels: 177 us -> 174 us
  waiting for transfers between devices: 45.4 us -> 42.7 us
    pallas_call x2 -> x1, Pallas kernels: 9.31 us -> 4.63 us  [merge(): pl.pallas_call(fold, grid=(rows // tile,), in_specs=[pl.BlockSpec((2, til...]
    sin x0 -> x2, other arithmetic: none -> 3.94 us  [pair(): return [jnp.cos(angle), jnp.sin(angle)]]
where the time goes in v5:
time: 259 us
  Pallas kernels  174 us (67%)
  waiting for transfers between devices  42.7 us (16%)
  starting transfers between devices  30.6 us (12%)
  local copies, waits for them, and re-layouts  6.03 us (2%)
  other arithmetic  5.29 us (2%)
    pallas_call x3, Pallas kernels, stencil(): pl.pallas_call(kernel, grid_spec=grid_spec, out_shape=jax.ShapeDtypeStruc...  98.4 us
    all_to_all x5, waiting for transfers between devices, exchange(): lax.all_to_all(values, axes, split_axis=0, concat_axis=0, tiled=True)  42.7 us
    pallas_call x2, Pallas kernels, filter_columns(): pl.pallas_call(functools.partial(columns_kernel, chunks=chunks, half=half...  26.1 us
    all_to_all x5, starting transfers between devices, exchange(): lax.all_to_all(values, axes, split_axis=0, concat_axis=0, tiled=True)  24.4 us
    pallas_call x3, Pallas kernels, transform_rows(): pl.pallas_call(rows_kernel, grid=(len(parities), half // tile), in_specs=...  20.7 us
    pallas_call x1, Pallas kernels, cosine_halves(): pl.pallas_call(functools.partial(table_kernel, half=half), grid=(2, half...  8.97 us
    pallas_call x1, Pallas kernels, restore(): pl.pallas_call(functools.partial(odd_kernel, half=half, tile=tile), grid=...  8.63 us
    pallas_call x1, Pallas kernels, restore_even(): pl.pallas_call(functools.partial(even_kernel, half=half), grid=(half // t...  6.42 us
  transfers between devices with their start and end apart: 8, of which 4 were waited for; matrix products, arithmetic and copies ran while one was open for 3% of the time, Pallas kernels for 41%

profile of v5, /device:TPU:0, one launch (start us, length us, event | category | flops | bytes accessed | tf_op | source)
XLA Modules:
  0.0 258.6 jit_solution(14853714421105971469)
XLA Ops:
  0.0 1.5 fusion.12
  1.5 4.9 %collective-permute-start = (bf16[8,4,4096]{2,1,0:T(4,128)(2,1)S(1)}, bf16[8,4,4096]{2,1,0:T(4,128)(2,1)S(1)}, u32[]{:S(2)}, u32[]{:S(2)}) collective-permute-start(bf16[8,4,4096]{2,1,0:T(4,128)(2,1)S(1)} %get-tuple-element.36), channel_id=1, source_target_pairs={{0,1},{1,2},{2,3},{3,4},{4,5},{5,6},{6,7},{8,9},{9,10},{10,11},{11... | collective-permute-start | bytes 786440 | tf_op jit(solution)/shard_map/ppermute | solution.py:31
  6.4 1.3 collective-permute-start.1
  7.8 0.7 multiply_sine_fusion
  8.5 3.2 %fusion.6 = (f32[2,256,128]{2,1,0:T(8,128)}, f32[2,256,128]{2,1,0:T(8,128)}, f32[2,256,128]{2,1,0:T(8,128)}, f32[2,256,128]{2,1,0:T(8,128)}) fusion(s32[256]{0:T(256)S(1)} %iota_multiply_fusion, s32[128]{0:T(128)S(1)} %multiply_add_fusion), kind=kLoop, calls=%fused_computation.14 | loop fusion | flops 1900544 | bytes 1050112 | tf_op jit(solution)/shard_map/sin | solution.py:240
  11.7 9.0 %cosines.1.table.refs_0_ = bf16[2,2048,2048]{2,1,0:T(8,128)(2,1)} custom-call(f32[2,256,128]{2,1,0:T(8,128)} %get-tuple-element.45.near_cos, f32[2,256,128]{2,1,0:T(8,128)} %get-tuple-element.46.near_sin, f32[2,256,128]{2,1,0:T(8,128)} %get-tuple-element.44.step_cos, f32[2,256,128]{2,1,0:T(8,128)} %get-tuple-element.43.step_sin, ...), custom_call_target="tpu_custom_call" | custom-call | tf_op jit(solution)/shard_map/cosines/pallas_call | solution.py:250
  20.7 1.3 pad_add_fusion.ends
  22.0 45.5 %stencil.4 = f32[2,256,4096]{2,1,0:T(8,128)} custom-call(s32[1]{0:T(128)} %bitcast.3.place, bf16[8,512,4096]{2,1,0:T(8,128)(2,1)} %below.5, bf16[8,512,4096]{2,1,0:T(8,128)(2,1)} %below.5, bf16[8,512,4096]{2,1,0:T(8,128)(2,1)} %below.5, bf16[8,16,4096]{2,1,0:T(8,128)(2,1)} %pad_add_fusion.ends), custom_call_target="tpu_custom_call" | custom-call | flops 17179869184 | bytes 25165824 | tf_op jit(solution)/shard_map/stencil/pallas_call | solution.py:193
  67.5 26.0 %stencil.3.own = f32[2,128,4096]{2,1,0:T(8,128)} custom-call(s32[1]{0:T(128)} %bitcast.2.place, bf16[8,512,4096]{2,1,0:T(8,128)(2,1)} %below.5, bf16[8,512,4096]{2,1,0:T(8,128)(2,1)} %below.5, bf16[8,512,4096]{2,1,0:T(8,128)(2,1)} %below.5, bf16[8,16,4096]{2,1,0:T(8,128)(2,1)} %pad_add_fusion.ends), custom_call_target="tpu_custom_call" | custom-call | flops 8589934592 | bytes 12582912 | tf_op jit(solution)/shard_map/stencil/pallas_call | solution.py:193
  93.6 4.6 %merge.1.folded = bf16[2,128,2048]{2,1,0:T(8,128)(2,1)} custom-call(f32[2,128,4096]{2,1,0:T(8,128)} %stencil.3.own, f32[2,256,4096]{2,1,0:T(8,128)} %collective-permute-done.2.other.rest_0_), custom_call_target="tpu_custom_call" | custom-call | tf_op jit(solution)/shard_map/merge/pallas_call | solution.py:284
  98.2 9.5 %transform_rows.3 = bf16[16,2,128,128]{3,2,1,0:T(8,128)(2,1)} custom-call(bf16[2,2048,2048]{2,1,0:T(8,128)(2,1)} %cosines.1.table.refs_0_, bf16[2,128,2048]{2,1,0:T(8,128)(2,1)} %merge.1.folded), custom_call_target="tpu_custom_call" | custom-call | tf_op jit(solution)/shard_map/transform_rows/pallas_call | solution.py:307
  107.7 7.2 %all-to-all-start = ((bf16[16,2,128,128]{3,2,1,0:T(8,128)(2,1)}), bf16[16,2,128,128]{3,2,1,0:T(8,128)(2,1)S(1)}, u32[]{:S(2)}, u32[]{:S(2)}) async-start(bf16[16,2,128,128]{3,2,1,0:T(8,128)(2,1)} %transform_rows.3), calls=%async_computation | async-start | bytes 2097152 | tf_op jit(solution)/shard_map/all_to_all | solution.py:495
  114.9 26.8 %stencil.5.folded = bf16[2,128,2048]{2,1,0:T(8,128)(2,1)} custom-call(s32[1]{0:T(128)} %bitcast.1.place, bf16[8,512,4096]{2,1,0:T(8,128)(2,1)} %below.5, bf16[8,512,4096]{2,1,0:T(8,128)(2,1)} %below.5, bf16[8,512,4096]{2,1,0:T(8,128)(2,1)} %below.5, bf16[8,16,4096]{2,1,0:T(8,128)(2,1)} %pad_add_fusion.ends, f32[2,256,4096]{2,1,0:T(8,128)} %collective-permute-done.2.other.rest_0_), custom_call_target="tpu_custom_call" | custom-call | flops 8589934592 | bytes 12582912 | tf_op jit(solution)/shard_map/stencil/pallas_call | solution.py:193
  141.7 5.6 %transform_rows.5 = bf16[16,1,128,128]{3,2,1,0:T(8,128)(2,1)} custom-call(bf16[2,2048,2048]{2,1,0:T(8,128)(2,1)} %cosines.1.table.refs_0_, bf16[2,128,2048]{2,1,0:T(8,128)(2,1)} %stencil.5.folded), custom_call_target="tpu_custom_call" | custom-call | tf_op jit(solution)/shard_map/transform_rows/pallas_call | solution.py:307
  147.3 6.0 %all-to-all-start.1 = ((bf16[16,1,128,128]{3,2,1,0:T(8,128)(2,1)}), bf16[16,1,128,128]{3,2,1,0:T(8,128)(2,1)S(1)}, u32[]{:S(2)}, u32[]{:S(2)}) async-start(bf16[16,1,128,128]{3,2,1,0:T(8,128)(2,1)} %transform_rows.5), calls=%async_computation.1 | async-start | bytes 1048576 | tf_op jit(solution)/shard_map/all_to_all | solution.py:495
  153.3 5.6 %transform_rows.4 = bf16[16,1,128,128]{3,2,1,0:T(8,128)(2,1)} custom-call(bf16[2,2048,2048]{2,1,0:T(8,128)(2,1)} %cosines.1.table.refs_0_, bf16[2,128,2048]{2,1,0:T(8,128)(2,1)} %stencil.5.folded), custom_call_target="tpu_custom_call" | custom-call | tf_op jit(solution)/shard_map/transform_rows/pallas_call | solution.py:307
  158.9 1.0 reshape.148
  160.3 0.6 reshape.149.refs_1_
  160.9 0.8 dynamic_slice.3
  161.8 7.3 %all-to-all-done.1.refs_4_ = bf16[16,1,128,128]{3,2,1,0:T(8,128)(2,1)S(1)} async-done(((bf16[16,1,128,128]{3,2,1,0:T(8,128)(2,1)}), bf16[16,1,128,128]{3,2,1,0:T(8,128)(2,1)S(1)}, u32[]{:S(2)}, u32[]{:S(2)}) %all-to-all-start.1) | async-done | bytes 524320 | tf_op jit(solution)/shard_map/all_to_all | solution.py:495
  169.1 3.6 %all-to-all-start.2 = ((bf16[16,1,128,128]{3,2,1,0:T(8,128)(2,1)}), bf16[16,1,128,128]{3,2,1,0:T(8,128)(2,1)S(1)}, u32[]{:S(2)}, u32[]{:S(2)}) async-start(bf16[16,1,128,128]{3,2,1,0:T(8,128)(2,1)} %transform_rows.4), calls=%async_computation.2 | async-start | bytes 1048576 | tf_op jit(solution)/shard_map/all_to_all | solution.py:495
  172.7 0.7 slice_bitcast_fusion
  173.4 13.1 %filter_columns.3 = bf16[16,128,256]{2,1,0:T(8,128)(2,1)} custom-call(bf16[2,2048,2048]{2,1,0:T(8,128)(2,1)} %cosines.1.table.refs_0_, f32[2,1,2048]{2,1,0:T(1,128)} %reshape.149.refs_1_, f32[128,1]{1,0:T(8,128)} %get-tuple-element.37.refs_2_, bf16[16,2,128,128]{3,2,1,0:T(8,128)(2,1)} %copy-done, bf16[16,1,128,128]{3,2,1,0:T(8,128)(2,1)} %copy-done.3), custom_call_target="tpu_custom_call" | custom-call | tf_op jit(solution)/shard_map/filter_columns/pallas_call | solution.py:371
  186.4 2.0 all-to-all-done.2.refs_4_
  188.4 4.0 %all-to-all-start.3 = ((bf16[16,128,256]{2,1,0:T(8,128)(2,1)}), bf16[16,128,256]{2,1,0:T(8,128)(2,1)S(1)}, u32[]{:S(2)}, u32[]{:S(2)}) async-start(bf16[16,128,256]{2,1,0:T(8,128)(2,1)} %filter_columns.3), calls=%async_computation.3 | async-start | bytes 2097152 | tf_op jit(solution)/shard_map/all_to_all | solution.py:495
  192.4 13.1 %filter_columns.2 = bf16[16,128,256]{2,1,0:T(8,128)(2,1)} custom-call(bf16[2,2048,2048]{2,1,0:T(8,128)(2,1)} %cosines.1.table.refs_0_, f32[2,1,2048]{2,1,0:T(1,128)} %reshape.149.refs_1_, f32[128,1]{1,0:T(8,128)} %get-tuple-element.38.refs_2_, bf16[16,2,128,128]{3,2,1,0:T(8,128)(2,1)} %copy-done, bf16[16,1,128,128]{3,2,1,0:T(8,128)(2,1)} %copy-done.4), custom_call_target="tpu_custom_call" | custom-call | tf_op jit(solution)/shard_map/filter_columns/pallas_call | solution.py:371
  205.5 13.4 %all-to-all-done.3.arrived = bf16[16,128,256]{2,1,0:T(8,128)(2,1)S(1)} async-done(((bf16[16,128,256]{2,1,0:T(8,128)(2,1)}), bf16[16,128,256]{2,1,0:T(8,128)(2,1)S(1)}, u32[]{:S(2)}, u32[]{:S(2)}) %all-to-all-start.3) | async-done | bytes 1048608 | tf_op jit(solution)/shard_map/all_to_all | solution.py:495
  218.9 3.7 %all-to-all-start.4 = ((bf16[16,128,256]{2,1,0:T(8,128)(2,1)}), bf16[16,128,256]{2,1,0:T(8,128)(2,1)S(1)}, u32[]{:S(2)}, u32[]{:S(2)}) async-start(bf16[16,128,256]{2,1,0:T(8,128)(2,1)} %filter_columns.2), calls=%async_computation.4 | async-start | bytes 2097152 | tf_op jit(solution)/shard_map/all_to_all | solution.py:495
  222.6 6.4 %restore_even.1.even = f32[256,2048]{1,0:T(8,128)} custom-call(bf16[2,2048,2048]{2,1,0:T(8,128)(2,1)} %cosines.1.table.refs_0_, bf16[16,128,256]{2,1,0:T(8,128)(2,1)} %copy-done.1), custom_call_target="tpu_custom_call" | custom-call | tf_op jit(solution)/shard_map/restore_even/pallas_call | solution.py:408
  229.0 20.0 %all-to-all-done.4.arrived = bf16[16,128,256]{2,1,0:T(8,128)(2,1)S(1)} async-done(((bf16[16,128,256]{2,1,0:T(8,128)(2,1)}), bf16[16,128,256]{2,1,0:T(8,128)(2,1)S(1)}, u32[]{:S(2)}, u32[]{:S(2)}) %all-to-all-start.4) | async-done | bytes 1048608 | tf_op jit(solution)/shard_map/all_to_all | solution.py:495
  249.0 1.0 copy-done.2
  250.0 8.6 %restore.1 = f32[256,4096]{1,0:T(8,128)} custom-call(bf16[2,2048,2048]{2,1,0:T(8,128)(2,1)} %cosines.1.table.refs_0_, bf16[16,128,256]{2,1,0:T(8,128)(2,1)} %copy-done.2, f32[256,2048]{1,0:T(8,128)} %restore_even.1.even), custom_call_target="tpu_custom_call" | custom-call | tf_op jit(solution)/shard_map/restore/pallas_call | solution.py:450
  (22 shorter events, 0.6 us)
Async XLA Ops:
  1.5 19.2 %collective-permute-start = (bf16[8,4,4096]{2,1,0:T(4,128)(2,1)S(1)}, bf16[8,4,4096]{2,1,0:T(4,128)(2,1)S(1)}, u32[]{:S(2)}, u32[]{:S(2)}) collective-permute-start(bf16[8,4,4096]{2,1,0:T(4,128)(2,1)S(1)} %get-tuple-element.36), channel_id=1, source_target_pairs={{0,1},{1,2},{2,3},{3,4},{4,5},{5,6},{6,7},{8,9},{9,10},{10,11},{11... | collective-permute-start | bytes 786440 | tf_op jit(solution)/shard_map/ppermute | solution.py:31
  6.4 14.3 %collective-permute-start.1 = (bf16[8,4,4096]{2,1,0:T(4,128)(2,1)S(1)}, bf16[8,4,4096]{2,1,0:T(4,128)(2,1)S(1)}, u32[]{:S(2)}, u32[]{:S(2)}) collective-permute-start(bf16[8,4,4096]{2,1,0:T(4,128)(2,1)S(1)} %get-tuple-element.35), channel_id=1, source_target_pairs={{1,0},{2,1},{3,2},{4,3},{5,4},{6,5},{7,6},{9,8},{10,9},{11,10},{12... | collective-permute-start | bytes 786440 | tf_op jit(solution)/shard_map/ppermute | solution.py:32
  67.5 26.1 %collective-permute-start.2 = (f32[2,256,4096]{2,1,0:T(8,128)}, f32[2,256,4096]{2,1,0:T(8,128)}, u32[]{:S(2)}, u32[]{:S(2)}) collective-permute-start(f32[2,256,4096]{2,1,0:T(8,128)} %stencil.4), channel_id=1, source_target_pairs={{0,8},{8,0},{1,9},{9,1},{2,10},{10,2},{3,11},{11,3},{4,12},{12,4},... | collective-permute-start | bytes 25165832 | tf_op jit(solution)/shard_map/ppermute | solution.py:502
  107.7 39.6 %all-to-all-start = ((bf16[16,2,128,128]{3,2,1,0:T(8,128)(2,1)}), bf16[16,2,128,128]{3,2,1,0:T(8,128)(2,1)S(1)}, u32[]{:S(2)}, u32[]{:S(2)}) async-start(bf16[16,2,128,128]{3,2,1,0:T(8,128)(2,1)} %transform_rows.3), calls=%async_computation | async-start | bytes 2097152 | tf_op jit(solution)/shard_map/all_to_all | solution.py:495
  147.3 11.6 %copy-start = (bf16[16,2,128,128]{3,2,1,0:T(8,128)(2,1)}, bf16[16,2,128,128]{3,2,1,0:T(8,128)(2,1)S(1)}, u32[]{:S(2)}) copy-start(bf16[16,2,128,128]{3,2,1,0:T(8,128)(2,1)S(1)} %all-to-all-done.refs_3_) | copy-start | bytes 3145732
  147.3 21.8 %all-to-all-start.1 = ((bf16[16,1,128,128]{3,2,1,0:T(8,128)(2,1)}), bf16[16,1,128,128]{3,2,1,0:T(8,128)(2,1)S(1)}, u32[]{:S(2)}, u32[]{:S(2)}) async-start(bf16[16,1,128,128]{3,2,1,0:T(8,128)(2,1)} %transform_rows.5), calls=%async_computation.1 | async-start | bytes 1048576 | tf_op jit(solution)/shard_map/all_to_all | solution.py:495
  153.3 5.6 %copy-start.5 = (f32[4096]{0:T(1024)S(1)}, f32[4096]{0:T(1024)}, u32[]{:S(2)}) copy-start(f32[4096]{0:T(1024)} %param.4) | copy-start | bytes 49156
  169.1 4.3 %copy-start.3 = (bf16[16,1,128,128]{3,2,1,0:T(8,128)(2,1)}, bf16[16,1,128,128]{3,2,1,0:T(8,128)(2,1)S(1)}, u32[]{:S(2)}) copy-start(bf16[16,1,128,128]{3,2,1,0:T(8,128)(2,1)S(1)} %all-to-all-done.1.refs_4_) | copy-start | bytes 1572868
  169.1 19.3 %all-to-all-start.2 = ((bf16[16,1,128,128]{3,2,1,0:T(8,128)(2,1)}), bf16[16,1,128,128]{3,2,1,0:T(8,128)(2,1)S(1)}, u32[]{:S(2)}, u32[]{:S(2)}) async-start(bf16[16,1,128,128]{3,2,1,0:T(8,128)(2,1)} %transform_rows.4), calls=%async_computation.2 | async-start | bytes 1048576 | tf_op jit(solution)/shard_map/all_to_all | solution.py:495
  188.4 4.0 %copy-start.4 = (bf16[16,1,128,128]{3,2,1,0:T(8,128)(2,1)}, bf16[16,1,128,128]{3,2,1,0:T(8,128)(2,1)S(1)}, u32[]{:S(2)}) copy-start(bf16[16,1,128,128]{3,2,1,0:T(8,128)(2,1)S(1)} %all-to-all-done.2.refs_4_) | copy-start | bytes 1572868
  188.4 30.5 %all-to-all-start.3 = ((bf16[16,128,256]{2,1,0:T(8,128)(2,1)}), bf16[16,128,256]{2,1,0:T(8,128)(2,1)S(1)}, u32[]{:S(2)}, u32[]{:S(2)}) async-start(bf16[16,128,256]{2,1,0:T(8,128)(2,1)} %filter_columns.3), calls=%async_computation.3 | async-start | bytes 2097152 | tf_op jit(solution)/shard_map/all_to_all | solution.py:495
  218.9 3.7 %copy-start.1 = (bf16[16,128,256]{2,1,0:T(8,128)(2,1)}, bf16[16,128,256]{2,1,0:T(8,128)(2,1)S(1)}, u32[]{:S(2)}) copy-start(bf16[16,128,256]{2,1,0:T(8,128)(2,1)S(1)} %all-to-all-done.3.arrived) | copy-start | bytes 3145732
  218.9 30.1 %all-to-all-start.4 = ((bf16[16,128,256]{2,1,0:T(8,128)(2,1)}), bf16[16,128,256]{2,1,0:T(8,128)(2,1)S(1)}, u32[]{:S(2)}, u32[]{:S(2)}) async-start(bf16[16,128,256]{2,1,0:T(8,128)(2,1)} %filter_columns.2), calls=%async_computation.4 | async-start | bytes 2097152 | tf_op jit(solution)/shard_map/all_to_all | solution.py:495
  249.0 1.0 copy-start.2

commit v6 on v5

--- a/solution.py
+++ b/solution.py
@@ -383,7 +383,7 @@
             pltpu.VMEM((2, own, half), jnp.bfloat16),
             pltpu.VMEM((2, own, half), jnp.float32),
         ],
-        compiler_params=pltpu.CompilerParams(vmem_limit_bytes=60 << 20),
+        compiler_params=pltpu.CompilerParams(vmem_limit_bytes=40 << 20),
         name="filter_columns",
     )(table, rows_response, cols_response, *(part for part, _ in arrived))
 
@@ -415,7 +415,7 @@
         out_specs=pl.BlockSpec((rows, tile), lambda t: (0, t)),
         out_shape=jax.ShapeDtypeStruct((rows, half), jnp.float32),
         scratch_shapes=[pltpu.VMEM((rows, half), jnp.bfloat16)],
-        compiler_params=pltpu.CompilerParams(vmem_limit_bytes=60 << 20),
+        compiler_params=pltpu.CompilerParams(vmem_limit_bytes=40 << 20),
         name="restore_even",
     )(table, arrived)
 
@@ -458,7 +458,7 @@
         out_specs=pl.BlockSpec((rows, 2 * half), lambda t: (0, 0)),
         out_shape=jax.ShapeDtypeStruct((rows, 2 * half), jnp.float32),
         scratch_shapes=[pltpu.VMEM((rows, half), jnp.bfloat16)],
-        compiler_params=pltpu.CompilerParams(vmem_limit_bytes=60 << 20),
+        compiler_params=pltpu.CompilerParams(vmem_limit_bytes=40 << 20),
         name="restore",
     )(table, arrived, even)
 

time: 259 us -> 258 us (level)
  waiting for transfers between devices: 42.7 us -> 45.6 us
    all_to_all x5, waiting for transfers between devices: 42.7 us -> 45.6 us  [exchange(): lax.all_to_all(values, axes, split_axis=0, concat_axis=0, tiled=True)]
  transfers between devices with their start and end apart: 8 -> 8, of which waited for: 4 -> 4; matrix products, arithmetic and copies ran while one was open for 3% -> 2% of each run, Pallas kernels for 41% -> 40%
where the time goes in v6:
time: 258 us
  Pallas kernels  172 us (67%)
  waiting for transfers between devices  45.6 us (18%)
  starting transfers between devices  31.2 us (12%)
  other arithmetic  5.24 us (2%)
  local copies, waits for them, and re-layouts  3.79 us (1%)
    pallas_call x3, Pallas kernels, stencil(): pl.pallas_call(kernel, grid_spec=grid_spec, out_shape=jax.ShapeDtypeStruc...  98.4 us
    all_to_all x5, waiting for transfers between devices, exchange(): lax.all_to_all(values, axes, split_axis=0, concat_axis=0, tiled=True)  45.6 us
    pallas_call x2, Pallas kernels, filter_columns(): pl.pallas_call(functools.partial(columns_kernel, chunks=chunks, half=half...  25.5 us
    all_to_all x5, starting transfers between devices, exchange(): lax.all_to_all(values, axes, split_axis=0, concat_axis=0, tiled=True)  25 us
    pallas_call x3, Pallas kernels, transform_rows(): pl.pallas_call(rows_kernel, grid=(len(parities), half // tile), in_specs=...  20.7 us
    pallas_call x1, Pallas kernels, cosine_halves(): pl.pallas_call(functools.partial(table_kernel, half=half), grid=(2, half...  8.93 us
    pallas_call x1, Pallas kernels, restore(): pl.pallas_call(functools.partial(odd_kernel, half=half, tile=tile), grid=...  8.33 us
    pallas_call x1, Pallas kernels, restore_even(): pl.pallas_call(functools.partial(even_kernel, half=half), grid=(half // t...  5.18 us
  transfers between devices with their start and end apart: 8, of which 4 were waited for; matrix products, arithmetic and copies ran while one was open for 2% of the time, Pallas kernels for 40%

profile of v6, /device:TPU:0, one launch (start us, length us, event | category | flops | bytes accessed | tf_op | source)
XLA Modules:
  0.0 257.6 jit_solution(812286130448142827)
XLA Ops:
  0.0 1.5 fusion.12
  1.5 4.9 %collective-permute-start = (bf16[8,4,4096]{2,1,0:T(4,128)(2,1)S(1)}, bf16[8,4,4096]{2,1,0:T(4,128)(2,1)S(1)}, u32[]{:S(2)}, u32[]{:S(2)}) collective-permute-start(bf16[8,4,4096]{2,1,0:T(4,128)(2,1)S(1)} %get-tuple-element.36), channel_id=1, source_target_pairs={{0,1},{1,2},{2,3},{3,4},{4,5},{5,6},{6,7},{8,9},{9,10},{10,11},{11... | collective-permute-start | bytes 786440 | tf_op jit(solution)/shard_map/ppermute | solution.py:31
  6.4 1.3 collective-permute-start.1
  7.7 0.1 fusion.10
  7.8 0.7 multiply_sine_fusion
  8.5 3.2 %fusion.6 = (f32[2,256,128]{2,1,0:T(8,128)}, f32[2,256,128]{2,1,0:T(8,128)}, f32[2,256,128]{2,1,0:T(8,128)}, f32[2,256,128]{2,1,0:T(8,128)}) fusion(s32[256]{0:T(256)S(1)} %iota_multiply_fusion, s32[128]{0:T(128)S(1)} %multiply_add_fusion), kind=kLoop, calls=%fused_computation.14 | loop fusion | flops 1900544 | bytes 1050112 | tf_op jit(solution)/shard_map/sin | solution.py:240
  11.7 8.9 %cosines.1.table.refs_0_ = bf16[2,2048,2048]{2,1,0:T(8,128)(2,1)} custom-call(f32[2,256,128]{2,1,0:T(8,128)} %get-tuple-element.45.near_cos, f32[2,256,128]{2,1,0:T(8,128)} %get-tuple-element.46.near_sin, f32[2,256,128]{2,1,0:T(8,128)} %get-tuple-element.44.step_cos, f32[2,256,128]{2,1,0:T(8,128)} %get-tuple-element.43.step_sin, ...), custom_call_target="tpu_custom_call" | custom-call | tf_op jit(solution)/shard_map/cosines/pallas_call | solution.py:250
  20.6 1.2 pad_add_fusion.ends
  21.9 45.5 %stencil.4 = f32[2,256,4096]{2,1,0:T(8,128)} custom-call(s32[1]{0:T(128)} %bitcast.3.place, bf16[8,512,4096]{2,1,0:T(8,128)(2,1)} %below.5, bf16[8,512,4096]{2,1,0:T(8,128)(2,1)} %below.5, bf16[8,512,4096]{2,1,0:T(8,128)(2,1)} %below.5, bf16[8,16,4096]{2,1,0:T(8,128)(2,1)} %pad_add_fusion.ends), custom_call_target="tpu_custom_call" | custom-call | flops 17179869184 | bytes 25165824 | tf_op jit(solution)/shard_map/stencil/pallas_call | solution.py:193
  67.4 26.0 %stencil.3.own = f32[2,128,4096]{2,1,0:T(8,128)} custom-call(s32[1]{0:T(128)} %bitcast.2.place, bf16[8,512,4096]{2,1,0:T(8,128)(2,1)} %below.5, bf16[8,512,4096]{2,1,0:T(8,128)(2,1)} %below.5, bf16[8,512,4096]{2,1,0:T(8,128)(2,1)} %below.5, bf16[8,16,4096]{2,1,0:T(8,128)(2,1)} %pad_add_fusion.ends), custom_call_target="tpu_custom_call" | custom-call | flops 8589934592 | bytes 12582912 | tf_op jit(solution)/shard_map/stencil/pallas_call | solution.py:193
  93.5 4.6 %merge.1.folded = bf16[2,128,2048]{2,1,0:T(8,128)(2,1)} custom-call(f32[2,128,4096]{2,1,0:T(8,128)} %stencil.3.own, f32[2,256,4096]{2,1,0:T(8,128)} %collective-permute-done.2.other.rest_0_), custom_call_target="tpu_custom_call" | custom-call | tf_op jit(solution)/shard_map/merge/pallas_call | solution.py:284
  98.1 9.5 %transform_rows.3 = bf16[16,2,128,128]{3,2,1,0:T(8,128)(2,1)} custom-call(bf16[2,2048,2048]{2,1,0:T(8,128)(2,1)} %cosines.1.table.refs_0_, bf16[2,128,2048]{2,1,0:T(8,128)(2,1)} %merge.1.folded), custom_call_target="tpu_custom_call" | custom-call | tf_op jit(solution)/shard_map/transform_rows/pallas_call | solution.py:307
  107.6 7.2 %all-to-all-start = ((bf16[16,2,128,128]{3,2,1,0:T(8,128)(2,1)}), bf16[16,2,128,128]{3,2,1,0:T(8,128)(2,1)S(1)}, u32[]{:S(2)}, u32[]{:S(2)}) async-start(bf16[16,2,128,128]{3,2,1,0:T(8,128)(2,1)} %transform_rows.3), calls=%async_computation | async-start | bytes 2097152 | tf_op jit(solution)/shard_map/all_to_all | solution.py:495
  114.8 26.8 %stencil.5.folded = bf16[2,128,2048]{2,1,0:T(8,128)(2,1)} custom-call(s32[1]{0:T(128)} %bitcast.1.place, bf16[8,512,4096]{2,1,0:T(8,128)(2,1)} %below.5, bf16[8,512,4096]{2,1,0:T(8,128)(2,1)} %below.5, bf16[8,512,4096]{2,1,0:T(8,128)(2,1)} %below.5, bf16[8,16,4096]{2,1,0:T(8,128)(2,1)} %pad_add_fusion.ends, f32[2,256,4096]{2,1,0:T(8,128)} %collective-permute-done.2.other.rest_0_), custom_call_target="tpu_custom_call" | custom-call | flops 8589934592 | bytes 12582912 | tf_op jit(solution)/shard_map/stencil/pallas_call | solution.py:193
  141.6 5.6 %transform_rows.5 = bf16[16,1,128,128]{3,2,1,0:T(8,128)(2,1)} custom-call(bf16[2,2048,2048]{2,1,0:T(8,128)(2,1)} %cosines.1.table.refs_0_, bf16[2,128,2048]{2,1,0:T(8,128)(2,1)} %stencil.5.folded), custom_call_target="tpu_custom_call" | custom-call | tf_op jit(solution)/shard_map/transform_rows/pallas_call | solution.py:307
  147.2 6.0 %all-to-all-start.1 = ((bf16[16,1,128,128]{3,2,1,0:T(8,128)(2,1)}), bf16[16,1,128,128]{3,2,1,0:T(8,128)(2,1)S(1)}, u32[]{:S(2)}, u32[]{:S(2)}) async-start(bf16[16,1,128,128]{3,2,1,0:T(8,128)(2,1)} %transform_rows.5), calls=%async_computation.1 | async-start | bytes 1048576 | tf_op jit(solution)/shard_map/all_to_all | solution.py:495
  153.2 5.6 %transform_rows.4 = bf16[16,1,128,128]{3,2,1,0:T(8,128)(2,1)} custom-call(bf16[2,2048,2048]{2,1,0:T(8,128)(2,1)} %cosines.1.table.refs_0_, bf16[2,128,2048]{2,1,0:T(8,128)(2,1)} %stencil.5.folded), custom_call_target="tpu_custom_call" | custom-call | tf_op jit(solution)/shard_map/transform_rows/pallas_call | solution.py:307
  158.8 1.0 reshape.148
  159.8 0.3 copy.13
  160.2 0.8 dynamic_slice.3
  161.0 0.1 reshape.150
  161.1 7.9 %all-to-all-done.1.refs_4_ = bf16[16,1,128,128]{3,2,1,0:T(8,128)(2,1)S(1)} async-done(((bf16[16,1,128,128]{3,2,1,0:T(8,128)(2,1)}), bf16[16,1,128,128]{3,2,1,0:T(8,128)(2,1)S(1)}, u32[]{:S(2)}, u32[]{:S(2)}) %all-to-all-start.1) | async-done | bytes 524320 | tf_op jit(solution)/shard_map/all_to_all | solution.py:495
  169.0 3.6 %all-to-all-start.2 = ((bf16[16,1,128,128]{3,2,1,0:T(8,128)(2,1)}), bf16[16,1,128,128]{3,2,1,0:T(8,128)(2,1)S(1)}, u32[]{:S(2)}, u32[]{:S(2)}) async-start(bf16[16,1,128,128]{3,2,1,0:T(8,128)(2,1)} %transform_rows.4), calls=%async_computation.2 | async-start | bytes 1048576 | tf_op jit(solution)/shard_map/all_to_all | solution.py:495
  172.6 12.7 %filter_columns.3 = bf16[16,128,256]{2,1,0:T(8,128)(2,1)} custom-call(bf16[2,2048,2048]{2,1,0:T(8,128)(2,1)} %cosines.1.table.refs_0_, f32[2,1,2048]{2,1,0:T(1,128)S(1)} %reshape.149.refs_1_, f32[128,1]{1,0:T(8,128)S(1)} %get-tuple-element.37.refs_2_, bf16[16,2,128,128]{3,2,1,0:T(8,128)(2,1)S(1)} %all-to-all-done.refs_3_, ...), custom_call_target="tpu_custom_call" | custom-call | tf_op jit(solution)/shard_map/filter_columns/pallas_call | solution.py:371
  185.4 2.9 %all-to-all-done.2.refs_4_ = bf16[16,1,128,128]{3,2,1,0:T(8,128)(2,1)S(1)} async-done(((bf16[16,1,128,128]{3,2,1,0:T(8,128)(2,1)}), bf16[16,1,128,128]{3,2,1,0:T(8,128)(2,1)S(1)}, u32[]{:S(2)}, u32[]{:S(2)}) %all-to-all-start.2) | async-done | bytes 524320 | tf_op jit(solution)/shard_map/all_to_all | solution.py:495
  188.3 3.9 %all-to-all-start.3 = ((bf16[16,128,256]{2,1,0:T(8,128)(2,1)}), bf16[16,128,256]{2,1,0:T(8,128)(2,1)S(1)}, u32[]{:S(2)}, u32[]{:S(2)}) async-start(bf16[16,128,256]{2,1,0:T(8,128)(2,1)} %filter_columns.3), calls=%async_computation.3 | async-start | bytes 2097152 | tf_op jit(solution)/shard_map/all_to_all | solution.py:495
  192.2 12.7 %filter_columns.2 = bf16[16,128,256]{2,1,0:T(8,128)(2,1)} custom-call(bf16[2,2048,2048]{2,1,0:T(8,128)(2,1)} %cosines.1.table.refs_0_, f32[2,1,2048]{2,1,0:T(1,128)S(1)} %reshape.149.refs_1_, f32[128,1]{1,0:T(8,128)S(1)} %get-tuple-element.38.refs_2_, bf16[16,2,128,128]{3,2,1,0:T(8,128)(2,1)S(1)} %all-to-all-done.refs_3_, ...), custom_call_target="tpu_custom_call" | custom-call | tf_op jit(solution)/shard_map/filter_columns/pallas_call | solution.py:371
  204.9 13.5 %all-to-all-done.3.arrived = bf16[16,128,256]{2,1,0:T(8,128)(2,1)S(1)} async-done(((bf16[16,128,256]{2,1,0:T(8,128)(2,1)}), bf16[16,128,256]{2,1,0:T(8,128)(2,1)S(1)}, u32[]{:S(2)}, u32[]{:S(2)}) %all-to-all-start.3) | async-done | bytes 1048608 | tf_op jit(solution)/shard_map/all_to_all | solution.py:495
  218.4 4.4 %all-to-all-start.4 = ((bf16[16,128,256]{2,1,0:T(8,128)(2,1)}), bf16[16,128,256]{2,1,0:T(8,128)(2,1)}, u32[]{:S(2)}, u32[]{:S(2)}) async-start(bf16[16,128,256]{2,1,0:T(8,128)(2,1)} %filter_columns.2), calls=%async_computation.4 | async-start | bytes 2097152 | tf_op jit(solution)/shard_map/all_to_all | solution.py:495
  222.8 5.2 %restore_even.1.even = f32[256,2048]{1,0:T(8,128)S(1)} custom-call(bf16[2,2048,2048]{2,1,0:T(8,128)(2,1)} %cosines.1.table.refs_0_, bf16[16,128,256]{2,1,0:T(8,128)(2,1)S(1)} %all-to-all-done.3.arrived), custom_call_target="tpu_custom_call" | custom-call | tf_op jit(solution)/shard_map/restore_even/pallas_call | solution.py:408
  227.9 21.3 %all-to-all-done.4.arrived = bf16[16,128,256]{2,1,0:T(8,128)(2,1)} async-done(((bf16[16,128,256]{2,1,0:T(8,128)(2,1)}), bf16[16,128,256]{2,1,0:T(8,128)(2,1)}, u32[]{:S(2)}, u32[]{:S(2)}) %all-to-all-start.4) | async-done | bytes 1048608 | tf_op jit(solution)/shard_map/all_to_all | solution.py:495
  249.2 8.3 %restore.1 = f32[256,4096]{1,0:T(8,128)} custom-call(bf16[2,2048,2048]{2,1,0:T(8,128)(2,1)} %cosines.1.table.refs_0_, bf16[16,128,256]{2,1,0:T(8,128)(2,1)} %all-to-all-done.4.arrived, f32[256,2048]{1,0:T(8,128)S(1)} %restore_even.1.even), custom_call_target="tpu_custom_call" | custom-call | tf_op jit(solution)/shard_map/restore/pallas_call | solution.py:450
  (12 shorter events, 0.1 us)
Async XLA Ops:
  1.5 19.2 %collective-permute-start = (bf16[8,4,4096]{2,1,0:T(4,128)(2,1)S(1)}, bf16[8,4,4096]{2,1,0:T(4,128)(2,1)S(1)}, u32[]{:S(2)}, u32[]{:S(2)}) collective-permute-start(bf16[8,4,4096]{2,1,0:T(4,128)(2,1)S(1)} %get-tuple-element.36), channel_id=1, source_target_pairs={{0,1},{1,2},{2,3},{3,4},{4,5},{5,6},{6,7},{8,9},{9,10},{10,11},{11... | collective-permute-start | bytes 786440 | tf_op jit(solution)/shard_map/ppermute | solution.py:31
  6.4 14.3 %collective-permute-start.1 = (bf16[8,4,4096]{2,1,0:T(4,128)(2,1)S(1)}, bf16[8,4,4096]{2,1,0:T(4,128)(2,1)S(1)}, u32[]{:S(2)}, u32[]{:S(2)}) collective-permute-start(bf16[8,4,4096]{2,1,0:T(4,128)(2,1)S(1)} %get-tuple-element.35), channel_id=1, source_target_pairs={{1,0},{2,1},{3,2},{4,3},{5,4},{6,5},{7,6},{9,8},{10,9},{11,10},{12... | collective-permute-start | bytes 786440 | tf_op jit(solution)/shard_map/ppermute | solution.py:32
  67.4 26.1 %collective-permute-start.2 = (f32[2,256,4096]{2,1,0:T(8,128)}, f32[2,256,4096]{2,1,0:T(8,128)}, u32[]{:S(2)}, u32[]{:S(2)}) collective-permute-start(f32[2,256,4096]{2,1,0:T(8,128)} %stencil.4), channel_id=1, source_target_pairs={{0,8},{8,0},{1,9},{9,1},{2,10},{10,2},{3,11},{11,3},{4,12},{12,4},... | collective-permute-start | bytes 25165832 | tf_op jit(solution)/shard_map/ppermute | solution.py:502
  107.6 39.6 %all-to-all-start = ((bf16[16,2,128,128]{3,2,1,0:T(8,128)(2,1)}), bf16[16,2,128,128]{3,2,1,0:T(8,128)(2,1)S(1)}, u32[]{:S(2)}, u32[]{:S(2)}) async-start(bf16[16,2,128,128]{3,2,1,0:T(8,128)(2,1)} %transform_rows.3), calls=%async_computation | async-start | bytes 2097152 | tf_op jit(solution)/shard_map/all_to_all | solution.py:495
  147.2 21.8 %all-to-all-start.1 = ((bf16[16,1,128,128]{3,2,1,0:T(8,128)(2,1)}), bf16[16,1,128,128]{3,2,1,0:T(8,128)(2,1)S(1)}, u32[]{:S(2)}, u32[]{:S(2)}) async-start(bf16[16,1,128,128]{3,2,1,0:T(8,128)(2,1)} %transform_rows.5), calls=%async_computation.1 | async-start | bytes 1048576 | tf_op jit(solution)/shard_map/all_to_all | solution.py:495
  153.2 5.6 %copy-start = (f32[4096]{0:T(1024)S(1)}, f32[4096]{0:T(1024)}, u32[]{:S(2)}) copy-start(f32[4096]{0:T(1024)} %param.4) | copy-start | bytes 49156
  169.0 19.3 %all-to-all-start.2 = ((bf16[16,1,128,128]{3,2,1,0:T(8,128)(2,1)}), bf16[16,1,128,128]{3,2,1,0:T(8,128)(2,1)S(1)}, u32[]{:S(2)}, u32[]{:S(2)}) async-start(bf16[16,1,128,128]{3,2,1,0:T(8,128)(2,1)} %transform_rows.4), calls=%async_computation.2 | async-start | bytes 1048576 | tf_op jit(solution)/shard_map/all_to_all | solution.py:495
  188.3 30.1 %all-to-all-start.3 = ((bf16[16,128,256]{2,1,0:T(8,128)(2,1)}), bf16[16,128,256]{2,1,0:T(8,128)(2,1)S(1)}, u32[]{:S(2)}, u32[]{:S(2)}) async-start(bf16[16,128,256]{2,1,0:T(8,128)(2,1)} %filter_columns.3), calls=%async_computation.3 | async-start | bytes 2097152 | tf_op jit(solution)/shard_map/all_to_all | solution.py:495
  218.4 30.8 %all-to-all-start.4 = ((bf16[16,128,256]{2,1,0:T(8,128)(2,1)}), bf16[16,128,256]{2,1,0:T(8,128)(2,1)}, u32[]{:S(2)}, u32[]{:S(2)}) async-start(bf16[16,128,256]{2,1,0:T(8,128)(2,1)} %filter_columns.2), calls=%async_computation.4 | async-start | bytes 2097152 | tf_op jit(solution)/shard_map/all_to_all | solution.py:495
